TPU v7x, 32 devices: a whole 2x2x4 slice. The times are simulated.
32 devices in a mesh: row: 4 (over x, core), col: 8 (over z, y).
Axes of the slice: x: 2, y: 2, z: 4, core: 2. Of those that a mesh axis runs over, the one named last changes fastest.
Arguments:
- y_prev: float32 [16384, 512], P('row'), may hold values from -6 to 6
- u_cols: float32 [512, 16384], P('col', 'row'), may hold values from -0.046875 to 0.046875
- b_panel: float32 [512, 512], P('col'), may hold values from -6 to 6
- u_diag: float32 [512, 512], replicated, may hold values from -1 to 2, as said below
- l_diag: float32 [512, 512], replicated, may hold values from -1 to 1, as said below
- l_coupling: float32 [512, 512], P('col'), may hold values from -0.25 to 0.25
- l_prev_diag: float32 [512, 512], replicated, may hold values from -1 to 1, as said below
- perm: int32 [1024], P('col'), may hold values from 0 to 1023, each once
Outputs:
- y_panel: float32 [512, 512], P('col')
- x_tail: float32 [1024, 512], P('col', 'row')
Inputs may be any that keep to these rules, and one draw needn't show every extreme that they name: `u_diag`: upper triangular: zero below the diagonal, diagonal between 1 and 2. `l_diag`: unit lower triangular: zero above the diagonal, ones on it. `l_prev_diag`: unit lower triangular: zero above the diagonal, ones on it.
All inputs are finite; a program needn't handle non-finite values.
Results may differ from a plain program's by a relative error of at most 0.00011.
Values sent between devices are 32-bit elements; how exact they have to be, the bound alone decides.
No kernel may reach another device: no remote copies, remote signals or barrier semaphores. Data moves between devices by JAX's collectives and lax.ppermute only.
A program may use at most 128 MiB of HBM per device.

v0:
```python
import jax
import jax.numpy as jnp
from jax import lax
from jax.sharding import PartitionSpec as P


def from_root(block, axis, holder):
    block = jnp.where(lax.axis_index(axis) == holder, block, jnp.zeros_like(block))
    return lax.psum(block, axis)


def block_inverse(block):
    high = lax.Precision.HIGHEST
    size = block.shape[0]
    pivots = jnp.diagonal(block)
    scaled = block / pivots[:, None]
    identity = jnp.eye(size, dtype=jnp.float32)
    negated = identity - scaled
    inverse = identity + negated
    power = negated
    rounds = max((size - 1).bit_length(), 1)
    for _ in range(rounds - 1):
        power = jnp.dot(power, power, precision=high, preferred_element_type=jnp.float32)
        inverse = inverse + jnp.dot(
            inverse, power, precision=high, preferred_element_type=jnp.float32
        )
    return inverse / pivots[None, :]


def triangle_solve(matrix, target, lower):
    high = lax.Precision.HIGHEST
    total = matrix.shape[0]
    block_size = min(64, total)
    blocks = total // block_size
    visit = list(range(blocks)) if lower else list(range(blocks - 1, -1, -1))
    solved = {}
    for index in visit:
        low = index * block_size
        remain = target[low : low + block_size]
        for other in solved:
            left = other * block_size
            remain = remain - jnp.dot(
                matrix[low : low + block_size, left : left + block_size],
                solved[other],
                precision=high,
                preferred_element_type=jnp.float32,
            )
        inverse = block_inverse(matrix[low : low + block_size, low : low + block_size])
        solved[index] = jnp.dot(inverse, remain, precision=high, preferred_element_type=jnp.float32)
    return jnp.concatenate([solved[index] for index in range(blocks)], axis=0)


def per_device(y_prev, u_cols, b_panel, u_diag, l_diag, l_coupling, l_prev_diag, perm):
    high = lax.Precision.HIGHEST
    width = u_diag.shape[0]
    share = u_cols.shape[0]
    partial_value = jnp.dot(u_cols, y_prev, precision=high, preferred_element_type=jnp.float32)
    summed = lax.psum(partial_value, "row")
    resid_part = b_panel - summed
    resid = lax.all_gather(resid_part, "col", axis=0, tiled=True)
    y_full = triangle_solve(u_diag.T, resid, True)
    z_last = triangle_solve(l_diag.T, y_full, False)
    start = lax.axis_index("col") * share
    contract = (((0,), (0,)), ((), ()))
    y_tail = y_prev[y_prev.shape[0] - width :]
    y_before = from_root(y_tail, "row", lax.axis_size("row") - 1)
    z_part = lax.dynamic_slice_in_dim(z_last, start, share, 0)
    term = lax.dot_general(
        l_coupling, z_part, contract, precision=high, preferred_element_type=jnp.float32
    )
    couple = lax.psum(term, "col")
    tail_side = y_before - couple
    w_prev = triangle_solve(l_prev_diag.T, tail_side, False)
    stacked = jnp.concatenate([w_prev, z_last], axis=0)
    column_share = stacked.shape[1] // lax.axis_size("row")
    my_columns = lax.dynamic_slice_in_dim(
        stacked, lax.axis_index("row") * column_share, column_share, 1
    )
    selector = (perm[:, None] == jnp.arange(stacked.shape[0], dtype=jnp.int32)[None, :]).astype(
        jnp.float32
    )
    x_part = jnp.dot(selector, my_columns, precision=high, preferred_element_type=jnp.float32)
    y_part = lax.dynamic_slice_in_dim(y_full, start, share, 0)
    return (y_part, x_part)


def solution(mesh):
    return jax.shard_map(
        per_device,
        mesh=mesh,
        in_specs=(
            P("row", None),
            P("col", "row"),
            P("col", None),
            P(),
            P(),
            P("col", None),
            P(),
            P("col"),
        ),
        out_specs=(P("col", None), P("col", "row")),
        check_vma=False,
    )
```

profile of v0, /device:TPU:0, one launch (start us, length us, event | category | flops | bytes accessed | tf_op | source)
XLA Modules:
  0.0 310.6 jit_solution(10976952297782359105)
XLA Ops:
  7.2 1.2 copy-done
  8.4 8.2 %fusion.281 = f32[64,512]{1,0:T(8,128)} fusion(f32[64,4096]{1,0:T(8,128)S(1)} %copy-done, f32[4096,512]{1,0:T(8,128)} %param.8), kind=kOutput, calls=%fused_computation.595 | convolution fusion | flops 1610612736 | bytes 9568256 | tf_op jit(solution)/shard_map/dot_general | solution.py:57
  17.0 1.1 broadcast_select_fusion
  18.7 1.6 copy.14
  20.4 0.8 gather_fusion
  21.2 1.1 fusion.200
  22.3 1.6 convolution_add_fusion.119
  25.5 1.1 fusion.201
  26.6 1.6 convolution_add_fusion.114
  29.8 1.1 fusion.202
  30.8 1.6 convolution_add_fusion.109
  34.0 1.1 fusion.203
  35.1 1.7 convolution_add_fusion.104
  38.4 1.1 fusion.204
  39.4 1.6 convolution_add_fusion.99
  42.0 1.1 fusion.205
  43.1 1.6 convolution_add_fusion.94
  44.9 0.8 gather_fusion.6
  45.7 1.1 fusion.206
  46.8 1.6 convolution_add_fusion.89
  49.4 1.1 fusion.207
  50.5 1.6 convolution_add_fusion.84
  52.7 0.8 gather_fusion.8
  53.8 0.8 convolution_add_fusion.79
  55.9 0.8 convolution_add_fusion.34
  56.9 1.6 copy.17
  58.5 0.8 gather_fusion.9
  59.6 0.8 convolution_add_fusion.74
  61.7 0.8 convolution_add_fusion.69
  63.7 0.8 convolution_add_fusion.64
  65.8 0.8 convolution_add_fusion.59
  73.5 1.1 fusion.218
  74.6 1.0 convolution_add_fusion.29
  76.6 1.1 fusion.219
  77.7 1.0 convolution_add_fusion.24
  79.7 1.1 fusion.220
  80.8 1.0 convolution_add_fusion.19
  82.8 1.1 fusion.221
  83.9 1.0 convolution_add_fusion.14
  85.9 1.1 fusion.222
  87.0 1.1 convolution_add_fusion.9
  89.1 1.1 fusion.223
  90.2 1.0 convolution_add_fusion.4
  96.8 1.0 convolution_add_fusion.93
  127.8 1.6 sub.331
  132.1 0.8 fusion.98
  133.0 1.0 fusion.99
  134.0 1.0 fusion.100
  135.0 1.6 fusion.102
  136.6 1.0 fusion.103
  137.6 34.8 %all-gather.2.cloned.1.call-done = f32[512,512]{1,0:T(8,128)} async-done(((f32[64,512]{1,0:T(8,128)}), f32[512,512]{1,0:T(8,128)}) %all-gather.2.cloned.1.call-update) | async-done | bytes 1048592 | tf_op jit(solution)/shard_map/all_gather | solution.py:60
  172.4 1.3 constant_dynamic-update-slice_fusion.7
  173.7 1.2 fusion.83
  175.2 1.2 fusion.82
  176.4 1.1 fusion.81
  177.5 1.0 fusion.80
  178.5 1.1 fusion.79
  179.6 1.0 fusion.77
  180.6 1.1 fusion.76
  200.7 2.0 convolution_bitcast_fusion
  204.2 1.6 constant_dynamic-slice_fusion
  205.8 74.0 %all-reduce.4.cloned.1.call-done = f32[512,512]{0,1:T(8,128)} async-done(((f32[512,512]{0,1:T(8,128)}), f32[512,512]{0,1:T(8,128)}) %all-reduce.4.cloned.1.call-update) | async-done | bytes 1048592 | tf_op jit(solution)/shard_map/psum | solution.py:71
  279.8 1.7 sub.404
  302.8 1.1 fusion.108
  (500 shorter events, 105.0 us)
Async XLA Ops:
  7.2 120.6 %all-reduce.6.cloned.1.call-start = ((), (), s32[]{:S(2)}) async-start(), calls=%async_computation.2 | async-start | bytes 2359296 | tf_op jit(solution)/shard_map/psum | solution.py:58
  8.4 8.2 %slice-start = ((f32[4096,512]{1,0:T(8,128)}), f32[512,512]{1,0:T(8,128)S(1)}, s32[]{:S(2)}) async-start(f32[4096,512]{1,0:T(8,128)} %param.8), calls=%async_computation.3 | async-start | bytes 2097152 | tf_op jit(solution)/shard_map/slice | solution.py:65
  18.1 154.3 %all-gather.2.cloned.1.call-start = ((), (), s32[]{:S(2)}) async-start(), calls=%async_computation | async-start | bytes 1179648 | tf_op jit(solution)/shard_map/all_gather | solution.py:60
  21.2 12.8 %copy-start.42 = (f32[64]{0:T(128)}, f32[64]{0:T(128)S(1)}, u32[]{:S(2)}) copy-start(f32[64]{0:T(128)S(1)} %gather_fusion) | copy-start | bytes 772
  25.5 19.4 %copy-start.44 = (f32[64]{0:T(128)}, f32[64]{0:T(128)S(1)}, u32[]{:S(2)}) copy-start(f32[64]{0:T(128)S(1)} %gather_fusion.1) | copy-start | bytes 772
  29.8 18.8 %copy-start.46 = (f32[64]{0:T(128)}, f32[64]{0:T(128)S(1)}, u32[]{:S(2)}) copy-start(f32[64]{0:T(128)S(1)} %gather_fusion.2) | copy-start | bytes 772
  34.0 18.2 %copy-start.48 = (f32[64]{0:T(128)}, f32[64]{0:T(128)S(1)}, u32[]{:S(2)}) copy-start(f32[64]{0:T(128)S(1)} %gather_fusion.3) | copy-start | bytes 772
  35.1 17.1 %copy-start.6 = (f32[512,512]{1,0:T(8,128)S(1)}, f32[512,512]{1,0:T(8,128)}, u32[]{:S(2)}) copy-start(f32[512,512]{1,0:T(8,128)} %param.14) | copy-start | bytes 3145732
  38.4 14.2 %copy-start.50 = (f32[64]{0:T(128)}, f32[64]{0:T(128)S(1)}, u32[]{:S(2)}) copy-start(f32[64]{0:T(128)S(1)} %gather_fusion.4) | copy-start | bytes 772
  42.0 10.6 %copy-start.52 = (f32[64]{0:T(128)}, f32[64]{0:T(128)S(1)}, u32[]{:S(2)}) copy-start(f32[64]{0:T(128)S(1)} %gather_fusion.5) | copy-start | bytes 772
  52.6 4.1 %copy-start.3 = (f32[512,512]{0,1:T(8,128)}, f32[512,512]{0,1:T(8,128)S(1)}, u32[]{:S(2)}) copy-start(f32[512,512]{0,1:T(8,128)S(1)} %copy.15) | copy-start | bytes 3145732
  53.5 3.2 %copy-start.64 = (f32[64]{0:T(128)}, f32[64]{0:T(128)S(1)}, u32[]{:S(2)}) copy-start(f32[64]{0:T(128)S(1)} %gather_fusion.8) | copy-start | bytes 772
  59.4 8.9 %copy-start.68 = (f32[64]{0:T(128)}, f32[64]{0:T(128)S(1)}, u32[]{:S(2)}) copy-start(f32[64]{0:T(128)S(1)} %gather_fusion.9) | copy-start | bytes 772
  61.4 8.4 %copy-start.70 = (f32[64]{0:T(128)}, f32[64]{0:T(128)S(1)}, u32[]{:S(2)}) copy-start(f32[64]{0:T(128)S(1)} %gather_fusion.10) | copy-start | bytes 772
  67.6 8.2 %copy-start.54 = (f32[64]{0:T(128)}, f32[64]{0:T(128)S(1)}, u32[]{:S(2)}) copy-start(f32[64]{0:T(128)S(1)} %gather_fusion.13) | copy-start | bytes 772
  69.1 9.8 %copy-start.57 = (f32[64]{0:T(128)}, f32[64]{0:T(128)S(1)}, u32[]{:S(2)}) copy-start(f32[64]{0:T(128)S(1)} %gather_fusion.14) | copy-start | bytes 772
  70.6 11.4 %copy-start.60 = (f32[64]{0:T(128)}, f32[64]{0:T(128)S(1)}, u32[]{:S(2)}) copy-start(f32[64]{0:T(128)S(1)} %gather_fusion.15) | copy-start | bytes 772
  72.1 13.0 %copy-start.61 = (f32[64]{0:T(128)}, f32[64]{0:T(128)S(1)}, u32[]{:S(2)}) copy-start(f32[64]{0:T(128)S(1)} %gather_fusion.16) | copy-start | bytes 772
  73.5 14.7 %copy-start.62 = (f32[64]{0:T(128)}, f32[64]{0:T(128)S(1)}, u32[]{:S(2)}) copy-start(f32[64]{0:T(128)S(1)} %gather_fusion.18) | copy-start | bytes 772
  76.6 14.8 %copy-start.63 = (f32[64]{0:T(128)}, f32[64]{0:T(128)S(1)}, u32[]{:S(2)}) copy-start(f32[64]{0:T(128)S(1)} %gather_fusion.19) | copy-start | bytes 772
  77.7 13.7 %copy-start.10 = (f32[64,64]{1,0:T(8,128)S(1)}, f32[64,64]{1,0:T(8,128)}, u32[]{:S(2)}) copy-start(f32[64,64]{1,0:T(8,128)} %fusion.277) | copy-start | bytes 49156
  77.7 13.9 %copy-start.28 = (f32[64,64]{1,0:T(8,128)S(1)}, f32[64,64]{1,0:T(8,128)}, u32[]{:S(2)}) copy-start(f32[64,64]{1,0:T(8,128)} %convolution_add_fusion.119) | copy-start | bytes 49156
  78.9 13.5 %copy-start.9 = (f32[64,64]{1,0:T(8,128)S(1)}, f32[64,64]{1,0:T(8,128)}, u32[]{:S(2)}) copy-start(f32[64,64]{1,0:T(8,128)} %fusion.282) | copy-start | bytes 49156
  79.7 12.9 %copy-start.27 = (f32[64,64]{1,0:T(8,128)S(1)}, f32[64,64]{1,0:T(8,128)}, u32[]{:S(2)}) copy-start(f32[64,64]{1,0:T(8,128)} %convolution_add_fusion.114) | copy-start | bytes 49156
  81.8 11.7 %copy-start.8 = (f32[64,64]{1,0:T(8,128)S(1)}, f32[64,64]{1,0:T(8,128)}, u32[]{:S(2)}) copy-start(f32[64,64]{1,0:T(8,128)} %fusion.286) | copy-start | bytes 49156
  82.0 11.7 %copy-start.26 = (f32[64,64]{1,0:T(8,128)S(1)}, f32[64,64]{1,0:T(8,128)}, u32[]{:S(2)}) copy-start(f32[64,64]{1,0:T(8,128)} %convolution_add_fusion.109) | copy-start | bytes 49156
  82.8 11.7 %copy-start.7 = (f32[64,64]{1,0:T(8,128)S(1)}, f32[64,64]{1,0:T(8,128)}, u32[]{:S(2)}) copy-start(f32[64,64]{1,0:T(8,128)} %fusion.290) | copy-start | bytes 49156
  82.8 11.9 %copy-start.24 = (f32[64,64]{1,0:T(8,128)S(1)}, f32[64,64]{1,0:T(8,128)}, u32[]{:S(2)}) copy-start(f32[64,64]{1,0:T(8,128)} %convolution_add_fusion.104) | copy-start | bytes 49156
  85.1 10.7 %copy-start.23 = (f32[64,64]{1,0:T(8,128)S(1)}, f32[64,64]{1,0:T(8,128)}, u32[]{:S(2)}) copy-start(f32[64,64]{1,0:T(8,128)} %convolution_add_fusion.99) | copy-start | bytes 49156
  89.1 9.9 %copy-start.40 = (f32[64]{0:T(128)}, f32[64]{0:T(128)S(1)}, u32[]{:S(2)}) copy-start(f32[64]{0:T(128)S(1)} %gather_fusion.23) | copy-start | bytes 772
  89.1 9.6 %copy-start.21 = (f32[64,64]{1,0:T(8,128)S(1)}, f32[64,64]{1,0:T(8,128)}, u32[]{:S(2)}) copy-start(f32[64,64]{1,0:T(8,128)} %convolution_add_fusion.89) | copy-start | bytes 49156
  91.4 8.3 %copy-start.18 = (f32[64,64]{1,0:T(8,128)S(1)}, f32[64,64]{1,0:T(8,128)}, u32[]{:S(2)}) copy-start(f32[64,64]{1,0:T(8,128)} %convolution_add_fusion.84) | copy-start | bytes 49156
  92.5 8.3 %copy-start.20 = (f32[64,64]{1,0:T(8,128)S(1)}, f32[64,64]{1,0:T(8,128)}, u32[]{:S(2)}) copy-start(f32[64,64]{1,0:T(8,128)} %convolution_add_fusion.79) | copy-start | bytes 49156
  93.5 8.2 %copy-start.17 = (f32[64,64]{1,0:T(8,128)S(1)}, f32[64,64]{1,0:T(8,128)}, u32[]{:S(2)}) copy-start(f32[64,64]{1,0:T(8,128)} %convolution_add_fusion.34) | copy-start | bytes 49156
  94.5 8.2 %copy-start.19 = (f32[64,64]{1,0:T(8,128)S(1)}, f32[64,64]{1,0:T(8,128)}, u32[]{:S(2)}) copy-start(f32[64,64]{1,0:T(8,128)} %convolution_add_fusion.74) | copy-start | bytes 49156
  95.6 8.2 %copy-start.16 = (f32[64,64]{1,0:T(8,128)S(1)}, f32[64,64]{1,0:T(8,128)}, u32[]{:S(2)}) copy-start(f32[64,64]{1,0:T(8,128)} %convolution_add_fusion.69) | copy-start | bytes 49156
  96.6 8.2 %copy-start.15 = (f32[64,64]{1,0:T(8,128)S(1)}, f32[64,64]{1,0:T(8,128)}, u32[]{:S(2)}) copy-start(f32[64,64]{1,0:T(8,128)} %convolution_add_fusion.64) | copy-start | bytes 49156
  98.5 7.4 %copy-start.14 = (f32[64,64]{1,0:T(8,128)S(1)}, f32[64,64]{1,0:T(8,128)}, u32[]{:S(2)}) copy-start(f32[64,64]{1,0:T(8,128)} %convolution_add_fusion.59) | copy-start | bytes 49156
  109.7 12.2 %copy-start.43 = (f32[64]{0:T(128)S(1)}, f32[64]{0:T(128)}, u32[]{:S(2)}) copy-start(f32[64]{0:T(128)} %copy-done.42) | copy-start | bytes 772
  110.0 12.0 %copy-start.45 = (f32[64]{0:T(128)S(1)}, f32[64]{0:T(128)}, u32[]{:S(2)}) copy-start(f32[64]{0:T(128)} %copy-done.44) | copy-start | bytes 772
  110.8 11.4 %copy-start.47 = (f32[64]{0:T(128)S(1)}, f32[64]{0:T(128)}, u32[]{:S(2)}) copy-start(f32[64]{0:T(128)} %copy-done.46) | copy-start | bytes 772
  111.6 10.8 %copy-start.49 = (f32[64]{0:T(128)S(1)}, f32[64]{0:T(128)}, u32[]{:S(2)}) copy-start(f32[64]{0:T(128)} %copy-done.48) | copy-start | bytes 772
  111.7 10.8 %copy-start.51 = (f32[64]{0:T(128)S(1)}, f32[64]{0:T(128)}, u32[]{:S(2)}) copy-start(f32[64]{0:T(128)} %copy-done.50) | copy-start | bytes 772
  111.9 10.8 %copy-start.53 = (f32[64]{0:T(128)S(1)}, f32[64]{0:T(128)}, u32[]{:S(2)}) copy-start(f32[64]{0:T(128)} %copy-done.52) | copy-start | bytes 772
  112.1 11.4 %copy-start.56 = (f32[64]{0:T(128)S(1)}, f32[64]{0:T(128)}, u32[]{:S(2)}) copy-start(f32[64]{0:T(128)} %copy-done.55) | copy-start | bytes 772
  113.0 11.3 %copy-start.59 = (f32[64]{0:T(128)S(1)}, f32[64]{0:T(128)}, u32[]{:S(2)}) copy-start(f32[64]{0:T(128)} %copy-done.58) | copy-start | bytes 772
  113.8 11.3 %copy-start.65 = (f32[64]{0:T(128)S(1)}, f32[64]{0:T(128)}, u32[]{:S(2)}) copy-start(f32[64]{0:T(128)} %copy-done.64) | copy-start | bytes 772
  114.0 11.9 %copy-start.67 = (f32[64]{0:T(128)S(1)}, f32[64]{0:T(128)}, u32[]{:S(2)}) copy-start(f32[64]{0:T(128)} %copy-done.66) | copy-start | bytes 772
  114.3 12.5 %copy-start.69 = (f32[64]{0:T(128)S(1)}, f32[64]{0:T(128)}, u32[]{:S(2)}) copy-start(f32[64]{0:T(128)} %copy-done.68) | copy-start | bytes 772
  114.5 13.1 %copy-start.71 = (f32[64]{0:T(128)S(1)}, f32[64]{0:T(128)}, u32[]{:S(2)}) copy-start(f32[64]{0:T(128)} %copy-done.70) | copy-start | bytes 772
  116.1 11.7 %copy-start.11 = (f32[64,512]{1,0:T(8,128)S(1)}, f32[64,512]{1,0:T(8,128)}, u32[]{:S(2)}) copy-start(f32[64,512]{1,0:T(8,128)} %param.10) | copy-start | bytes 393220
  118.9 13.2 %copy-start.22 = (f32[64,64]{1,0:T(8,128)S(1)}, f32[64,64]{1,0:T(8,128)}, u32[]{:S(2)}) copy-start(f32[64,64]{1,0:T(8,128)} %convolution_add_fusion.46) | copy-start | bytes 49156
  119.3 13.7 %copy-start.25 = (f32[64,64]{1,0:T(8,128)S(1)}, f32[64,64]{1,0:T(8,128)}, u32[]{:S(2)}) copy-start(f32[64,64]{1,0:T(8,128)} %fusion.346) | copy-start | bytes 49156
  129.4 150.4 %all-reduce.4.cloned.1.call-start = ((), (), s32[]{:S(2)}) async-start(), calls=%async_computation.1 | async-start | bytes 2097152 | tf_op jit(solution)/shard_map/psum | solution.py:71
  172.4 5.1 %copy-start.5 = (f32[512,512]{1,0:T(8,128)S(1)}, f32[512,512]{1,0:T(8,128)}, u32[]{:S(2)}) copy-start(f32[512,512]{1,0:T(8,128)} %all-gather.2.cloned.1.call-done) | copy-start | bytes 3145732
  172.4 9.6 %copy-start.2 = (f32[512,512]{0,1:T(8,128)S(1)}, f32[512,512]{0,1:T(8,128)}, u32[]{:S(2)}) copy-start(f32[512,512]{0,1:T(8,128)} %copy-done.1) | copy-start | bytes 3145732
  189.6 3.4 %copy-start.13 = (f32[512,512]{1,0:T(8,128)}, f32[512,512]{1,0:T(8,128)S(1)}, u32[]{:S(2)}) copy-start(f32[512,512]{1,0:T(8,128)S(1)} %get-tuple-element.42) | copy-start | bytes 3145732
  197.0 3.3 %copy-start.34 = (f32[64,64]{1,0:T(8,128)S(1)}, f32[64,64]{1,0:T(8,128)}, u32[]{:S(2)}) copy-start(f32[64,64]{1,0:T(8,128)} %fusion.93) | copy-start | bytes 49156
  200.6 3.5 %copy-start.41 = (f32[64]{0:T(128)S(1)}, f32[64]{0:T(128)}, u32[]{:S(2)}) copy-start(f32[64]{0:T(128)} %copy-done.40) | copy-start | bytes 772
  202.7 78.8 %copy-start.32 = (f32[64,64]{1,0:T(8,128)S(1)}, f32[64,64]{1,0:T(8,128)}, u32[]{:S(2)}) copy-start(f32[64,64]{1,0:T(8,128)} %fusion.101) | copy-start | bytes 49156
  203.7 78.4 %copy-start.4 = (f32[512,512]{0,1:T(8,128)S(1)}, f32[512,512]{0,1:T(8,128)}, u32[]{:S(2)}) copy-start(f32[512,512]{0,1:T(8,128)} %copy-done.3) | copy-start | bytes 3145732
  282.7 3.8 %copy-start.33 = (f32[64,64]{1,0:T(8,128)S(1)}, f32[64,64]{1,0:T(8,128)}, u32[]{:S(2)}) copy-start(f32[64,64]{1,0:T(8,128)} %fusion.102) | copy-start | bytes 49156
  288.1 3.5 %copy-start.38 = (f32[64,64]{1,0:T(8,128)S(1)}, f32[64,64]{1,0:T(8,128)}, u32[]{:S(2)}) copy-start(f32[64,64]{1,0:T(8,128)} %fusion.104) | copy-start | bytes 49156
  298.2 3.9 %copy-start.31 = (f32[64,64]{1,0:T(8,128)S(1)}, f32[64,64]{1,0:T(8,128)}, u32[]{:S(2)}) copy-start(f32[64,64]{1,0:T(8,128)} %fusion.92) | copy-start | bytes 49156
  (12 other events, 25.1 us)
Sparse Core Ops, SparseCore 0:
  18.2 40.3 all-reduce.5
  129.5 42.8 all-gather.1
  202.9 76.9 all-reduce.3
where the time goes:
time: 316 us; the launch traced here: 311 us
  matrix products  152 us (48%)
  waiting for transfers between devices  109 us (34%)
  local copies, waits for them, and re-layouts  26.8 us (8%)
  between operations  17.4 us (6%)
  other arithmetic  4.43 us (1%)
    psum x1, waiting for transfers between devices, per_device(): couple = lax.psum(term, 'col')  74 us
    dot_general x120, matrix products, block_inverse(): jnp.dot(inverse, power, precision=high, preferred_element_type=jnp.float32)  55 us
    dot_general x84, matrix products, triangle_solve(): jnp.dot(matrix[low:low + block_size, left:left + block_size], solved[othe...  39.2 us
    dot_general x120, matrix products, block_inverse(): jnp.dot(power, power, precision=high, preferred_element_type=jnp.float32)  37.8 us
    all_gather x1, waiting for transfers between devices, per_device(): resid = lax.all_gather(resid_part, 'col', axis=0, tiled=True)  34.8 us
    gather x24, local copies, waits for them, and re-layouts, block_inverse(): pivots = jnp.diagonal(block)  19.4 us
    dot_general x24, matrix products, triangle_solve(): jnp.dot(inverse, remain, precision=high, preferred_element_type=jnp.float32)  8.83 us
    dot_general x1, matrix products, per_device(): jnp.dot(u_cols, y_prev, precision=high, preferred_element_type=jnp.float32)  8.23 us
  transfers between devices with their start and end apart: 3, of which 2 were waited for; matrix products, arithmetic and copies ran while one was open for 38% of the time, Pallas kernels for 0%

commit v1 on v0

v1 whole, which is shorter than its diff:
```python
import functools

import jax
import jax.numpy as jnp
from jax import lax
from jax.experimental import pallas as pl
from jax.experimental.pallas import tpu as pltpu
from jax.sharding import PartitionSpec as P

F32, BF16 = jnp.float32, jnp.bfloat16
TILE = 128
BASE = 16
VMEM = pl.BlockSpec(memory_space=pltpu.VMEM)
SMEM = pl.BlockSpec(memory_space=pltpu.SMEM)


def halves(value):
    high = value.astype(BF16)
    return high, (value - high.astype(F32)).astype(BF16)


def mm(left, right):
    return jnp.dot(left, right, preferred_element_type=F32)


def dot3(left, right):
    lh, ll = left if isinstance(left, tuple) else halves(left)
    rh, rl = right if isinstance(right, tuple) else halves(right)
    return mm(lh, rh) + (mm(lh, rl) + mm(ll, rh))


def tile_of(ref, i, j):
    return ref[i * TILE : (i + 1) * TILE, j * TILE : (j + 1) * TILE]


def iotas():
    shape = (TILE, TILE)
    return lax.broadcasted_iota(jnp.int32, shape, 0), lax.broadcasted_iota(jnp.int32, shape, 1)


def unit_lower_inverses(blocks):
    rows, cols = iotas()
    shift = BASE.bit_length() - 1
    same = (rows >> shift) == (cols >> shift)
    eye = (rows == cols).astype(F32)
    base = rows & ~(BASE - 1)
    found = []
    for block in blocks:
        inner = jnp.where(same & (rows > cols), block, 0.0)
        inv = eye
        for i in range(BASE - 1):
            column = jnp.take_along_axis(inner, base + i, axis=1)
            pivot = inv.reshape(TILE // BASE, BASE, TILE)[:, i : i + 1, :]
            pivot = jnp.broadcast_to(pivot, (TILE // BASE, BASE, TILE)).reshape(TILE, TILE)
            inv = inv - column * pivot
        found.append(inv)
    size = BASE
    while size < TILE:
        shift = size.bit_length() - 1
        off = ((rows >> (shift + 1)) == (cols >> (shift + 1))) & ((rows >> shift) > (cols >> shift))
        parts = [halves(inv) for inv in found]
        mids = [dot3(part, jnp.where(off, block, 0.0)) for part, block in zip(parts, blocks)]
        found = [inv - dot3(mid, part) for inv, mid, part in zip(found, mids, parts)]
        size *= 2
    return found


def prepare_kernel(u_ref, l_ref, lp_ref, perm_ref, tail_ref, use_ref, du_ref, dl_ref, a_ref, v_ref):
    width = u_ref.shape[0]
    count = width // TILE
    rows, cols = iotas()
    diag = rows == cols
    blocks, scales = [], []
    for i in range(count):
        upper = tile_of(u_ref, i, i).T
        pivot_col = 1.0 / jnp.sum(jnp.where(diag, upper, 0.0), axis=1, keepdims=True)
        pivot_row = 1.0 / jnp.sum(jnp.where(diag, upper, 0.0), axis=0, keepdims=True)
        blocks.append(upper * pivot_col)
        scales.append(pivot_row)
    blocks += [tile_of(l_ref, i, i) for i in range(count)]
    blocks += [tile_of(lp_ref, i, i) for i in range(count)]
    found = unit_lower_inverses(blocks)
    for i in range(count):
        du_ref[i * TILE : (i + 1) * TILE, :] = (found[i] * scales[i]).T
        dl_ref[i * TILE : (i + 1) * TILE, :] = found[count + i]
    inv_prev = found[2 * count :]
    perm = perm_ref[...]
    picks = perm.shape[1]
    solved = []
    for i in range(count):
        row_ids = i * TILE + lax.broadcasted_iota(jnp.int32, (TILE, picks), 0)
        remain = (row_ids == perm).astype(F32)
        for j in range(i):
            remain = remain - dot3(tile_of(lp_ref, i, j), solved[j])
        solved.append(halves(dot3(inv_prev[i], remain)))
        a_ref[i * TILE : (i + 1) * TILE, :] = solved[i][0].astype(F32) + solved[i][1].astype(F32)
    a_t = jnp.concatenate([a_ref[i * TILE : (i + 1) * TILE, :].T for i in range(count)], axis=1)
    scale = use_ref[0, 0]
    v_ref[...] = dot3(a_t, tail_ref[...]) * scale


def solve_u_kernel(resid_ref, u_ref, du_ref, where_ref, yt_ref, y_ref, full_ref):
    count = u_ref.shape[0] // TILE
    share = y_ref.shape[0]
    solved = []
    for i in range(count):
        span = slice(i * TILE, (i + 1) * TILE)
        remain = resid_ref[span, :].T
        for j in range(i):
            remain = remain - dot3(solved[j], tile_of(u_ref, j, i))
        value = dot3(remain, du_ref[span, :])
        yt_ref[:, span] = value
        full_ref[span, :] = value.T
        solved.append(halves(value))
    y_ref[...] = full_ref[pl.ds(pl.multiple_of(where_ref[0, 0] * share, share), share), :]


def finish_kernel(yt_ref, l_ref, dl_ref, lc_ref, a_ref, perm_ref, v_ref, x_ref):
    width = l_ref.shape[0]
    count = width // TILE
    perm = perm_ref[...]
    picks = perm.shape[1]
    solved = {}
    total = None
    for i in reversed(range(count)):
        span = slice(i * TILE, (i + 1) * TILE)
        remain = yt_ref[:, span]
        for j in range(i + 1, count):
            remain = remain - dot3(solved[j], tile_of(l_ref, j, i))
        solved[i] = halves(dot3(remain, dl_ref[span, :]))
        row_ids = width + i * TILE + lax.broadcasted_iota(jnp.int32, (TILE, picks), 0)
        select = (row_ids == perm).astype(F32).astype(BF16)
        term = mm(solved[i][0], select) + mm(solved[i][1], select)
        total = term if total is None else total + term
    z = tuple(jnp.concatenate([solved[i][k] for i in range(count)], axis=1) for k in range(2))
    couple = dot3(z, lc_ref[...])
    total = total - dot3(couple, a_ref[...])
    x_ref[...] = total.T + v_ref[...]


def call(kernel, outs, flops, bytes_accessed, scratch=(), **specs):
    return pl.pallas_call(
        kernel,
        out_shape=outs,
        scratch_shapes=scratch,
        cost_estimate=pl.CostEstimate(flops=flops, bytes_accessed=bytes_accessed, transcendentals=0),
        compiler_params=pltpu.CompilerParams(vmem_limit_bytes=48 << 20),
        **specs,
    )


def shape(*dims):
    return jax.ShapeDtypeStruct(dims, F32)


def inner_size(size):
    inner = 1
    while inner * inner * 4 <= size and size % (inner * 2) == 0:
        inner *= 2
    return inner


def shifted(value, axis, size, step, group):
    stride, length = group
    pairs = []
    for dst in range(size):
        place = (dst // stride) % length
        src = dst + ((place + step) % length - place) * stride
        pairs.append((src, dst))
    return lax.ppermute(value, axis, pairs)


def ordered(parts, place):
    count = len(parts)
    stack = jnp.concatenate(parts + parts[: count - 1], axis=0)
    rows = parts[0].shape[0]
    return lax.dynamic_slice_in_dim(stack, lax.rem(count - place, count) * rows, count * rows, 0)


def gather_group(value, axis, size, group):
    stride, length = group
    parts = [value] + [shifted(value, axis, size, step, group) for step in range(1, length)]
    place = lax.rem(lax.axis_index(axis) // stride, length)
    return ordered(parts, place)


def per_device(y_prev, u_cols, b_panel, u_diag, l_diag, l_coupling, l_prev_diag, perm):
    width = u_diag.shape[0]
    share = u_cols.shape[0]
    row_size, col_size = lax.axis_size("row"), lax.axis_size("col")
    row, col = lax.axis_index("row"), lax.axis_index("col")
    column_share = b_panel.shape[1] // row_size
    picks = perm.shape[0]

    coupling = lax.all_gather(l_coupling, "col", axis=0, tiled=True)
    partial_value = jnp.dot(u_cols, y_prev, precision=lax.Precision.HIGH, preferred_element_type=F32)
    perm_row = jnp.pad(perm, (0, max(TILE - picks, 0)), constant_values=-1)[None, :]
    lanes = perm_row.shape[1]
    use = (row == row_size - 1).astype(F32).reshape(1, 1)
    tail = y_prev[y_prev.shape[0] - width :]
    du, dl, a, v = call(
        prepare_kernel,
        (shape(width, TILE), shape(width, TILE), shape(width, lanes), shape(lanes, b_panel.shape[1])),
        1 << 30,
        6 << 20,
        in_specs=[VMEM] * 5 + [SMEM],
        out_specs=[VMEM] * 4,
    )(u_diag, l_diag, l_prev_diag, perm_row, tail, use)

    payload = jnp.concatenate([partial_value, v], axis=0)
    blocks = lambda place: lax.dynamic_slice_in_dim(payload, place * column_share, column_share, 1)
    own = blocks(row)
    for step in range(1, row_size):
        target = lax.rem(row + row_size - step, row_size)
        own = own + shifted(blocks(target), "row", row_size, step, (1, row_size))
    mine = lax.dynamic_slice_in_dim(b_panel, row * column_share, column_share, 1)
    resid = mine - own[:share]
    v_mine = own[share:]

    inner = inner_size(col_size)
    resid = gather_group(resid, "col", col_size, (1, inner))
    resid = gather_group(resid, "col", col_size, (inner, col_size // inner))

    rhs = max(TILE, column_share)
    widen = lambda value: jnp.pad(value, ((0, 0), (0, rhs - value.shape[1])))
    where = col.astype(jnp.int32).reshape(1, 1)
    yt, y_mine = call(
        solve_u_kernel,
        (shape(rhs, width), shape(share, rhs)),
        200 << 20,
        2 << 20,
        scratch=[pltpu.VMEM((width, rhs), F32)],
        in_specs=[VMEM] * 3 + [SMEM],
        out_specs=[VMEM] * 2,
    )(widen(resid), u_diag, du, where)
    y_part = lax.all_gather(y_mine[:, :column_share], "row", axis=1, tiled=True)

    x = call(
        finish_kernel,
        shape(lanes, rhs),
        400 << 20,
        4 << 20,
        in_specs=[VMEM] * 7,
        out_specs=VMEM,
    )(yt, l_diag, dl, coupling, a, perm_row, widen(v_mine))
    return (y_part, x[:picks, :column_share])


def solution(mesh):
    return jax.shard_map(
        per_device,
        mesh=mesh,
        in_specs=(
            P("row", None),
            P("col", "row"),
            P("col", None),
            P(),
            P(),
            P("col", None),
            P(),
            P("col"),
        ),
        out_specs=(P("col", None), P("col", "row")),
        check_vma=False,
    )
```

time: 316 us -> 86.4 us (0.27); the launches traced: 311 us -> 85.8 us
  matrix products: 152 us -> 6.08 us
  waiting for transfers between devices: 109 us -> 12.4 us
  Pallas kernels: 0 us -> 15.6 us
  starting transfers between devices: 0.86 us -> 9.71 us
  local copies, waits for them, and re-layouts: 26.8 us -> 18.8 us
  blocking collectives: 0 us -> 5.91 us
  between operations: 17.4 us -> 14.2 us
    dot_general x351 -> x1, matrix products: 152 us -> 6.08 us  [per_device(): jnp.dot(u_cols, y_prev, precision=lax.Precision.HIGH, preferred_element_t...]
    psum x2 -> x0, waiting for transfers between devices: 74 us -> none  [the longest x1 74 us: per_device(): couple = lax.psum(term, 'col')]
    all_gather x1, waiting for transfers between devices: 34.8 us -> 0.01 us  [per_device(): coupling = lax.all_gather(l_coupling, 'col', axis=0, tiled=True)]
    gather x24 -> x0, local copies, waits for them, and re-layouts: 19.4 us -> none  [block_inverse(): pivots = jnp.diagonal(block)]
    pallas_call x0 -> x3, Pallas kernels: none -> 15.6 us  [the longest x1 11.7 us: per_device(): call(prepare_kernel, (shape(width, TILE), shape(width, TILE), shape(width...]
    ppermute x0 -> x7, waiting for transfers between devices: none -> 11.7 us  [shifted(): return lax.ppermute(value, axis, pairs)]
    ppermute x0 -> x7, starting transfers between devices: none -> 9.68 us  [shifted(): return lax.ppermute(value, axis, pairs)]
    unnamed x168 -> x34, local copies, waits for them, and re-layouts: 5.54 us -> 13.9 us
  transfers between devices with their start and end apart: 3 -> 8, of which waited for: 2 -> 5; matrix products, arithmetic and copies ran while one was open for 38% -> 20% of each run, Pallas kernels for 0% -> 15%
where the time goes in v1:
time: 86.4 us; the launch traced here: 85.8 us
  local copies, waits for them, and re-layouts  18.8 us (22%)
  Pallas kernels  15.6 us (18%)
  between operations  14.2 us (16%)
  waiting for transfers between devices  12.4 us (14%)
  starting transfers between devices  9.71 us (11%)
  matrix products  6.08 us (7%)
  blocking collectives  5.91 us (7%)
  other arithmetic  3.17 us (4%)
    unnamed x34, local copies, waits for them, and re-layouts  13.9 us
    pallas_call x1, Pallas kernels, per_device(): call(prepare_kernel, (shape(width, TILE), shape(width, TILE), shape(width...  11.7 us
    ppermute x7, waiting for transfers between devices, shifted(): return lax.ppermute(value, axis, pairs)  11.7 us
    ppermute x7, starting transfers between devices, shifted(): return lax.ppermute(value, axis, pairs)  9.68 us
    dot_general x1, matrix products, per_device(): jnp.dot(u_cols, y_prev, precision=lax.Precision.HIGH, preferred_element_t...  6.08 us
    all_gather x1, blocking collectives, per_device(): y_part = lax.all_gather(y_mine[:, :column_share], 'row', axis=1, tiled=True)  5.91 us
    pallas_call x1, Pallas kernels, per_device(): call(finish_kernel, shape(lanes, rhs), 400 << 20, 4 << 20, in_specs=[VMEM...  2.62 us
    slice x1, local copies, waits for them, and re-layouts, per_device(): tail = y_prev[y_prev.shape[0] - width:]  2.4 us
  transfers between devices with their start and end apart: 8, of which 5 were waited for; matrix products, arithmetic and copies ran while one was open for 20% of the time, Pallas kernels for 15%

profile of v1, /device:TPU:0, one launch (start us, length us, event | category | flops | bytes accessed | tf_op | source)
XLA Modules:
  0.0 85.8 jit_solution(15631284667564564280)
XLA Ops:
  7.2 0.0 copy-start
  7.2 0.0 copy-start.12
  7.2 0.0 copy-start.2
  7.2 0.0 copy-start.1
  7.2 0.0 all-gather.2.cloned.1.call-start
  7.3 0.7 all-gather.2.cloned.1.call-update
  8.0 2.4 %slice.9.tail_ref = f32[512,512]{1,0:T(8,128)} slice(f32[4096,512]{1,0:T(8,128)} %param.8), slice={[3584:4096], [0:512]} | slice | bytes 2097152 | tf_op jit(solution)/shard_map/slice | solution.py:200
  10.4 0.0 copy-done
  10.4 6.1 %fusion.10 = f32[64,512]{1,0:T(8,128)S(1)} fusion(f32[64,4096]{1,0:T(8,128)S(1)} %copy-done, f32[4096,512]{1,0:T(8,128)} %param.8), kind=kOutput, calls=%fused_computation.29 | convolution fusion | flops 805306368 | bytes 9568256 | tf_op jit(solution)/shard_map/dot_general | solution.py:196
  16.5 0.0 copy-done.12
  16.5 0.0 copy-done.2
  16.5 0.0 copy-done.1
  16.5 0.0 copy-start.3
  16.5 1.2 %copy-done.3 = f32[512,512]{1,0:T(8,128)S(1)} copy-done((f32[512,512]{1,0:T(8,128)S(1)}, f32[512,512]{1,0:T(8,128)}, u32[]{:S(2)}) %copy-start.3) | copy-done | bytes 1048600
  17.7 0.0 copy-start.4
  17.7 1.2 %copy-done.4 = f32[512,512]{1,0:T(8,128)S(1)} copy-done((f32[512,512]{1,0:T(8,128)S(1)}, f32[512,512]{1,0:T(8,128)}, u32[]{:S(2)}) %copy-start.4) | copy-done | bytes 1048600
  19.0 11.7 %shard_map.95 = (f32[512,128]{1,0:T(8,128)S(1)}, f32[512,128]{1,0:T(8,128)S(1)}, f32[512,128]{1,0:T(8,128)S(1)}, f32[128,512]{1,0:T(8,128)S(1)}) custom-call(f32[512,512]{1,0:T(8,128)S(1)} %copy-done.2, f32[512,512]{1,0:T(8,128)S(1)} %copy-done.1, f32[512,512]{1,0:T(8,128)S(1)} %copy-done.4, s32[1,128]{1,0:T(1,128)S(1)} %bitcast.5, ...), custom_call_target="tpu_custom_call" | custom-call | flops 1073741824 | bytes 6291456 | tf_op jit(solution)/shard_map/pallas_call | solution.py:201
  30.7 0.0 copy-start.6
  30.7 0.7 copy-done.6
  31.4 0.0 copy-start.8
  31.4 0.7 copy-done.8
  32.1 0.0 copy-start.10
  32.1 0.7 copy-done.10
  32.8 0.7 fusion.5
  33.5 2.4 %collective-permute-start = (f32[192,128]{1,0:T(8,128)}, f32[192,128]{1,0:T(8,128)}, u32[]{:S(2)}, u32[]{:S(2)}) collective-permute-start(f32[192,128]{1,0:T(8,128)} %get-tuple-element.16), channel_id=1, source_target_pairs={{8,0},{16,8},{24,16},{0,24},{9,1},{17,9},{25,17},{1,25},{10,2},{18... | collective-permute-start | bytes 294920 | tf_op jit(solution)/shard_map/ppermute | solution.py:170
  35.9 0.6 collective-permute-start.1
  36.4 0.2 collective-permute-start.2
  36.7 2.6 %collective-permute-done = f32[192,128]{1,0:T(8,128)} collective-permute-done((f32[192,128]{1,0:T(8,128)}, f32[192,128]{1,0:T(8,128)}, u32[]{:S(2)}, u32[]{:S(2)}) %collective-permute-start) | collective-permute-done | bytes 98336 | tf_op jit(solution)/shard_map/ppermute | solution.py:170
  39.2 3.1 %collective-permute-done.1 = f32[192,128]{1,0:T(8,128)} collective-permute-done((f32[192,128]{1,0:T(8,128)}, f32[192,128]{1,0:T(8,128)}, u32[]{:S(2)}, u32[]{:S(2)}) %collective-permute-start.1) | collective-permute-done | bytes 98336 | tf_op jit(solution)/shard_map/ppermute | solution.py:170
  42.3 0.0 collective-permute-done.2
  42.3 1.0 %fusion.4 = f32[192,128]{1,0:T(8,128)S(1)} fusion(f32[192,128]{1,0:T(8,128)} %collective-permute-done.2, f32[192,128]{1,0:T(8,128)} %collective-permute-done.1, f32[192,128]{1,0:T(8,128)} %collective-permute-done, s32[]{:T(128)S(6)} %select_n.25, f32[128,512]{1,0:T(8,128)S(1)} %get-tuple-element.8, f32[64,512]{1,0:T(8,128)S(1)} %fusion.10), kind=kLoop, calls=%fused_computation.12 | loop fusion | flops 98304 | bytes 786436 | tf_op jit(solution)/shard_map/add | solution.py:215
  43.4 0.0 copy-start.13
  43.4 0.6 copy-done.13
  44.0 0.8 slice_subtract_fusion
  44.8 1.7 %collective-permute-start.3 = (f32[64,128]{1,0:T(8,128)S(1)}, f32[64,128]{1,0:T(8,128)S(1)}, u32[]{:S(2)}, u32[]{:S(2)}) collective-permute-start(f32[64,128]{1,0:T(8,128)S(1)} %slice_subtract_fusion), channel_id=1, source_target_pairs={{1,0},{0,1},{3,2},{2,3},{5,4},{4,5},{7,6},{6,7},{9,8},{8,9},{11,10... | collective-permute-start | bytes 98312 | tf_op jit(solution)/shard_map/ppermute | solution.py:170
  46.5 2.2 %collective-permute-done.3 = f32[64,128]{1,0:T(8,128)S(1)} collective-permute-done((f32[64,128]{1,0:T(8,128)S(1)}, f32[64,128]{1,0:T(8,128)S(1)}, u32[]{:S(2)}, u32[]{:S(2)}) %collective-permute-start.3) | collective-permute-done | bytes 32800 | tf_op jit(solution)/shard_map/ppermute | solution.py:170
  48.7 0.7 constant_dynamic-update-slice_fusion.6
  49.4 3.8 %collective-permute-start.4 = (f32[128,128]{1,0:T(8,128)S(1)}, f32[128,128]{1,0:T(8,128)S(1)}, u32[]{:S(2)}, u32[]{:S(2)}) collective-permute-start(f32[128,128]{1,0:T(8,128)S(1)} %get-tuple-element.15), channel_id=1, source_target_pairs={{2,0},{3,1},{4,2},{5,3},{6,4},{7,5},{0,6},{1,7},{10,8},{11,9},{12,... | collective-permute-start | bytes 196616 | tf_op jit(solution)/shard_map/ppermute | solution.py:170
  53.1 0.8 slice.13.v_ref
  54.0 0.0 collective-permute-start.5
  54.0 1.0 %collective-permute-start.6 = (f32[128,128]{1,0:T(8,128)S(1)}, f32[128,128]{1,0:T(8,128)S(1)}, u32[]{:S(2)}, u32[]{:S(2)}) collective-permute-start(f32[128,128]{1,0:T(8,128)S(1)} %get-tuple-element.15), channel_id=1, source_target_pairs={{6,0},{7,1},{0,2},{1,3},{2,4},{3,5},{4,6},{5,7},{14,8},{15,9},{8,1... | collective-permute-start | bytes 196616 | tf_op jit(solution)/shard_map/ppermute | solution.py:170
  55.0 0.0 collective-permute-done.4
  55.0 0.6 constant_dynamic-update-slice_fusion.5
  55.7 3.5 %collective-permute-done.5 = f32[128,128]{1,0:T(8,128)S(1)} collective-permute-done((f32[128,128]{1,0:T(8,128)S(1)}, f32[128,128]{1,0:T(8,128)S(1)}, u32[]{:S(2)}, u32[]{:S(2)}) %collective-permute-start.5) | collective-permute-done | bytes 65568 | tf_op jit(solution)/shard_map/ppermute | solution.py:170
  59.1 0.6 constant_dynamic-update-slice_fusion.4
  59.8 0.3 collective-permute-done.6
  60.0 0.6 constant_dynamic-update-slice_fusion.3
  60.7 0.6 constant_dynamic-update-slice_fusion.2
  61.3 0.6 constant_dynamic-update-slice_fusion.1
  61.9 0.6 constant_dynamic-update-slice_fusion
  62.5 1.0 %constant_dynamic-slice_fusion.resid_ref = f32[512,128]{1,0:T(8,128)S(1)} fusion(f32[896,128]{1,0:T(8,128)} %constant_dynamic-update-slice_fusion, s32[]{:T(128)S(6)} %select_n.31), kind=kLoop, calls=%fused_computation.28 | loop fusion | bytes 524292 | tf_op jit(solution)/shard_map/dynamic_slice | solution.py:177
  63.5 0.0 copy-start.11
  63.5 0.9 %copy-done.11 = f32[512,128]{1,0:T(8,128)S(1)} copy-done((f32[512,128]{1,0:T(8,128)S(1)}, f32[512,128]{1,0:T(8,128)}, u32[]{:S(2)}) %copy-start.11) | copy-done | bytes 262168
  64.5 1.3 %shard_map.96 = (f32[128,512]{1,0:T(8,128)S(1)}, f32[64,128]{1,0:T(8,128)S(1)}) custom-call(f32[512,128]{1,0:T(8,128)S(1)} %constant_dynamic-slice_fusion.resid_ref, f32[512,512]{1,0:T(8,128)S(1)} %copy-done.2, f32[512,128]{1,0:T(8,128)S(1)} %copy-done.11, s32[1,1]{1,0:T(1,128)} %bitcast.2.where_ref), custom_call_target="tpu_custom_call" | custom-call | flops 209715200 | bytes 2097152 | tf_op jit(solution)/shard_map/pallas_call | solution.py:227
  65.7 5.9 %all_gather.6 = f32[64,512]{1,0:T(8,128)} all-gather(f32[64,128]{1,0:T(8,128)S(1)} %get-tuple-element.10), channel_id=1, replica_groups=mesh['row'=4,'col'=8] {'row'}, dimensions={1}, use_global_device_ids=true | all-gather | bytes 163840 | tf_op jit(solution)/shard_map/all_gather | solution.py:236
  71.6 0.0 all-gather.2.cloned.1.call-done.lc_ref
  71.6 0.0 copy-start.5
  71.6 1.2 %copy-done.5 = f32[512,512]{1,0:T(8,128)S(1)} copy-done((f32[512,512]{1,0:T(8,128)S(1)}, f32[512,512]{1,0:T(8,128)}, u32[]{:S(2)}) %copy-start.5) | copy-done | bytes 1048600
  72.9 0.0 copy-start.7
  72.9 0.9 %copy-done.7 = f32[512,128]{1,0:T(8,128)S(1)} copy-done((f32[512,128]{1,0:T(8,128)S(1)}, f32[512,128]{1,0:T(8,128)}, u32[]{:S(2)}) %copy-start.7) | copy-done | bytes 262168
  73.8 0.0 copy-start.9
  73.8 0.9 %copy-done.9 = f32[512,128]{1,0:T(8,128)S(1)} copy-done((f32[512,128]{1,0:T(8,128)S(1)}, f32[512,128]{1,0:T(8,128)}, u32[]{:S(2)}) %copy-start.9) | copy-done | bytes 262168
  74.8 2.6 %shard_map.97 = f32[128,128]{1,0:T(8,128)} custom-call(f32[128,512]{1,0:T(8,128)S(1)} %get-tuple-element.11.yt_ref, f32[512,512]{1,0:T(8,128)S(1)} %copy-done.1, f32[512,128]{1,0:T(8,128)S(1)} %copy-done.7, f32[512,512]{1,0:T(8,128)S(1)} %copy-done.5, f32[512,128]{1,0:T(8,128)S(1)} %copy-done.9, s32[1,128]{1,0:T(1,128)S(1)} %bitcast.6, ...), custom_call_target="tpu_custom_call" | custom-call | flops 419430400 | bytes 4194304 | tf_op jit(solution)/shard_map/pallas_call | solution.py:238
  77.4 1.6 %copy.17 = f32[64,512]{1,0:T(8,128)} copy(f32[64,512]{1,0:T(8,128)} %all_gather.6) | data formatting | bytes 262144
Async XLA Ops:
  7.2 3.2 %copy-start = (f32[64,4096]{1,0:T(8,128)S(1)}, f32[64,4096]{1,0:T(8,128)}, u32[]{:S(2)}) copy-start(f32[64,4096]{1,0:T(8,128)} %param.9) | copy-start | bytes 3145732
  7.2 9.3 %copy-start.12 = (s32[128]{0:T(128)S(1)}, s32[128]{0:T(128)}, u32[]{:S(2)}) copy-start(s32[128]{0:T(128)} %param.15) | copy-start | bytes 1540
  7.2 9.3 %copy-start.2 = (f32[512,512]{1,0:T(8,128)S(1)}, f32[512,512]{1,0:T(8,128)}, u32[]{:S(2)}) copy-start(f32[512,512]{1,0:T(8,128)} %u_ref.3) | copy-start | bytes 3145732
  7.2 9.3 %copy-start.1 = (f32[512,512]{1,0:T(8,128)S(1)}, f32[512,512]{1,0:T(8,128)}, u32[]{:S(2)}) copy-start(f32[512,512]{1,0:T(8,128)} %l_ref.3) | copy-start | bytes 3145732
  7.2 64.4 %all-gather.2.cloned.1.call-start = ((), (), s32[]{:S(2)}) async-start(), calls=%async_computation | async-start | bytes 1179648 | tf_op jit(solution)/shard_map/all_gather | solution.py:195
  16.5 1.2 %copy-start.3 = (f32[512,512]{1,0:T(8,128)S(1)}, f32[512,512]{1,0:T(8,128)}, u32[]{:S(2)}) copy-start(f32[512,512]{1,0:T(8,128)} %slice.9.tail_ref) | copy-start | bytes 3145732
  17.7 1.2 %copy-start.4 = (f32[512,512]{1,0:T(8,128)S(1)}, f32[512,512]{1,0:T(8,128)}, u32[]{:S(2)}) copy-start(f32[512,512]{1,0:T(8,128)} %lp_ref.1) | copy-start | bytes 3145732
  30.7 0.7 copy-start.6
  31.4 0.7 copy-start.8
  32.1 0.7 copy-start.10
  33.5 5.8 %collective-permute-start = (f32[192,128]{1,0:T(8,128)}, f32[192,128]{1,0:T(8,128)}, u32[]{:S(2)}, u32[]{:S(2)}) collective-permute-start(f32[192,128]{1,0:T(8,128)} %get-tuple-element.16), channel_id=1, source_target_pairs={{8,0},{16,8},{24,16},{0,24},{9,1},{17,9},{25,17},{1,25},{10,2},{18... | collective-permute-start | bytes 294920 | tf_op jit(solution)/shard_map/ppermute | solution.py:170
  35.9 6.5 %collective-permute-start.1 = (f32[192,128]{1,0:T(8,128)}, f32[192,128]{1,0:T(8,128)}, u32[]{:S(2)}, u32[]{:S(2)}) collective-permute-start(f32[192,128]{1,0:T(8,128)} %get-tuple-element.17), channel_id=1, source_target_pairs={{16,0},{24,8},{0,16},{8,24},{17,1},{25,9},{1,17},{9,25},{18,2},{26... | collective-permute-start | bytes 294920 | tf_op jit(solution)/shard_map/ppermute | solution.py:170
  36.4 5.9 %collective-permute-start.2 = (f32[192,128]{1,0:T(8,128)}, f32[192,128]{1,0:T(8,128)}, u32[]{:S(2)}, u32[]{:S(2)}) collective-permute-start(f32[192,128]{1,0:T(8,128)} %get-tuple-element.18), channel_id=1, source_target_pairs={{24,0},{0,8},{8,16},{16,24},{25,1},{1,9},{9,17},{17,25},{26,2},{2,... | collective-permute-start | bytes 294920 | tf_op jit(solution)/shard_map/ppermute | solution.py:170
  43.4 0.6 copy-start.13
  44.8 3.9 %collective-permute-start.3 = (f32[64,128]{1,0:T(8,128)S(1)}, f32[64,128]{1,0:T(8,128)S(1)}, u32[]{:S(2)}, u32[]{:S(2)}) collective-permute-start(f32[64,128]{1,0:T(8,128)S(1)} %slice_subtract_fusion), channel_id=1, source_target_pairs={{1,0},{0,1},{3,2},{2,3},{5,4},{4,5},{7,6},{6,7},{9,8},{8,9},{11,10... | collective-permute-start | bytes 98312 | tf_op jit(solution)/shard_map/ppermute | solution.py:170
  49.4 5.7 %collective-permute-start.4 = (f32[128,128]{1,0:T(8,128)S(1)}, f32[128,128]{1,0:T(8,128)S(1)}, u32[]{:S(2)}, u32[]{:S(2)}) collective-permute-start(f32[128,128]{1,0:T(8,128)S(1)} %get-tuple-element.15), channel_id=1, source_target_pairs={{2,0},{3,1},{4,2},{5,3},{6,4},{7,5},{0,6},{1,7},{10,8},{11,9},{12,... | collective-permute-start | bytes 196616 | tf_op jit(solution)/shard_map/ppermute | solution.py:170
  54.0 5.2 %collective-permute-start.5 = (f32[128,128]{1,0:T(8,128)S(1)}, f32[128,128]{1,0:T(8,128)S(1)}, u32[]{:S(2)}, u32[]{:S(2)}) collective-permute-start(f32[128,128]{1,0:T(8,128)S(1)} %get-tuple-element.15), channel_id=1, source_target_pairs={{4,0},{5,1},{6,2},{7,3},{0,4},{1,5},{2,6},{3,7},{12,8},{13,9},{14,... | collective-permute-start | bytes 196616 | tf_op jit(solution)/shard_map/ppermute | solution.py:170
  54.0 6.1 %collective-permute-start.6 = (f32[128,128]{1,0:T(8,128)S(1)}, f32[128,128]{1,0:T(8,128)S(1)}, u32[]{:S(2)}, u32[]{:S(2)}) collective-permute-start(f32[128,128]{1,0:T(8,128)S(1)} %get-tuple-element.15), channel_id=1, source_target_pairs={{6,0},{7,1},{0,2},{1,3},{2,4},{3,5},{4,6},{5,7},{14,8},{15,9},{8,1... | collective-permute-start | bytes 196616 | tf_op jit(solution)/shard_map/ppermute | solution.py:170
  63.5 1.0 %copy-start.11 = (f32[512,128]{1,0:T(8,128)S(1)}, f32[512,128]{1,0:T(8,128)}, u32[]{:S(2)}) copy-start(f32[512,128]{1,0:T(8,128)} %copy-done.10) | copy-start | bytes 786436
  71.6 1.2 %copy-start.5 = (f32[512,512]{1,0:T(8,128)S(1)}, f32[512,512]{1,0:T(8,128)}, u32[]{:S(2)}) copy-start(f32[512,512]{1,0:T(8,128)} %all-gather.2.cloned.1.call-done.lc_ref) | copy-start | bytes 3145732
  72.9 0.9 %copy-start.7 = (f32[512,128]{1,0:T(8,128)S(1)}, f32[512,128]{1,0:T(8,128)}, u32[]{:S(2)}) copy-start(f32[512,128]{1,0:T(8,128)} %copy-done.6) | copy-start | bytes 786436
  73.8 0.9 %copy-start.9 = (f32[512,128]{1,0:T(8,128)S(1)}, f32[512,128]{1,0:T(8,128)}, u32[]{:S(2)}) copy-start(f32[512,128]{1,0:T(8,128)} %copy-done.8) | copy-start | bytes 786436
Sparse Core Ops, SparseCore 0:
  10.2 42.9 all-gather.1

commit v2 on v1

v2 whole, which is shorter than its diff:
```python
import functools

import jax
import jax.numpy as jnp
from jax import lax
from jax.experimental import pallas as pl
from jax.experimental.pallas import tpu as pltpu
from jax.sharding import PartitionSpec as P

F32, BF16 = jnp.float32, jnp.bfloat16
TILE = 128
VMEM = pl.BlockSpec(memory_space=pltpu.VMEM)
SMEM = pl.BlockSpec(memory_space=pltpu.SMEM)
HBM = pl.BlockSpec(memory_space=pltpu.HBM)


def halves(value):
    high = value.astype(BF16)
    return high, (value - high.astype(F32)).astype(BF16)


def mm(left, right):
    return jnp.dot(left, right, preferred_element_type=F32)


def dot3(left, right):
    lh, ll = left if isinstance(left, tuple) else halves(left)
    rh, rl = right if isinstance(right, tuple) else halves(right)
    return mm(lh, rh) + (mm(lh, rl) + mm(ll, rh))


def joined(left, right):
    lh, ll = left
    rh, rl = right
    across = jnp.concatenate([jnp.concatenate([rh, rh], axis=0), jnp.concatenate([rl, jnp.zeros_like(rl)], axis=0)], axis=1)
    both = mm(jnp.concatenate([lh, ll], axis=1), across)
    return both[:, : rh.shape[1]] + both[:, rh.shape[1] :]


def tile_of(ref, i, j):
    return ref[i * TILE : (i + 1) * TILE, j * TILE : (j + 1) * TILE]


def iotas():
    shape = (TILE, TILE)
    return lax.broadcasted_iota(jnp.int32, shape, 0), lax.broadcasted_iota(jnp.int32, shape, 1)


def unit_lower_inverses(blocks):
    rows, cols = iotas()
    eye = (rows == cols).astype(F32)
    first = ((rows >> 1) == (cols >> 1)) & (rows > cols)
    found = [eye - jnp.where(first, block, 0.0) for block in blocks]
    pieces = [halves(block) for block in blocks]
    none = jnp.zeros((TILE, TILE), BF16)
    for shift in range(1, TILE.bit_length() - 1):
        off = ((rows >> (shift + 1)) == (cols >> (shift + 1))) & ((rows >> shift) > (cols >> shift))
        parts = [halves(inv) for inv in found]
        mids = [
            halves(joined(part, tuple(jnp.where(off, half, none) for half in piece)))
            for part, piece in zip(parts, pieces)
        ]
        found = [inv - joined(mid, part) for inv, mid, part in zip(found, mids, parts)]
    return found


def product_kernel(chunk, u_cols_ref, y_ref, out_ref, y_buf, u_buf, sems):
    steps = y_buf.shape[0]
    share = out_ref.shape[0]
    copies = []
    for k in range(steps):
        span = pl.ds(k * chunk, chunk)
        copies.append(
            (
                pltpu.make_async_copy(u_cols_ref.at[:, span], u_buf.at[k], sems.at[0, k]),
                pltpu.make_async_copy(y_ref.at[span, :], y_buf.at[k], sems.at[1, k]),
            )
        )
    for pair in copies:
        for copy in pair:
            copy.start()
    total = jnp.zeros(out_ref.shape, F32)
    for k in range(steps):
        for copy in copies[k]:
            copy.wait()
        lh, ll = halves(u_buf[k])
        rh, rl = halves(y_buf[k])
        top = mm(jnp.concatenate([lh, ll], axis=0), rh)
        total = total - (top[:share] + top[share:] + mm(lh, rl))
    out_ref[...] = total


def prepare_kernel(sends, row_ref, part_ref, perm_ref, after_ref, b_hbm, u_hbm, l_hbm, lp_hbm, y_hbm, *refs):
    du_ref, dl_ref, a_ref = refs[:3]
    out_refs = refs[3:-7]
    b_ref, u_ref, l_ref, lp_ref, tail_ref, sems, pay_ref = refs[-7:]
    width = u_ref.shape[0]
    rest = y_hbm.shape[0] - width
    sources = [
        (u_hbm, u_ref),
        (l_hbm, l_ref),
        (lp_hbm, lp_ref),
        (y_hbm.at[pl.ds(rest, width), :], tail_ref),
        (b_hbm, b_ref),
    ]
    copies = [pltpu.make_async_copy(src, dst, sems.at[k]) for k, (src, dst) in enumerate(sources)]
    for copy in copies:
        copy.start()
    share = part_ref.shape[0]
    count = width // TILE
    rows, cols = iotas()
    diag = rows == cols
    blocks, scales = [], []
    copies[0].wait()
    for i in range(count):
        upper = tile_of(u_ref, i, i).T
        only = jnp.where(diag, upper, 0.0)
        blocks.append(upper * (1.0 / jnp.sum(only, axis=1, keepdims=True)))
        scales.append(1.0 / jnp.sum(only, axis=0, keepdims=True))
    copies[1].wait()
    blocks += [tile_of(l_ref, i, i) for i in range(count)]
    copies[2].wait()
    blocks += [tile_of(lp_ref, i, i) for i in range(count)]
    found = unit_lower_inverses(blocks)
    for i in range(count):
        du_ref[i * TILE : (i + 1) * TILE, :] = (found[i] * scales[i]).T
        dl_ref[i * TILE : (i + 1) * TILE, :] = found[count + i]
    perm = perm_ref[...]
    picks = perm.shape[1]
    solved, turned = [], []
    for i in range(count):
        row_ids = i * TILE + lax.broadcasted_iota(jnp.int32, (TILE, picks), 0)
        remain = (row_ids == perm).astype(F32)
        for j in range(i):
            remain = remain - joined(halves(tile_of(lp_ref, i, j)), solved[j])
        value = joined(halves(found[2 * count + i]), halves(remain))
        solved.append(halves(value))
        turned.append(value.T)
        a_ref[i * TILE : (i + 1) * TILE, :] = value
    copies[3].wait()
    copies[4].wait()
    row = row_ref[0, 0]
    size = sends + 1
    use = (row == size - 1).astype(F32)
    pay_ref[:share, :] = part_ref[...]
    pay_ref[share:, :] = dot3(jnp.concatenate(turned, axis=1), tail_ref[...]) * use
    if len(out_refs) == 1:
        out_refs[0][...] = pay_ref[...]
        return
    column_share = width // size
    for step, out_ref in enumerate(out_refs):
        target = lax.rem(row + size - step, size)
        columns = pl.ds(pl.multiple_of(target * column_share, column_share), column_share)
        out_ref[...] = pay_ref[:, columns]
        if step == 0:
            out_ref[:share, :] = out_ref[:share, :] + b_ref[:, columns]


def place_piece(col, inner, outer, share, step, piece, full_ref, columns):
    low, high = lax.rem(col, inner), lax.div(col, inner)
    high_at = lax.rem(high + step, outer)
    for turn in range(inner):
        at = high_at * inner + lax.rem(low + turn, inner)
        start = pl.multiple_of(at * share, share)
        full_ref[pl.ds(start, share), columns] = piece[turn * share : (turn + 1) * share, :]


def solve_u_kernel(inner, outer, share, col_ref, u_ref, du_ref, *refs):
    piece_refs = refs[:outer]
    yt_ref, y_ref, full_ref = refs[outer:]
    col = col_ref[0, 0]
    for step, piece_ref in enumerate(piece_refs):
        place_piece(col, inner, outer, share, step, piece_ref[...], full_ref, slice(None))
    count = u_ref.shape[0] // TILE
    solved = []
    for i in range(count):
        span = slice(i * TILE, (i + 1) * TILE)
        remain = full_ref[span, :].T
        for j in range(i):
            remain = remain - joined(solved[j], halves(tile_of(u_ref, j, i)))
        value = joined(halves(remain), halves(du_ref[span, :]))
        yt_ref[:, span] = value
        full_ref[span, :] = value.T
        solved.append(halves(value))
    y_ref[...] = full_ref[pl.ds(pl.multiple_of(col * share, share), share), :]


def finish_kernel(inner, outer, share, sides, col_ref, row_ref, yt_ref, l_ref, dl_ref, a_ref, perm_ref, v_ref, *refs):
    side_refs = refs[:sides]
    x_ref, lc_ref = refs[sides:]
    rows = inner * share
    for step, side_ref in enumerate(side_refs):
        half = side_ref.shape[1]
        at = lax.rem(row_ref[0, 0] + step, sides)
        columns = pl.ds(pl.multiple_of(at * half, half), half)
        for piece in range(outer):
            place_piece(col_ref[0, 0], inner, outer, share, piece, side_ref[piece * rows : (piece + 1) * rows, :], lc_ref, columns)
    width = l_ref.shape[0]
    count = width // TILE
    perm = perm_ref[...]
    picks = perm.shape[1]
    solved = {}
    total = None
    for i in reversed(range(count)):
        span = slice(i * TILE, (i + 1) * TILE)
        remain = yt_ref[:, span]
        for j in range(i + 1, count):
            remain = remain - joined(solved[j], halves(tile_of(l_ref, j, i)))
        solved[i] = halves(joined(halves(remain), halves(dl_ref[span, :])))
        row_ids = width + i * TILE + lax.broadcasted_iota(jnp.int32, (TILE, picks), 0)
        select = (row_ids == perm).astype(F32).astype(BF16)
        term = mm(solved[i][0], select) + mm(solved[i][1], select)
        total = term if total is None else total + term
    z = tuple(jnp.concatenate([solved[i][k] for i in range(count)], axis=1) for k in range(2))
    couple = dot3(z, lc_ref[...])
    total = total - dot3(couple, a_ref[...])
    x_ref[...] = total.T + v_ref[...]


def merge_kernel(row_ref, *refs):
    out_ref = refs[-1]
    size = len(refs) - 1
    for step, ref in enumerate(refs[:-1]):
        at = lax.rem(row_ref[0, 0] + step, size)
        columns = ref.shape[1]
        out_ref[:, pl.ds(pl.multiple_of(at * columns, columns), columns)] = ref[...]


def call(kernel, outs, flops, bytes_accessed, limit, scratch=(), **specs):
    return pl.pallas_call(
        kernel,
        out_shape=outs,
        scratch_shapes=scratch,
        cost_estimate=pl.CostEstimate(flops=flops, bytes_accessed=bytes_accessed, transcendentals=0),
        compiler_params=pltpu.CompilerParams(vmem_limit_bytes=limit << 20),
        **specs,
    )


def shape(*dims):
    return jax.ShapeDtypeStruct(dims, F32)


def in_hbm(array):
    return pltpu.with_memory_space_constraint(array, pltpu.HBM)


def inner_size(size):
    inner = 1
    while inner * inner * 4 <= size and size % (inner * 2) == 0:
        inner *= 2
    return inner


def shifted(value, axis, size, step, stride, length):
    pairs = []
    for dst in range(size):
        place = (dst // stride) % length
        pairs.append((dst + ((place + step) % length - place) * stride, dst))
    return lax.ppermute(value, axis, pairs)


def gather_pieces(value, axis, size, inner):
    near = [value] + [shifted(value, axis, size, step, 1, inner) for step in range(1, inner)]
    near = jnp.concatenate(near, axis=0)
    outer = size // inner
    return [near] + [shifted(near, axis, size, step, inner, outer) for step in range(1, outer)]


def per_device(y_prev, u_cols, b_panel, u_diag, l_diag, l_coupling, l_prev_diag, perm):
    width = u_diag.shape[0]
    share = u_cols.shape[0]
    row_size, col_size = lax.axis_size("row"), lax.axis_size("col")
    row, col = lax.axis_index("row"), lax.axis_index("col")
    columns = b_panel.shape[1]
    column_share = columns // row_size
    picks = perm.shape[0]
    aligned = column_share % TILE == 0
    row_at = row.astype(jnp.int32).reshape(1, 1)
    col_at = col.astype(jnp.int32).reshape(1, 1)
    inner = inner_size(col_size)
    outer = col_size // inner

    sides = 2 if row_size % 2 == 0 and width % (2 * TILE) == 0 else 1
    side = lax.rem(row, sides)
    half = width // sides
    coupling = gather_pieces(
        lax.dynamic_slice_in_dim(l_coupling, side * half, half, 1), "col", col_size, inner
    )

    perm_row = jnp.pad(perm, (0, max(TILE - picks, 0)), constant_values=-1)[None, :]
    lanes = perm_row.shape[1]
    steps = y_prev.shape[0] // width
    sent = share + lanes
    outs = [shape(sent, column_share)] * row_size if aligned else [shape(sent, columns)]
    part = call(
        functools.partial(product_kernel, width),
        shape(share, columns),
        1 << 30,
        9 << 20,
        24,
        scratch=[
            pltpu.VMEM((steps, width, columns), F32),
            pltpu.VMEM((steps, share, width), F32),
            pltpu.SemaphoreType.DMA((2, steps)),
        ],
        in_specs=[HBM] * 2,
        out_specs=VMEM,
    )(in_hbm(u_cols), in_hbm(y_prev))
    du, dl, a, *payload = call(
        functools.partial(prepare_kernel, row_size - 1),
        [shape(width, TILE), shape(width, TILE), shape(width, lanes)] + outs,
        1 << 30,
        5 << 20,
        12,
        scratch=[
            pltpu.VMEM(b_panel.shape, F32),
            pltpu.VMEM((width, width), F32),
            pltpu.VMEM((width, width), F32),
            pltpu.VMEM((width, width), F32),
            pltpu.VMEM((width, columns), F32),
            pltpu.SemaphoreType.DMA((5,)),
            pltpu.VMEM((sent, columns), F32),
        ],
        in_specs=[SMEM, VMEM, VMEM, pl.BlockSpec(memory_space=pl.ANY)] + [HBM] * 5,
        out_specs=[VMEM] * (3 + len(outs)),
    )(row_at, part, perm_row, coupling[0], *map(in_hbm, (b_panel, u_diag, l_diag, l_prev_diag, y_prev)))

    if aligned:
        own = payload[0]
        others = payload[1:]
    else:
        block = lambda array, place: lax.dynamic_slice_in_dim(array, place * column_share, column_share, 1)
        own = block(payload[0], row) + jnp.pad(block(b_panel, row), ((0, lanes), (0, 0)))
        others = [block(payload[0], lax.rem(row + row_size - step, row_size)) for step in range(1, row_size)]
    for step, other in enumerate(others):
        own = own + shifted(other, "row", row_size, step + 1, 1, row_size)
    rhs = max(TILE, column_share)
    widen = lambda value: jnp.pad(value, ((0, 0), (0, rhs - value.shape[1])))
    own, coupling = lax.optimization_barrier((own, coupling))
    if sides == 2:
        coupling = jnp.concatenate(coupling, axis=0)
        coupling = [coupling, shifted(coupling, "row", row_size, 1, 1, 2)]
    else:
        coupling = [jnp.concatenate(coupling, axis=0)]
    pieces = gather_pieces(widen(own[:share]), "col", col_size, inner)

    yt, y_mine = call(
        functools.partial(solve_u_kernel, inner, outer, share),
        (shape(rhs, width), shape(share, rhs)),
        200 << 20,
        2 << 20,
        8,
        scratch=[pltpu.VMEM((width, rhs), F32)],
        in_specs=[SMEM] + [VMEM] * (2 + outer),
        out_specs=[VMEM] * 2,
    )(col_at, u_diag, du, *pieces)

    if aligned:
        blocks = [y_mine] + [shifted(y_mine, "row", row_size, step, 1, row_size) for step in range(1, row_size)]
        y_part = call(merge_kernel, shape(share, columns), 0, 1 << 17, 4, in_specs=[SMEM] + [VMEM] * row_size, out_specs=VMEM)(
            row_at, *blocks
        )
    else:
        y_part = lax.all_gather(y_mine[:, :column_share], "row", axis=1, tiled=True)

    x = call(
        functools.partial(finish_kernel, inner, outer, share, sides),
        shape(lanes, rhs),
        400 << 20,
        4 << 20,
        8,
        scratch=[pltpu.VMEM((width, width), F32)],
        in_specs=[SMEM] * 2 + [VMEM] * (6 + sides),
        out_specs=VMEM,
    )(col_at, row_at, yt, l_diag, dl, a, perm_row, widen(own[share:]), *coupling)
    return (y_part, x[:picks, :column_share])


def solution(mesh):
    return jax.shard_map(
        per_device,
        mesh=mesh,
        in_specs=(
            P("row", None),
            P("col", "row"),
            P("col", None),
            P(),
            P(),
            P("col", None),
            P(),
            P("col"),
        ),
        out_specs=(P("col", None), P("col", "row")),
        check_vma=False,
    )
```

time: 86.4 us -> 57.9 us (0.67)
  local copies, waits for them, and re-layouts: 18.8 us -> 3.71 us
  between operations: 14.2 us -> 0.81 us
  starting transfers between devices: 9.71 us -> 19.2 us
  matrix products: 6.08 us -> 0 us
  blocking collectives: 5.91 us -> 0 us
  waiting for transfers between devices: 12.4 us -> 17.1 us
  other arithmetic: 3.17 us -> 0.68 us
    unnamed x34 -> x21, local copies, waits for them, and re-layouts: 13.9 us -> 2.85 us
    ppermute x7 -> x15, starting transfers between devices: 9.68 us -> 19.2 us  [shifted(): return lax.ppermute(value, axis, pairs)]
    dot_general x1 -> x0, matrix products: 6.08 us -> none  [per_device(): jnp.dot(u_cols, y_prev, precision=lax.Precision.HIGH, preferred_element_t...]
    all_gather x1 -> x0, blocking collectives: 5.91 us -> none  [per_device(): y_part = lax.all_gather(y_mine[:, :column_share], 'row', axis=1, tiled=True)]
    ppermute x7 -> x15, waiting for transfers between devices: 11.7 us -> 17.1 us  [shifted(): return lax.ppermute(value, axis, pairs)]
    slice x2, local copies, waits for them, and re-layouts: 3.25 us -> 0.85 us  [the longest x1 0.84 us: per_device(): own[share:]]
    add x1, other arithmetic: 1.02 us -> 0.03 us  [per_device(): own = own + shifted(other, 'row', row_size, step + 1, 1, row_size)]
    dynamic_slice x1, local copies, waits for them, and re-layouts: 0.97 us -> 0.01 us  [per_device(): lax.dynamic_slice_in_dim(l_coupling, side * half, half, 1)]
  transfers between devices with their start and end apart: 8 -> 15, of which waited for: 5 -> 8; matrix products, arithmetic and copies ran while one was open for 20% -> 3% of each run, Pallas kernels for 15% -> 12%
where the time goes in v2:
time: 57.9 us; the launch traced here: 57.2 us
  starting transfers between devices  19.2 us (33%)
  waiting for transfers between devices  17.1 us (30%)
  Pallas kernels  15.7 us (27%)
  local copies, waits for them, and re-layouts  3.71 us (6%)
  between operations  0.81 us (1%)
  other arithmetic  0.68 us (1%)
    ppermute x15, starting transfers between devices, shifted(): return lax.ppermute(value, axis, pairs)  19.2 us
    ppermute x15, waiting for transfers between devices, shifted(): return lax.ppermute(value, axis, pairs)  17.1 us
    pallas_call x1, Pallas kernels, per_device(): call(functools.partial(prepare_kernel, row_size - 1), [shape(width, TILE)...  6.46 us
    pallas_call x1, Pallas kernels, per_device(): call(functools.partial(product_kernel, width), shape(share, columns), 1 <...  4.18 us
    unnamed x21, local copies, waits for them, and re-layouts  2.85 us
    pallas_call x1, Pallas kernels, per_device(): call(functools.partial(finish_kernel, inner, outer, share, sides), shape(...  2.37 us
    pallas_call x1, Pallas kernels, per_device(): call(functools.partial(solve_u_kernel, inner, outer, share), (shape(rhs,...  1.99 us
  transfers between devices with their start and end apart: 15, of which 8 were waited for; matrix products, arithmetic and copies ran while one was open for 3% of the time, Pallas kernels for 12%

profile of v2, /device:TPU:0, one launch (start us, length us, event | category | flops | bytes accessed | tf_op | source)
XLA Modules:
  0.0 57.2 jit_solution(2177744938960486352)
XLA Ops:
  0.6 0.0 copy-start
  0.6 0.0 copy-start.7
  0.7 0.9 %copy-done = f32[64,512]{1,0:T(8,128)S(1)} copy-done((f32[64,512]{1,0:T(8,128)S(1)}, f32[64,512]{1,0:T(8,128)}, u32[]{:S(2)}) %copy-start) | copy-done | bytes 131096
  1.5 3.0 %collective-permute-start = (f32[64,256]{1,0:T(8,128)S(1)}, f32[64,256]{1,0:T(8,128)S(1)}, u32[]{:S(2)}, u32[]{:S(2)}) collective-permute-start(f32[64,256]{1,0:T(8,128)S(1)} %constant_dynamic-slice_fusion), channel_id=1, source_target_pairs={{1,0},{0,1},{3,2},{2,3},{5,4},{4,5},{7,6},{6,7},{9,8},{8,9},{11,10... | collective-permute-start | bytes 196616 | tf_op jit(solution)/shard_map/ppermute | solution.py:260
  4.5 4.2 %shard_map.95.part_ref = f32[64,512]{1,0:T(8,128)S(1)} custom-call(f32[64,4096]{1,0:T(8,128)} %u_cols_ref.1, f32[4096,512]{1,0:T(8,128)} %y_hbm.1), custom_call_target="tpu_custom_call" | custom-call | flops 1073741824 | bytes 9437184 | tf_op jit(solution)/shard_map/pallas_call | solution.py:296
  8.7 0.0 copy-start.1
  8.7 0.0 copy-start.2
  8.7 0.0 collective-permute-done
  8.8 0.0 copy-done.7
  8.8 6.5 %shard_map.96 = (f32[512,128]{1,0:T(8,128)S(1)}, f32[512,128]{1,0:T(8,128)S(1)}, f32[512,128]{1,0:T(8,128)S(1)}, f32[192,128]{1,0:T(8,128)S(1)}, f32[192,128]{1,...) custom-call(s32[1,1]{1,0:T(1,128)} %bitcast.row_ref, f32[64,512]{1,0:T(8,128)S(1)} %shard_map.95.part_ref, ...), custom_call_target="tpu_custom_call" | custom-call | flops 1073741824 | bytes 5242880 | tf_op jit(solution)/shard_map/pallas_call | solution.py:310
  15.2 0.0 copy-start.3
  15.2 0.0 copy-start.5
  15.3 0.7 %collective-permute-start.1 = (f32[192,128]{1,0:T(8,128)S(1)}, f32[192,128]{1,0:T(8,128)S(1)}, u32[]{:S(2)}, u32[]{:S(2)}) collective-permute-start(f32[192,128]{1,0:T(8,128)S(1)} %get-tuple-element.18), channel_id=1, source_target_pairs={{8,0},{16,8},{24,16},{0,24},{9,1},{17,9},{25,17},{1,25},{10,2},{18... | collective-permute-start | bytes 294920 | tf_op jit(solution)/shard_map/ppermute | solution.py:260
  16.0 0.9 %collective-permute-start.2 = (f32[192,128]{1,0:T(8,128)S(1)}, f32[192,128]{1,0:T(8,128)S(1)}, u32[]{:S(2)}, u32[]{:S(2)}) collective-permute-start(f32[192,128]{1,0:T(8,128)S(1)} %get-tuple-element.19), channel_id=1, source_target_pairs={{16,0},{24,8},{0,16},{8,24},{17,1},{25,9},{1,17},{9,25},{18,2},{26... | collective-permute-start | bytes 294920 | tf_op jit(solution)/shard_map/ppermute | solution.py:260
  16.9 0.2 collective-permute-start.3
  17.0 1.6 %collective-permute-start.6 = (f32[128,256]{1,0:T(8,128)S(1)}, f32[128,256]{1,0:T(8,128)S(1)}, u32[]{:S(2)}, u32[]{:S(2)}) collective-permute-start(f32[128,256]{1,0:T(8,128)S(1)} %pad_maximum_fusion.after_ref), channel_id=1, source_target_pairs={{6,0},{7,1},{0,2},{1,3},{2,4},{3,5},{4,6},{5,7},{14,8},{15,9},{8,1... | collective-permute-start | bytes 393224 | tf_op jit(solution)/shard_map/ppermute | solution.py:260
  18.6 2.6 %collective-permute-start.5 = (f32[128,256]{1,0:T(8,128)S(1)}, f32[128,256]{1,0:T(8,128)S(1)}, u32[]{:S(2)}, u32[]{:S(2)}) collective-permute-start(f32[128,256]{1,0:T(8,128)S(1)} %pad_maximum_fusion.after_ref), channel_id=1, source_target_pairs={{4,0},{5,1},{6,2},{7,3},{0,4},{1,5},{2,6},{3,7},{12,8},{13,9},{14,... | collective-permute-start | bytes 393224 | tf_op jit(solution)/shard_map/ppermute | solution.py:260
  21.2 0.0 collective-permute-done.1
  21.2 1.3 %collective-permute-start.4 = (f32[128,256]{1,0:T(8,128)S(1)}, f32[128,256]{1,0:T(8,128)S(1)}, u32[]{:S(2)}, u32[]{:S(2)}) collective-permute-start(f32[128,256]{1,0:T(8,128)S(1)} %pad_maximum_fusion.after_ref), channel_id=1, source_target_pairs={{2,0},{3,1},{4,2},{5,3},{6,4},{7,5},{0,6},{1,7},{10,8},{11,9},{12,... | collective-permute-start | bytes 393224 | tf_op jit(solution)/shard_map/ppermute | solution.py:260
  22.6 0.0 collective-permute-done.2
  22.6 0.0 collective-permute-done.3
  22.6 0.0 copy-start.8
  22.6 2.6 %collective-permute-done.6 = f32[128,256]{1,0:T(8,128)S(1)} collective-permute-done((f32[128,256]{1,0:T(8,128)S(1)}, f32[128,256]{1,0:T(8,128)S(1)}, u32[]{:S(2)}, u32[]{:S(2)}) %collective-permute-start.6) | collective-permute-done | bytes 131104 | tf_op jit(solution)/shard_map/ppermute | solution.py:260
  25.2 5.6 %collective-permute-done.5 = f32[128,256]{1,0:T(8,128)S(1)} collective-permute-done((f32[128,256]{1,0:T(8,128)S(1)}, f32[128,256]{1,0:T(8,128)S(1)}, u32[]{:S(2)}, u32[]{:S(2)}) %collective-permute-start.5) | collective-permute-done | bytes 131104 | tf_op jit(solution)/shard_map/ppermute | solution.py:260
  30.8 0.0 collective-permute-done.4
  30.9 0.0 copy-done.3
  30.9 0.2 collective-permute-start.14
  31.1 0.0 copy-done.5
  31.1 0.0 copy-done.8
  31.1 0.6 %collective-permute-start.7 = (f32[64,128]{1,0:T(8,128)S(1)}, f32[64,128]{1,0:T(8,128)S(1)}, u32[]{:S(2)}, u32[]{:S(2)}) collective-permute-start(f32[64,128]{1,0:T(8,128)S(1)} %slice.6), channel_id=1, source_target_pairs={{1,0},{0,1},{3,2},{2,3},{5,4},{4,5},{7,6},{6,7},{9,8},{8,9},{11,10... | collective-permute-start | bytes 98312 | tf_op jit(solution)/shard_map/ppermute | solution.py:260
  31.7 3.4 %collective-permute-done.7 = f32[64,128]{1,0:T(8,128)S(1)} collective-permute-done((f32[64,128]{1,0:T(8,128)S(1)}, f32[64,128]{1,0:T(8,128)S(1)}, u32[]{:S(2)}, u32[]{:S(2)}) %collective-permute-start.7) | collective-permute-done | bytes 32800 | tf_op jit(solution)/shard_map/ppermute | solution.py:260
  35.1 0.6 %pad_maximum_fusion.1.refs_0_ = f32[128,128]{1,0:T(8,128)} fusion(f32[64,128]{1,0:T(8,128)S(1)} %collective-permute-done.7, f32[64,128]{1,0:T(8,128)S(1)} %slice.6), kind=kLoop, calls=%fused_computation.2 | loop fusion | flops 16384 | bytes 131072 | tf_op jit(solution)/shard_map/concatenate | solution.py:265
  35.7 3.4 %collective-permute-start.10 = (f32[128,128]{1,0:T(8,128)}, f32[128,128]{1,0:T(8,128)}, u32[]{:S(2)}, u32[]{:S(2)}) collective-permute-start(f32[128,128]{1,0:T(8,128)} %pad_maximum_fusion.1.refs_0_), channel_id=1, source_target_pairs={{6,0},{7,1},{0,2},{1,3},{2,4},{3,5},{4,6},{5,7},{14,8},{15,9},{8,1... | collective-permute-start | bytes 196616 | tf_op jit(solution)/shard_map/ppermute | solution.py:260
  39.1 1.7 %collective-permute-start.9 = (f32[128,128]{1,0:T(8,128)}, f32[128,128]{1,0:T(8,128)}, u32[]{:S(2)}, u32[]{:S(2)}) collective-permute-start(f32[128,128]{1,0:T(8,128)} %pad_maximum_fusion.1.refs_0_), channel_id=1, source_target_pairs={{4,0},{5,1},{6,2},{7,3},{0,4},{1,5},{2,6},{3,7},{12,8},{13,9},{14,... | collective-permute-start | bytes 196616 | tf_op jit(solution)/shard_map/ppermute | solution.py:260
  40.7 0.7 %collective-permute-start.8 = (f32[128,128]{1,0:T(8,128)}, f32[128,128]{1,0:T(8,128)}, u32[]{:S(2)}, u32[]{:S(2)}) collective-permute-start(f32[128,128]{1,0:T(8,128)} %pad_maximum_fusion.1.refs_0_), channel_id=1, source_target_pairs={{2,0},{3,1},{4,2},{5,3},{6,4},{7,5},{0,6},{1,7},{10,8},{11,9},{12,... | collective-permute-start | bytes 196616 | tf_op jit(solution)/shard_map/ppermute | solution.py:260
  41.4 1.7 %collective-permute-done.10.refs_3_ = f32[128,128]{1,0:T(8,128)} collective-permute-done((f32[128,128]{1,0:T(8,128)}, f32[128,128]{1,0:T(8,128)}, u32[]{:S(2)}, u32[]{:S(2)}) %collective-permute-start.10) | collective-permute-done | bytes 65568 | tf_op jit(solution)/shard_map/ppermute | solution.py:260
  43.1 2.6 %collective-permute-done.9.refs_2_ = f32[128,128]{1,0:T(8,128)} collective-permute-done((f32[128,128]{1,0:T(8,128)}, f32[128,128]{1,0:T(8,128)}, u32[]{:S(2)}, u32[]{:S(2)}) %collective-permute-start.9) | collective-permute-done | bytes 65568 | tf_op jit(solution)/shard_map/ppermute | solution.py:260
  45.8 0.1 collective-permute-done.8.refs_1_
  45.9 0.0 copy-done.1
  45.9 0.0 copy-start.6
  45.9 0.9 %copy-done.6 = f32[512,128]{1,0:T(8,128)S(1)} copy-done((f32[512,128]{1,0:T(8,128)S(1)}, f32[512,128]{1,0:T(8,128)}, u32[]{:S(2)}) %copy-start.6) | copy-done | bytes 262168
  46.8 2.0 %shard_map.97 = (f32[128,512]{1,0:T(8,128)S(1)}, f32[64,128]{1,0:T(8,128)S(1)}) custom-call(s32[1,1]{1,0:T(1,128)} %bitcast.1.col_ref, f32[512,512]{1,0:T(8,128)S(1)} %copy-done.1, f32[512,128]{1,0:T(8,128)S(1)} %copy-done.6, f32[128,128]{1,0:T(8,128)} %pad_maximum_fusion.1.refs_0_, f32[128,128]{1,0:T(8,128)} %collective-permute-done.8.refs_1_, ...), custom_call_target="tpu_custom_call" | custom-call | flops 209715200 | bytes 2097152 | tf_op jit(solution)/shard_map/pallas_call | solution.py:348
  48.8 0.1 collective-permute-start.13
  48.9 1.0 %collective-permute-start.12 = (f32[64,128]{1,0:T(8,128)S(1)}, f32[64,128]{1,0:T(8,128)S(1)}, u32[]{:S(2)}, u32[]{:S(2)}) collective-permute-start(f32[64,128]{1,0:T(8,128)S(1)} %get-tuple-element.22.refs_0_), channel_id=1, source_target_pairs={{16,0},{24,8},{0,16},{8,24},{17,1},{25,9},{1,17},{9,25},{18,2},{26... | collective-permute-start | bytes 98312 | tf_op jit(solution)/shard_map/ppermute | solution.py:260
  49.9 1.4 %collective-permute-start.11 = (f32[64,128]{1,0:T(8,128)S(1)}, f32[64,128]{1,0:T(8,128)S(1)}, u32[]{:S(2)}, u32[]{:S(2)}) collective-permute-start(f32[64,128]{1,0:T(8,128)S(1)} %get-tuple-element.22.refs_0_), channel_id=1, source_target_pairs={{8,0},{16,8},{24,16},{0,24},{9,1},{17,9},{25,17},{1,25},{10,2},{18... | collective-permute-start | bytes 98312 | tf_op jit(solution)/shard_map/ppermute | solution.py:260
  51.3 0.8 %slice.7.v_ref = f32[128,128]{1,0:T(8,128)S(1)} slice(f32[192,128]{1,0:T(8,128)} %copy-done.8), slice={[64:192], [0:128]} | slice | bytes 131072 | tf_op jit(solution)/shard_map/slice | solution.py:376
  52.2 0.1 collective-permute-done.13.refs_3_
  52.2 1.0 %collective-permute-done.12.refs_2_ = f32[64,128]{1,0:T(8,128)S(1)} collective-permute-done((f32[64,128]{1,0:T(8,128)S(1)}, f32[64,128]{1,0:T(8,128)S(1)}, u32[]{:S(2)}, u32[]{:S(2)}) %collective-permute-start.12) | collective-permute-done | bytes 32800 | tf_op jit(solution)/shard_map/ppermute | solution.py:260
  53.2 0.0 collective-permute-done.11.refs_1_
  53.2 0.7 %shard_map.98 = f32[64,512]{1,0:T(8,128)} custom-call(s32[1,1]{1,0:T(1,128)} %bitcast.row_ref, f32[64,128]{1,0:T(8,128)S(1)} %get-tuple-element.22.refs_0_, f32[64,128]{1,0:T(8,128)S(1)} %collective-permute-done.11.refs_1_, f32[64,128]{1,0:T(8,128)S(1)} %collective-permute-done.12.refs_2_, f32[64,128]{1,0:T(8,128)S(1)} %collective-permute-done.13.refs_3_), custom_call_target="tpu_custom_call" | custom-call | bytes 131072 | tf_op jit(solution)/shard_map/pallas_call | solution.py:361
  53.9 0.0 collective-permute-done.14.refs_1_
  53.9 0.0 copy-done.2
  53.9 0.0 copy-start.4
  53.9 0.9 %copy-done.4 = f32[512,128]{1,0:T(8,128)S(1)} copy-done((f32[512,128]{1,0:T(8,128)S(1)}, f32[512,128]{1,0:T(8,128)}, u32[]{:S(2)}) %copy-start.4) | copy-done | bytes 262168
  54.8 2.4 %shard_map.99 = f32[128,128]{1,0:T(8,128)} custom-call(s32[1,1]{1,0:T(1,128)} %bitcast.1.col_ref, s32[1,1]{1,0:T(1,128)} %bitcast.row_ref, f32[128,512]{1,0:T(8,128)S(1)} %get-tuple-element.23.yt_ref, f32[512,512]{1,0:T(8,128)S(1)} %copy-done.2, f32[512,128]{1,0:T(8,128)S(1)} %get-tuple-element.24.dl_ref, f32[512,128]{1,0:T(8,128)S(1)} %copy-done.4, ...), custom_call_target="tpu_custom_call" | custom-call | flops 419430400 | bytes 4194304 | tf_op jit(solution)/shard_map/pallas_call | solution.py:367
  (8 shorter events, 0.1 us)
Async XLA Ops:
  0.6 0.9 %copy-start = (f32[64,512]{1,0:T(8,128)S(1)}, f32[64,512]{1,0:T(8,128)}, u32[]{:S(2)}) copy-start(f32[64,512]{1,0:T(8,128)} %param.13) | copy-start | bytes 393220
  0.6 8.1 %copy-start.7 = (s32[128]{0:T(128)S(1)}, s32[128]{0:T(128)}, u32[]{:S(2)}) copy-start(s32[128]{0:T(128)} %param.15) | copy-start | bytes 1540
  1.5 7.2 %collective-permute-start = (f32[64,256]{1,0:T(8,128)S(1)}, f32[64,256]{1,0:T(8,128)S(1)}, u32[]{:S(2)}, u32[]{:S(2)}) collective-permute-start(f32[64,256]{1,0:T(8,128)S(1)} %constant_dynamic-slice_fusion), channel_id=1, source_target_pairs={{1,0},{0,1},{3,2},{2,3},{5,4},{4,5},{7,6},{6,7},{9,8},{8,9},{11,10... | collective-permute-start | bytes 196616 | tf_op jit(solution)/shard_map/ppermute | solution.py:260
  8.7 37.2 %copy-start.1 = (f32[512,512]{1,0:T(8,128)S(1)}, f32[512,512]{1,0:T(8,128)}, u32[]{:S(2)}) copy-start(f32[512,512]{1,0:T(8,128)} %u_ref.1) | copy-start | bytes 3145732
  8.7 45.2 %copy-start.2 = (f32[512,512]{1,0:T(8,128)S(1)}, f32[512,512]{1,0:T(8,128)}, u32[]{:S(2)}) copy-start(f32[512,512]{1,0:T(8,128)} %l_ref.1) | copy-start | bytes 3145732
  15.2 15.7 %copy-start.3 = (f32[512,128]{1,0:T(8,128)}, f32[512,128]{1,0:T(8,128)S(1)}, u32[]{:S(2)}) copy-start(f32[512,128]{1,0:T(8,128)S(1)} %get-tuple-element.25.a_ref) | copy-start | bytes 786436
  15.2 15.8 %copy-start.5 = (f32[512,128]{1,0:T(8,128)}, f32[512,128]{1,0:T(8,128)S(1)}, u32[]{:S(2)}) copy-start(f32[512,128]{1,0:T(8,128)S(1)} %get-tuple-element.16.du_ref) | copy-start | bytes 786436
  15.3 6.0 %collective-permute-start.1 = (f32[192,128]{1,0:T(8,128)S(1)}, f32[192,128]{1,0:T(8,128)S(1)}, u32[]{:S(2)}, u32[]{:S(2)}) collective-permute-start(f32[192,128]{1,0:T(8,128)S(1)} %get-tuple-element.18), channel_id=1, source_target_pairs={{8,0},{16,8},{24,16},{0,24},{9,1},{17,9},{25,17},{1,25},{10,2},{18... | collective-permute-start | bytes 294920 | tf_op jit(solution)/shard_map/ppermute | solution.py:260
  16.0 6.6 %collective-permute-start.2 = (f32[192,128]{1,0:T(8,128)S(1)}, f32[192,128]{1,0:T(8,128)S(1)}, u32[]{:S(2)}, u32[]{:S(2)}) collective-permute-start(f32[192,128]{1,0:T(8,128)S(1)} %get-tuple-element.19), channel_id=1, source_target_pairs={{16,0},{24,8},{0,16},{8,24},{17,1},{25,9},{1,17},{9,25},{18,2},{26... | collective-permute-start | bytes 294920 | tf_op jit(solution)/shard_map/ppermute | solution.py:260
  16.9 5.7 %collective-permute-start.3 = (f32[192,128]{1,0:T(8,128)S(1)}, f32[192,128]{1,0:T(8,128)S(1)}, u32[]{:S(2)}, u32[]{:S(2)}) collective-permute-start(f32[192,128]{1,0:T(8,128)S(1)} %get-tuple-element.20), channel_id=1, source_target_pairs={{24,0},{0,8},{8,16},{16,24},{25,1},{1,9},{9,17},{17,25},{26,2},{2,... | collective-permute-start | bytes 294920 | tf_op jit(solution)/shard_map/ppermute | solution.py:260
  17.0 8.2 %collective-permute-start.6 = (f32[128,256]{1,0:T(8,128)S(1)}, f32[128,256]{1,0:T(8,128)S(1)}, u32[]{:S(2)}, u32[]{:S(2)}) collective-permute-start(f32[128,256]{1,0:T(8,128)S(1)} %pad_maximum_fusion.after_ref), channel_id=1, source_target_pairs={{6,0},{7,1},{0,2},{1,3},{2,4},{3,5},{4,6},{5,7},{14,8},{15,9},{8,1... | collective-permute-start | bytes 393224 | tf_op jit(solution)/shard_map/ppermute | solution.py:260
  18.6 12.2 %collective-permute-start.5 = (f32[128,256]{1,0:T(8,128)S(1)}, f32[128,256]{1,0:T(8,128)S(1)}, u32[]{:S(2)}, u32[]{:S(2)}) collective-permute-start(f32[128,256]{1,0:T(8,128)S(1)} %pad_maximum_fusion.after_ref), channel_id=1, source_target_pairs={{4,0},{5,1},{6,2},{7,3},{0,4},{1,5},{2,6},{3,7},{12,8},{13,9},{14,... | collective-permute-start | bytes 393224 | tf_op jit(solution)/shard_map/ppermute | solution.py:260
  21.2 9.6 %collective-permute-start.4 = (f32[128,256]{1,0:T(8,128)S(1)}, f32[128,256]{1,0:T(8,128)S(1)}, u32[]{:S(2)}, u32[]{:S(2)}) collective-permute-start(f32[128,256]{1,0:T(8,128)S(1)} %pad_maximum_fusion.after_ref), channel_id=1, source_target_pairs={{2,0},{3,1},{4,2},{5,3},{6,4},{7,5},{0,6},{1,7},{10,8},{11,9},{12,... | collective-permute-start | bytes 393224 | tf_op jit(solution)/shard_map/ppermute | solution.py:260
  22.6 8.5 %copy-start.8 = (f32[192,128]{1,0:T(8,128)}, f32[192,128]{1,0:T(8,128)S(1)}, u32[]{:S(2)}) copy-start(f32[192,128]{1,0:T(8,128)S(1)} %add_add_fusion) | copy-start | bytes 294916
  30.9 22.9 %collective-permute-start.14 = (f32[512,256]{1,0:T(8,128)S(1)}, f32[512,256]{1,0:T(8,128)S(1)}, u32[]{:S(2)}, u32[]{:S(2)}) collective-permute-start(f32[512,256]{1,0:T(8,128)S(1)} %constant_dynamic-update-slice_fusion.refs_0_), channel_id=1, source_target_pairs={{8,0},{0,8},{24,16},{16,24},{9,1},{1,9},{25,17},{17,25},{10,2},{2,... | collective-permute-start | bytes 1572872 | tf_op jit(solution)/shard_map/ppermute | solution.py:260
  31.1 4.0 %collective-permute-start.7 = (f32[64,128]{1,0:T(8,128)S(1)}, f32[64,128]{1,0:T(8,128)S(1)}, u32[]{:S(2)}, u32[]{:S(2)}) collective-permute-start(f32[64,128]{1,0:T(8,128)S(1)} %slice.6), channel_id=1, source_target_pairs={{1,0},{0,1},{3,2},{2,3},{5,4},{4,5},{7,6},{6,7},{9,8},{8,9},{11,10... | collective-permute-start | bytes 98312 | tf_op jit(solution)/shard_map/ppermute | solution.py:260
  35.7 7.4 %collective-permute-start.10 = (f32[128,128]{1,0:T(8,128)}, f32[128,128]{1,0:T(8,128)}, u32[]{:S(2)}, u32[]{:S(2)}) collective-permute-start(f32[128,128]{1,0:T(8,128)} %pad_maximum_fusion.1.refs_0_), channel_id=1, source_target_pairs={{6,0},{7,1},{0,2},{1,3},{2,4},{3,5},{4,6},{5,7},{14,8},{15,9},{8,1... | collective-permute-start | bytes 196616 | tf_op jit(solution)/shard_map/ppermute | solution.py:260
  39.1 6.7 %collective-permute-start.9 = (f32[128,128]{1,0:T(8,128)}, f32[128,128]{1,0:T(8,128)}, u32[]{:S(2)}, u32[]{:S(2)}) collective-permute-start(f32[128,128]{1,0:T(8,128)} %pad_maximum_fusion.1.refs_0_), channel_id=1, source_target_pairs={{4,0},{5,1},{6,2},{7,3},{0,4},{1,5},{2,6},{3,7},{12,8},{13,9},{14,... | collective-permute-start | bytes 196616 | tf_op jit(solution)/shard_map/ppermute | solution.py:260
  40.7 5.2 %collective-permute-start.8 = (f32[128,128]{1,0:T(8,128)}, f32[128,128]{1,0:T(8,128)}, u32[]{:S(2)}, u32[]{:S(2)}) collective-permute-start(f32[128,128]{1,0:T(8,128)} %pad_maximum_fusion.1.refs_0_), channel_id=1, source_target_pairs={{2,0},{3,1},{4,2},{5,3},{6,4},{7,5},{0,6},{1,7},{10,8},{11,9},{12,... | collective-permute-start | bytes 196616 | tf_op jit(solution)/shard_map/ppermute | solution.py:260
  45.9 1.0 %copy-start.6 = (f32[512,128]{1,0:T(8,128)S(1)}, f32[512,128]{1,0:T(8,128)}, u32[]{:S(2)}) copy-start(f32[512,128]{1,0:T(8,128)} %copy-done.5) | copy-start | bytes 786436
  48.8 3.4 %collective-permute-start.13 = (f32[64,128]{1,0:T(8,128)S(1)}, f32[64,128]{1,0:T(8,128)S(1)}, u32[]{:S(2)}, u32[]{:S(2)}) collective-permute-start(f32[64,128]{1,0:T(8,128)S(1)} %get-tuple-element.22.refs_0_), channel_id=1, source_target_pairs={{24,0},{0,8},{8,16},{16,24},{25,1},{1,9},{9,17},{17,25},{26,2},{2,... | collective-permute-start | bytes 98312 | tf_op jit(solution)/shard_map/ppermute | solution.py:260
  48.9 4.3 %collective-permute-start.12 = (f32[64,128]{1,0:T(8,128)S(1)}, f32[64,128]{1,0:T(8,128)S(1)}, u32[]{:S(2)}, u32[]{:S(2)}) collective-permute-start(f32[64,128]{1,0:T(8,128)S(1)} %get-tuple-element.22.refs_0_), channel_id=1, source_target_pairs={{16,0},{24,8},{0,16},{8,24},{17,1},{25,9},{1,17},{9,25},{18,2},{26... | collective-permute-start | bytes 98312 | tf_op jit(solution)/shard_map/ppermute | solution.py:260
  49.9 3.3 %collective-permute-start.11 = (f32[64,128]{1,0:T(8,128)S(1)}, f32[64,128]{1,0:T(8,128)S(1)}, u32[]{:S(2)}, u32[]{:S(2)}) collective-permute-start(f32[64,128]{1,0:T(8,128)S(1)} %get-tuple-element.22.refs_0_), channel_id=1, source_target_pairs={{8,0},{16,8},{24,16},{0,24},{9,1},{17,9},{25,17},{1,25},{10,2},{18... | collective-permute-start | bytes 98312 | tf_op jit(solution)/shard_map/ppermute | solution.py:260
  53.9 1.0 %copy-start.4 = (f32[512,128]{1,0:T(8,128)S(1)}, f32[512,128]{1,0:T(8,128)}, u32[]{:S(2)}) copy-start(f32[512,128]{1,0:T(8,128)} %copy-done.3) | copy-start | bytes 786436

commit v3 on v1

v3 whole, which is shorter than its diff:
```python
import functools

import jax
import jax.numpy as jnp
from jax import lax
from jax.experimental import pallas as pl
from jax.experimental.pallas import tpu as pltpu
from jax.sharding import PartitionSpec as P

F32, BF16 = jnp.float32, jnp.bfloat16
TILE = 128
VMEM = pl.BlockSpec(memory_space=pltpu.VMEM)
SMEM = pl.BlockSpec(memory_space=pltpu.SMEM)
HBM = pl.BlockSpec(memory_space=pltpu.HBM)
ANY = pl.BlockSpec(memory_space=pl.ANY)


def halves(value):
    high = value.astype(BF16)
    return high, (value - high.astype(F32)).astype(BF16)


def mm(left, right):
    return jnp.dot(left, right, preferred_element_type=F32)


def mm_t(left, right):
    return lax.dot_general(left, right, (((1,), (1,)), ((), ())), preferred_element_type=F32)


def dot3(left, right):
    lh, ll = left if isinstance(left, tuple) else halves(left)
    rh, rl = right if isinstance(right, tuple) else halves(right)
    return mm(lh, rh) + (mm(lh, rl) + mm(ll, rh))


def joined(left, right):
    lh, ll = left
    rh, rl = right
    across = jnp.concatenate([jnp.concatenate([rh, rh], axis=0), jnp.concatenate([rl, jnp.zeros_like(rl)], axis=0)], axis=1)
    both = mm(jnp.concatenate([lh, ll], axis=1), across)
    return both[:, : rh.shape[1]] + both[:, rh.shape[1] :]


def tile_of(ref, i, j):
    return ref[i * TILE : (i + 1) * TILE, j * TILE : (j + 1) * TILE]


def iotas():
    shape = (TILE, TILE)
    return lax.broadcasted_iota(jnp.int32, shape, 0), lax.broadcasted_iota(jnp.int32, shape, 1)


def unit_lower_inverses(blocks):
    rows, cols = iotas()
    eye = (rows == cols).astype(F32)
    first = ((rows >> 1) == (cols >> 1)) & (rows > cols)
    found = [eye - jnp.where(first, block, 0.0) for block in blocks]
    pieces = [halves(block) for block in blocks]
    none = jnp.zeros((TILE, TILE), BF16)
    for shift in range(1, TILE.bit_length() - 1):
        off = ((rows >> (shift + 1)) == (cols >> (shift + 1))) & ((rows >> shift) > (cols >> shift))
        parts = [halves(inv) for inv in found]
        mids = [
            halves(joined(part, tuple(jnp.where(off, half, none) for half in piece)))
            for part, piece in zip(parts, pieces)
        ]
        found = [inv - joined(mid, part) for inv, mid, part in zip(found, mids, parts)]
    return found


def started(copies):
    for copy in copies:
        copy.start()
    return copies


def invert_kernel(
    perm_hbm, u_hbm, l_hbm, lp_hbm, du_hbm, dl_hbm, at_ref, perm_ref, u_ref, l_ref, lp_ref, du_ref, dl_ref, sems
):
    width = lp_ref.shape[0]
    count = width // TILE
    spans = [slice(i * TILE, (i + 1) * TILE) for i in range(count)]
    tiles = [pl.ds(i * TILE, TILE) for i in range(count)]
    copies = started(
        [
            pltpu.make_async_copy(src.at[tiles[i], tiles[i]], dst.at[tiles[i], :], sems.at[k, i])
            for k, (src, dst) in enumerate([(u_hbm, u_ref), (l_hbm, l_ref)])
            for i in range(count)
        ]
        + [pltpu.make_async_copy(lp_hbm, lp_ref, sems.at[2, 0]), pltpu.make_async_copy(perm_hbm, perm_ref, sems.at[3, 0])]
    )
    for copy in copies:
        copy.wait()
    rows, cols = iotas()
    diag = rows == cols
    blocks, scales = [], []
    for span in spans:
        upper = u_ref[span, :].T
        only = jnp.where(diag, upper, 0.0)
        blocks.append(upper * (1.0 / jnp.sum(only, axis=1, keepdims=True)))
        scales.append(1.0 / jnp.sum(only, axis=0, keepdims=True))
    blocks += [l_ref[span, :] for span in spans]
    blocks += [tile_of(lp_ref, i, i) for i in range(count)]
    found = unit_lower_inverses(blocks)
    for i, span in enumerate(spans):
        du_ref[span, :] = (found[i] * scales[i]).T
        dl_ref[span, :] = found[count + i]
    out = started(
        [pltpu.make_async_copy(du_ref, du_hbm, sems.at[4, 0]), pltpu.make_async_copy(dl_ref, dl_hbm, sems.at[5, 0])]
    )
    perm = perm_ref[...]
    picks = perm.shape[1]
    solved = []
    for i, span in enumerate(spans):
        row_ids = i * TILE + lax.broadcasted_iota(jnp.int32, (TILE, picks), 0)
        remain = (row_ids == perm).astype(F32)
        for j in range(i):
            remain = remain - joined(halves(tile_of(lp_ref, i, j)), solved[j])
        value = joined(halves(found[2 * count + i]), halves(remain))
        solved.append(halves(value))
        at_ref[:, span] = value.T
    for copy in out:
        copy.wait()


def product_kernel(size, paired, row_ref, at_ref, after_ref, b_ref, u_cols_ref, y_ref, *refs):
    del after_ref
    out_refs, pay_ref = refs[:-1], refs[-1]
    share = b_ref.shape[0]
    chunk = at_ref.shape[1]
    steps = y_ref.shape[0] // chunk
    total = jnp.zeros(b_ref.shape, F32)
    for k in range(steps):
        lh, ll = halves(u_cols_ref[:, k * chunk : (k + 1) * chunk])
        rh, rl = halves(y_ref[k * chunk : (k + 1) * chunk, :])
        if k == steps - 1:
            ah, al = halves(at_ref[...])
            seen = mm(ah, rh) + (mm(ah, rl) + mm(al, rh))
        top = mm(jnp.concatenate([lh, ll], axis=0), rh)
        total = total - (top[:share] + top[share:] + mm(lh, rl))
    row = row_ref[0, 0]
    pay_ref[:share, :] = total
    pay_ref[share:, :] = seen * (row == size - 1).astype(F32)
    if not paired:
        out_refs[0][...] = pay_ref[...]
        return
    columns = b_ref.shape[1] // size
    chips = size // 2
    chip, core = lax.div(row, 2), lax.rem(row, 2)
    for out_ref, side in zip(out_refs, (core, 1 - core)):
        for step in range(chips):
            place = 2 * (chip ^ step) + side
            out_ref[:, step * columns : (step + 1) * columns] = pay_ref[:, aligned_span(place, columns)]
    keep_ref = out_refs[0]
    keep_ref[:share, :columns] = keep_ref[:share, :columns] + b_ref[:, aligned_span(row, columns)]


def aligned_span(place, size):
    return pl.ds(pl.multiple_of(place * size, size), size)


def place_piece(col, inner, outer, share, step, piece, full_ref, columns):
    low, high = lax.rem(col, inner), lax.div(col, inner)
    for turn in range(outer):
        at = (high ^ turn) * inner + (low ^ step)
        full_ref[aligned_span(at, share), columns] = piece[turn * share : (turn + 1) * share, :]


def solve_u_kernel(inner, outer, share, col_ref, u_ref, du_any, *refs):
    piece_refs = refs[:inner]
    yt_ref, y_ref, full_ref, du_ref, sem = refs[inner:]
    copy = pltpu.make_async_copy(du_any, du_ref, sem)
    copy.start()
    col = col_ref[0, 0]
    for step, piece_ref in enumerate(piece_refs):
        place_piece(col, inner, outer, share, step, piece_ref[...], full_ref, slice(None))
    copy.wait()
    count = u_ref.shape[0] // TILE
    solved = []
    for i in range(count):
        span = slice(i * TILE, (i + 1) * TILE)
        remain = full_ref[span, :].T
        for j in range(i):
            remain = remain - joined(solved[j], halves(tile_of(u_ref, j, i)))
        value = joined(halves(remain), halves(du_ref[span, :]))
        yt_ref[:, span] = value
        full_ref[span, :] = value.T
        solved.append(halves(value))
    y_ref[...] = full_ref[aligned_span(col, share), :]


def finish_kernel(inner, outer, share, parts, col_ref, row_ref, yt_ref, l_ref, dl_any, at_any, perm_ref, v_any, *refs):
    side_refs = refs[: 1 if parts == 1 else 2]
    x_ref, lc_ref, dl_ref, at_ref, v_ref, sems = refs[len(side_refs) :]
    copies = started(
        [
            pltpu.make_async_copy(src, dst, sems.at[k])
            for k, (src, dst) in enumerate([(dl_any, dl_ref), (at_any, at_ref), (v_any, v_ref)])
        ]
    )
    row, col = row_ref[0, 0], col_ref[0, 0]
    rows = outer * share
    columns = lc_ref.shape[1] // parts
    chips = max(parts // 2, 1)
    for turn, side_ref in enumerate(side_refs):
        for step in range(chips):
            if parts == 1:
                target = slice(None)
            else:
                target = aligned_span(row ^ (2 * step) ^ turn, columns)
            for piece in range(inner):
                value = side_ref[piece * rows : (piece + 1) * rows, step * columns : (step + 1) * columns]
                place_piece(col, inner, outer, share, piece, value, lc_ref, target)
    for copy in copies:
        copy.wait()
    width = l_ref.shape[0]
    count = width // TILE
    perm = perm_ref[...]
    picks = perm.shape[1]
    solved = {}
    total = None
    for i in reversed(range(count)):
        span = slice(i * TILE, (i + 1) * TILE)
        remain = yt_ref[:, span]
        for j in range(i + 1, count):
            remain = remain - joined(solved[j], halves(tile_of(l_ref, j, i)))
        solved[i] = halves(joined(halves(remain), halves(dl_ref[span, :])))
        row_ids = width + i * TILE + lax.broadcasted_iota(jnp.int32, (TILE, picks), 0)
        select = (row_ids == perm).astype(F32).astype(BF16)
        term = mm(solved[i][0], select) + mm(solved[i][1], select)
        total = term if total is None else total + term
    z = tuple(jnp.concatenate([solved[i][k] for i in range(count)], axis=1) for k in range(2))
    couple = dot3(z, lc_ref[...])
    ch, cl = halves(couple)
    ah, al = halves(at_ref[...])
    total = total - (mm_t(ch, ah) + (mm_t(ch, al) + mm_t(cl, ah)))
    x_ref[...] = total.T + v_ref[...]


def merge_kernel(row_ref, after_ref, *refs):
    del after_ref
    out_ref = refs[-1]
    for step, ref in enumerate(refs[:-1]):
        out_ref[:, aligned_span(row_ref[0, 0] ^ step, ref.shape[1])] = ref[...]


def call(kernel, outs, flops, bytes_accessed, limit, scratch=(), **specs):
    return pl.pallas_call(
        kernel,
        out_shape=outs,
        scratch_shapes=scratch,
        cost_estimate=pl.CostEstimate(flops=flops, bytes_accessed=bytes_accessed, transcendentals=0),
        compiler_params=pltpu.CompilerParams(vmem_limit_bytes=limit << 20),
        **specs,
    )


def shape(*dims):
    return jax.ShapeDtypeStruct(dims, F32)


def in_hbm(array):
    return pltpu.with_memory_space_constraint(array, pltpu.HBM)


def inner_size(size):
    inner = 1
    while inner * inner * 4 <= size and size % (inner * 2) == 0:
        inner *= 2
    return inner


def swapped(value, axis, size, mask):
    return lax.ppermute(value, axis, [(dst ^ mask, dst) for dst in range(size)])


def gather_line(value, axis, size, inner):
    return jnp.concatenate([value] + [swapped(value, axis, size, mask) for mask in range(inner, size, inner)], axis=0)


def gather_pieces(line, axis, size, inner):
    return [line] + [swapped(line, axis, size, mask) for mask in range(1, inner)]


def per_device(y_prev, u_cols, b_panel, u_diag, l_diag, l_coupling, l_prev_diag, perm):
    width = u_diag.shape[0]
    share = u_cols.shape[0]
    row_size, col_size = lax.axis_size("row"), lax.axis_size("col")
    assert row_size & (row_size - 1) == 0 and col_size & (col_size - 1) == 0
    row, col = lax.axis_index("row"), lax.axis_index("col")
    columns = b_panel.shape[1]
    column_share = columns // row_size
    picks = perm.shape[0]
    paired = row_size % 2 == 0 and column_share % TILE == 0
    chips = row_size // 2
    row_at = row.astype(jnp.int32).reshape(1, 1)
    col_at = col.astype(jnp.int32).reshape(1, 1)
    inner = inner_size(col_size)
    outer = col_size // inner

    parts = row_size if paired and width % (row_size * TILE) == 0 else 1
    quarter = width // parts
    line = lax.dynamic_slice_in_dim(l_coupling, lax.rem(row, parts) * quarter, quarter, 1)
    lines = []
    mask = inner
    while mask < col_size:
        line = jnp.concatenate([line, swapped(line, "col", col_size, mask)], axis=0)
        lines.append(line)
        mask *= 2

    perm_row = jnp.pad(perm, (0, max(TILE - picks, 0)), constant_values=-1)[None, :]
    lanes = perm_row.shape[1]
    sent = share + lanes
    du, dl, at = call(
        invert_kernel,
        [shape(width, TILE), shape(width, TILE), shape(lanes, width)],
        6 << 30,
        2 << 20,
        10,
        scratch=[
            pltpu.VMEM(perm_row.shape, jnp.int32),
            pltpu.VMEM((width, TILE), F32),
            pltpu.VMEM((width, TILE), F32),
            pltpu.VMEM((width, width), F32),
            pltpu.VMEM((width, TILE), F32),
            pltpu.VMEM((width, TILE), F32),
            pltpu.SemaphoreType.DMA((6, width // TILE)),
        ],
        in_specs=[HBM] * 4,
        out_specs=[HBM, HBM, VMEM],
    )(*map(in_hbm, (perm_row, u_diag, l_diag, l_prev_diag)))
    outs = [shape(sent, columns // 2)] * 2 if paired else [shape(sent, columns)]
    payload = call(
        functools.partial(product_kernel, row_size, paired),
        outs,
        1 << 30,
        10 << 20,
        12,
        scratch=[pltpu.VMEM((sent, columns), F32)],
        in_specs=[SMEM, VMEM, ANY] + [VMEM] * 3,
        out_specs=[VMEM] * len(outs),
    )(row_at, at, lines[0], b_panel, u_cols, y_prev)

    payload, line = lax.optimization_barrier((payload, line))
    far = gather_pieces(line, "col", col_size, inner)
    mine = jnp.concatenate(far, axis=0)
    if paired:
        keep = payload[0] + swapped(payload[1], "row", row_size, 1)
        turn = lambda step: slice(step * column_share, (step + 1) * column_share)
        resid = keep[:share, turn(0)]
        for step in range(1, chips):
            resid = resid + swapped(keep[:share, turn(step)], "row", row_size, 2 * step)
        v = keep[share:, turn(0)]
    else:
        block = lambda array, place: lax.dynamic_slice_in_dim(array, place * column_share, column_share, 1)
        own = block(payload[0], row)
        for step in range(1, row_size):
            own = own + swapped(block(payload[0], row ^ step), "row", row_size, step)
        resid = own[:share] + block(b_panel, row)
        v = own[share:]
    rhs = max(TILE, column_share)
    resid, mine = lax.optimization_barrier((resid, mine))
    resid = jnp.pad(resid, ((0, 0), (0, rhs - column_share)))
    sides = [mine]
    for step in range(1, chips if paired else 1):
        if parts > 1:
            got = swapped(jnp.concatenate([mine, keep[share:, turn(step)]], axis=0), "row", row_size, 2 * step)
            sides.append(got[:width])
            v = v + got[width:]
        else:
            v = v + swapped(keep[share:, turn(step)], "row", row_size, 2 * step)
    v = jnp.pad(v, ((0, 0), (0, rhs - column_share)))
    pieces = gather_pieces(gather_line(resid, "col", col_size, inner), "col", col_size, inner)

    yt, y_mine = call(
        functools.partial(solve_u_kernel, inner, outer, share),
        (shape(rhs, width), shape(share, rhs)),
        200 << 20,
        2 << 20,
        8,
        scratch=[pltpu.VMEM((width, rhs), F32), pltpu.VMEM((width, TILE), F32), pltpu.SemaphoreType.DMA],
        in_specs=[SMEM, VMEM, ANY] + [VMEM] * inner,
        out_specs=[VMEM] * 2,
    )(col_at, u_diag, du, *pieces)

    yt, sides = lax.optimization_barrier((yt, sides))
    mine = jnp.concatenate(sides, axis=1)
    coupling = [mine, swapped(mine, "row", row_size, 1)] if parts > 1 else [mine]
    x = call(
        functools.partial(finish_kernel, inner, outer, share, parts),
        shape(lanes, rhs),
        400 << 20,
        4 << 20,
        8,
        scratch=[
            pltpu.VMEM((width, width), F32),
            pltpu.VMEM((width, TILE), F32),
            pltpu.VMEM((lanes, width), F32),
            pltpu.VMEM((lanes, rhs), F32),
            pltpu.SemaphoreType.DMA((3,)),
        ],
        in_specs=[SMEM, SMEM, VMEM, VMEM, ANY, ANY, VMEM, ANY] + [VMEM] * len(coupling),
        out_specs=VMEM,
    )(col_at, row_at, yt, l_diag, dl, at, perm_row, v, *coupling)

    if paired:
        blocks = [y_mine] + [swapped(y_mine, "row", row_size, step) for step in range(1, row_size)]
        y_part = call(
            merge_kernel,
            shape(share, columns),
            0,
            1 << 17,
            4,
            in_specs=[SMEM, HBM] + [VMEM] * row_size,
            out_specs=VMEM,
        )(row_at, in_hbm(x), *blocks)
    else:
        y_part = lax.all_gather(y_mine[:, :column_share], "row", axis=1, tiled=True)
    return (y_part, x[:picks, :column_share])


def solution(mesh):
    return jax.shard_map(
        per_device,
        mesh=mesh,
        in_specs=(
            P("row", None),
            P("col", "row"),
            P("col", None),
            P(),
            P(),
            P("col", None),
            P(),
            P("col"),
        ),
        out_specs=(P("col", None), P("col", "row")),
        check_vma=False,
    )
```

time: 86.4 us -> 45.2 us (0.52)
  local copies, waits for them, and re-layouts: 18.8 us -> 1.97 us
  between operations: 14.2 us -> 0.91 us
  starting transfers between devices: 9.71 us -> 18.5 us
  matrix products: 6.08 us -> 0 us
  blocking collectives: 5.91 us -> 0 us
  waiting for transfers between devices: 12.4 us -> 8.71 us
  Pallas kernels: 15.6 us -> 12.9 us
  other arithmetic: 3.17 us -> 1.7 us
    unnamed x34 -> x20, local copies, waits for them, and re-layouts: 13.9 us -> 0.96 us
    ppermute x7 -> x14, starting transfers between devices: 9.68 us -> 18.5 us  [swapped(): return lax.ppermute(value, axis, [(dst ^ mask, dst) for dst in range(size)])]
    dot_general x1 -> x0, matrix products: 6.08 us -> none  [per_device(): jnp.dot(u_cols, y_prev, precision=lax.Precision.HIGH, preferred_element_t...]
    all_gather x1 -> x0, blocking collectives: 5.91 us -> none  [per_device(): y_part = lax.all_gather(y_mine[:, :column_share], 'row', axis=1, tiled=True)]
    ppermute x7 -> x14, waiting for transfers between devices: 11.7 us -> 8.71 us  [swapped(): return lax.ppermute(value, axis, [(dst ^ mask, dst) for dst in range(size)])]
    pallas_call x3 -> x5, Pallas kernels: 15.6 us -> 12.9 us  [the longest x1 6.11 us: per_device(): call(invert_kernel, [shape(width, TILE), shape(width, TILE), shape(lanes,...]
    slice x2 -> x3, local copies, waits for them, and re-layouts: 3.25 us -> 0.98 us  [the longest x1 0.97 us: per_device(): sides.append(got[:width])]
    dynamic_slice x1, local copies, waits for them, and re-layouts: 0.97 us -> 0.01 us  [per_device(): lax.dynamic_slice_in_dim(l_coupling, lax.rem(row, parts) * quarter, quart...]
  transfers between devices with their start and end apart: 8 -> 14, of which waited for: 5 -> 4; matrix products, arithmetic and copies ran while one was open for 20% -> 4% of each run, Pallas kernels for 15% -> 27%
where the time goes in v3:
time: 45.2 us; the launch traced here: 44.8 us
  starting transfers between devices  18.5 us (41%)
  Pallas kernels  12.9 us (29%)
  waiting for transfers between devices  8.71 us (19%)
  local copies, waits for them, and re-layouts  1.97 us (4%)
  other arithmetic  1.7 us (4%)
  between operations  0.91 us (2%)
    ppermute x14, starting transfers between devices, swapped(): return lax.ppermute(value, axis, [(dst ^ mask, dst) for dst in range(size)])  18.5 us
    ppermute x14, waiting for transfers between devices, swapped(): return lax.ppermute(value, axis, [(dst ^ mask, dst) for dst in range(size)])  8.71 us
    pallas_call x1, Pallas kernels, per_device(): call(invert_kernel, [shape(width, TILE), shape(width, TILE), shape(lanes,...  6.11 us
    pallas_call x1, Pallas kernels, per_device(): call(functools.partial(finish_kernel, inner, outer, share, parts), shape(...  2.77 us
    pallas_call x1, Pallas kernels, per_device(): call(functools.partial(product_kernel, row_size, paired), outs, 1 << 30,...  2.31 us
    pallas_call x1, Pallas kernels, per_device(): call(functools.partial(solve_u_kernel, inner, outer, share), (shape(rhs,...  1.09 us
    slice x1, local copies, waits for them, and re-layouts, per_device(): sides.append(got[:width])  0.97 us
    unnamed x20, local copies, waits for them, and re-layouts  0.96 us
  transfers between devices with their start and end apart: 14, of which 4 were waited for; matrix products, arithmetic and copies ran while one was open for 4% of the time, Pallas kernels for 27%

profile of v3, /device:TPU:0, one launch (start us, length us, event | category | flops | bytes accessed | tf_op | source)
XLA Modules:
  0.0 44.8 jit_solution(9489009203516418199)
XLA Ops:
  0.6 0.0 copy-start
  0.7 0.9 %copy-done = f32[64,512]{1,0:T(8,128)S(1)} copy-done((f32[64,512]{1,0:T(8,128)S(1)}, f32[64,512]{1,0:T(8,128)}, u32[]{:S(2)}) %copy-start) | copy-done | bytes 131096
  1.5 3.0 %collective-permute-start = (f32[64,128]{1,0:T(8,128)S(1)}, f32[64,128]{1,0:T(8,128)S(1)}, u32[]{:S(2)}, u32[]{:S(2)}) collective-permute-start(f32[64,128]{1,0:T(8,128)S(1)} %constant_dynamic-slice_fusion), channel_id=1, source_target_pairs={{2,0},{3,1},{0,2},{1,3},{6,4},{7,5},{4,6},{5,7},{10,8},{11,9},{8,1... | collective-permute-start | bytes 98312 | tf_op jit(solution)/shard_map/ppermute | solution.py:275
  4.6 0.0 copy-start.1
  4.6 0.0 copy-start.2
  4.6 0.0 copy-start.5
  4.6 6.1 %shard_map.95 = (f32[512,128]{1,0:T(8,128)S(1)}, f32[512,128]{1,0:T(8,128)S(1)}, f32[128,512]{1,0:T(8,128)S(1)}) custom-call(s32[1,128]{1,0:T(1,128)} %bitcast.3, f32[512,512]{1,0:T(8,128)} %u_ref.1, f32[512,512]{1,0:T(8,128)} %l_ref.1, f32[512,512]{1,0:T(8,128)} %lp_hbm.1), custom_call_target="tpu_custom_call" | custom-call | flops 6442450944 | bytes 2097152 | tf_op jit(solution)/shard_map/pallas_call | solution.py:315
  10.7 0.0 copy-start.3
  10.7 0.0 copy-start.4
  10.7 0.0 copy-start.6
  10.7 0.0 collective-permute-done
  10.8 2.7 %collective-permute-start.1 = (f32[128,128]{1,0:T(8,128)S(1)}, f32[128,128]{1,0:T(8,128)S(1)}, u32[]{:S(2)}, u32[]{:S(2)}) collective-permute-start(f32[128,128]{1,0:T(8,128)S(1)} %pad_maximum_fusion.3.after_ref), channel_id=1, source_target_pairs={{4,0},{5,1},{6,2},{7,3},{0,4},{1,5},{2,6},{3,7},{12,8},{13,9},{14,... | collective-permute-start | bytes 196616 | tf_op jit(solution)/shard_map/ppermute | solution.py:275
  13.4 0.0 copy-done.1
  13.4 0.0 copy-done.2
  13.4 0.0 copy-done.5
  13.4 2.3 %shard_map.96 = (f32[192,256]{1,0:T(8,128)S(1)}, f32[192,256]{1,0:T(8,128)S(1)}) custom-call(s32[1,1]{1,0:T(1,128)} %bitcast.row_ref, f32[128,512]{1,0:T(8,128)S(1)} %get-tuple-element.18.at_ref.at_any, f32[128,128]{1,0:T(8,128)S(1)} %pad_maximum_fusion.3.after_ref, f32[64,512]{1,0:T(8,128)S(1)} %copy-done.5, f32[64,4096]{1,0:T(8,128)S(1)} %copy-done.2, ...), custom_call_target="tpu_custom_call" | custom-call | flops 1073741824 | bytes 10485760 | tf_op jit(solution)/shard_map/pallas_call | solution.py:334
  15.7 0.8 %collective-permute-done.1 = f32[128,128]{1,0:T(8,128)S(1)} collective-permute-done((f32[128,128]{1,0:T(8,128)S(1)}, f32[128,128]{1,0:T(8,128)S(1)}, u32[]{:S(2)}, u32[]{:S(2)}) %collective-permute-start.1) | collective-permute-done | bytes 65568 | tf_op jit(solution)/shard_map/ppermute | solution.py:275
  16.5 0.1 collective-permute-start.2
  16.6 1.6 %collective-permute-start.4 = (f32[256,128]{1,0:T(8,128)S(1)}, f32[256,128]{1,0:T(8,128)S(1)}, u32[]{:S(2)}, u32[]{:S(2)}) collective-permute-start(f32[256,128]{1,0:T(8,128)S(1)} %pad_maximum_fusion.2), channel_id=1, source_target_pairs={{1,0},{0,1},{3,2},{2,3},{5,4},{4,5},{7,6},{6,7},{9,8},{8,9},{11,10... | collective-permute-start | bytes 393224 | tf_op jit(solution)/shard_map/ppermute | solution.py:275
  18.3 0.0 collective-permute-done.2
  18.3 0.0 copy-start.7
  18.3 1.6 %collective-permute-start.3 = (f32[64,128]{1,0:T(8,128)S(1)}, f32[64,128]{1,0:T(8,128)S(1)}, u32[]{:S(2)}, u32[]{:S(2)}) collective-permute-start(f32[64,128]{1,0:T(8,128)S(1)} %slice.25), channel_id=1, source_target_pairs={{16,0},{24,8},{0,16},{8,24},{17,1},{25,9},{1,17},{9,25},{18,2},{26... | collective-permute-start | bytes 98312 | tf_op jit(solution)/shard_map/ppermute | solution.py:275
  19.9 2.7 %collective-permute-done.4 = f32[256,128]{1,0:T(8,128)S(1)} collective-permute-done((f32[256,128]{1,0:T(8,128)S(1)}, f32[256,128]{1,0:T(8,128)S(1)}, u32[]{:S(2)}, u32[]{:S(2)}) %collective-permute-start.4) | collective-permute-done | bytes 131104 | tf_op jit(solution)/shard_map/ppermute | solution.py:275
  22.6 0.0 collective-permute-done.3
  22.6 0.0 copy-done.7
  22.6 0.1 collective-permute-start.5
  22.7 2.8 %collective-permute-start.6 = (f32[64,128]{1,0:T(8,128)S(1)}, f32[64,128]{1,0:T(8,128)S(1)}, u32[]{:S(2)}, u32[]{:S(2)}) collective-permute-start(f32[64,128]{1,0:T(8,128)S(1)} %slice_add_fusion.1), channel_id=1, source_target_pairs={{4,0},{5,1},{6,2},{7,3},{0,4},{1,5},{2,6},{3,7},{12,8},{13,9},{14,... | collective-permute-start | bytes 98312 | tf_op jit(solution)/shard_map/ppermute | solution.py:275
  25.5 1.6 %collective-permute-start.7 = (f32[64,128]{1,0:T(8,128)S(1)}, f32[64,128]{1,0:T(8,128)S(1)}, u32[]{:S(2)}, u32[]{:S(2)}) collective-permute-start(f32[64,128]{1,0:T(8,128)S(1)} %slice_add_fusion.1), channel_id=1, source_target_pairs={{6,0},{7,1},{4,2},{5,3},{2,4},{3,5},{0,6},{1,7},{14,8},{15,9},{12,... | collective-permute-start | bytes 98312 | tf_op jit(solution)/shard_map/ppermute | solution.py:275
  27.1 0.7 %pad_maximum_fusion = f32[640,128]{1,0:T(8,128)} fusion(f32[128,128]{1,0:T(8,128)S(1)} %slice.26, f32[512,128]{1,0:T(8,128)S(1)} %pad_maximum_fusion.1), kind=kLoop, calls=%fused_computation | loop fusion | flops 81920 | bytes 655360 | tf_op jit(solution)/shard_map/concatenate | solution.py:368
  27.8 1.6 %collective-permute-start.9 = (f32[640,128]{1,0:T(8,128)}, f32[640,128]{1,0:T(8,128)}, u32[]{:S(2)}, u32[]{:S(2)}) collective-permute-start(f32[640,128]{1,0:T(8,128)} %pad_maximum_fusion), channel_id=1, source_target_pairs={{16,0},{24,8},{0,16},{8,24},{17,1},{25,9},{1,17},{9,25},{18,2},{26... | collective-permute-start | bytes 983048 | tf_op jit(solution)/shard_map/ppermute | solution.py:275
  29.4 0.0 collective-permute-done.5
  29.4 0.0 collective-permute-done.6
  29.4 1.8 %collective-permute-done.7 = f32[64,128]{1,0:T(8,128)S(1)} collective-permute-done((f32[64,128]{1,0:T(8,128)S(1)}, f32[64,128]{1,0:T(8,128)S(1)}, u32[]{:S(2)}, u32[]{:S(2)}) %collective-permute-start.7) | collective-permute-done | bytes 32800 | tf_op jit(solution)/shard_map/ppermute | solution.py:275
  31.2 1.5 %collective-permute-start.8 = (f32[256,128]{1,0:T(8,128)S(1)}, f32[256,128]{1,0:T(8,128)S(1)}, u32[]{:S(2)}, u32[]{:S(2)}) collective-permute-start(f32[256,128]{1,0:T(8,128)S(1)} %constant_dynamic-update-slice_fusion.refs_0_), channel_id=1, source_target_pairs={{1,0},{0,1},{3,2},{2,3},{5,4},{4,5},{7,6},{6,7},{9,8},{8,9},{11,10... | collective-permute-start | bytes 393224 | tf_op jit(solution)/shard_map/ppermute | solution.py:275
  32.7 3.4 %collective-permute-done.8.refs_1_ = f32[256,128]{1,0:T(8,128)S(1)} collective-permute-done((f32[256,128]{1,0:T(8,128)S(1)}, f32[256,128]{1,0:T(8,128)S(1)}, u32[]{:S(2)}, u32[]{:S(2)}) %collective-permute-start.8) | collective-permute-done | bytes 131104 | tf_op jit(solution)/shard_map/ppermute | solution.py:275
  36.2 0.0 copy-done.3
  36.2 1.1 %shard_map.97 = (f32[128,512]{1,0:T(8,128)S(1)}, f32[64,128]{1,0:T(8,128)S(1)}) custom-call(s32[1,1]{1,0:T(1,128)} %bitcast.1.col_ref, f32[512,512]{1,0:T(8,128)S(1)} %copy-done.3, f32[512,128]{1,0:T(8,128)S(1)} %get-tuple-element.17.du_any, f32[256,128]{1,0:T(8,128)S(1)} %constant_dynamic-update-slice_fusion.refs_0_, ...), custom_call_target="tpu_custom_call" | custom-call | flops 209715200 | bytes 2097152 | tf_op jit(solution)/shard_map/pallas_call | solution.py:376
  37.3 0.0 collective-permute-done.9
  37.3 1.0 %slice.27 = f32[512,128]{1,0:T(8,128)S(1)} slice(f32[640,128]{1,0:T(8,128)} %collective-permute-done.9), slice={[0:512], [0:128]} | slice | bytes 524288 | tf_op jit(solution)/shard_map/slice | solution.py:369
  38.3 0.1 collective-permute-start.10
  38.4 0.5 %collective-permute-start.11 = (f32[64,128]{1,0:T(8,128)S(1)}, f32[64,128]{1,0:T(8,128)S(1)}, u32[]{:S(2)}, u32[]{:S(2)}) collective-permute-start(f32[64,128]{1,0:T(8,128)S(1)} %get-tuple-element.31.refs_0_), channel_id=1, source_target_pairs={{8,0},{0,8},{24,16},{16,24},{9,1},{1,9},{25,17},{17,25},{10,2},{2,... | collective-permute-start | bytes 98312 | tf_op jit(solution)/shard_map/ppermute | solution.py:275
  38.9 1.5 %collective-permute-start.12 = (f32[64,128]{1,0:T(8,128)S(1)}, f32[64,128]{1,0:T(8,128)S(1)}, u32[]{:S(2)}, u32[]{:S(2)}) collective-permute-start(f32[64,128]{1,0:T(8,128)S(1)} %get-tuple-element.31.refs_0_), channel_id=1, source_target_pairs={{16,0},{24,8},{0,16},{8,24},{17,1},{25,9},{1,17},{9,25},{18,2},{26... | collective-permute-start | bytes 98312 | tf_op jit(solution)/shard_map/ppermute | solution.py:275
  40.4 0.0 collective-permute-start.13
  40.4 0.9 %slice_add_fusion.v_any = f32[128,128]{1,0:T(8,128)S(1)} fusion(f32[640,128]{1,0:T(8,128)} %collective-permute-done.9, f32[192,256]{1,0:T(8,128)} %copy-done.7), kind=kLoop, calls=%fused_computation.3 | loop fusion | flops 16384 | bytes 196608 | tf_op jit(solution)/shard_map/add | solution.py:370
  41.3 0.0 collective-permute-done.10.refs_1_
  41.3 0.0 copy-done.4
  41.3 0.0 copy-done.6
  41.3 2.8 %shard_map.98.after_ref = f32[128,128]{1,0:T(8,128)} custom-call(s32[1,1]{1,0:T(1,128)} %bitcast.1.col_ref, s32[1,1]{1,0:T(1,128)} %bitcast.row_ref, f32[128,512]{1,0:T(8,128)S(1)} %get-tuple-element.27.yt_ref, f32[512,512]{1,0:T(8,128)S(1)} %copy-done.4, f32[512,128]{1,0:T(8,128)S(1)} %get-tuple-element.28.dl_any, ...), custom_call_target="tpu_custom_call" | custom-call | flops 419430400 | bytes 4194304 | tf_op jit(solution)/shard_map/pallas_call | solution.py:390
  44.1 0.0 collective-permute-done.11.refs_1_
  44.1 0.0 collective-permute-done.12.refs_2_
  44.1 0.0 collective-permute-done.13.refs_3_
  44.1 0.7 %shard_map.99 = f32[64,512]{1,0:T(8,128)} custom-call(s32[1,1]{1,0:T(1,128)} %bitcast.row_ref, f32[128,128]{1,0:T(8,128)} %shard_map.98.after_ref, f32[64,128]{1,0:T(8,128)S(1)} %get-tuple-element.31.refs_0_, f32[64,128]{1,0:T(8,128)S(1)} %collective-permute-done.11.refs_1_, f32[64,128]{1,0:T(8,128)S(1)} %collective-permute-done.12.refs_2_, ...), custom_call_target="tpu_custom_call" | custom-call | bytes 131072 | tf_op jit(solution)/shard_map/pallas_call | solution.py:409
  (14 shorter events, 0.1 us)
Async XLA Ops:
  0.6 0.9 %copy-start = (f32[64,512]{1,0:T(8,128)S(1)}, f32[64,512]{1,0:T(8,128)}, u32[]{:S(2)}) copy-start(f32[64,512]{1,0:T(8,128)} %param.13) | copy-start | bytes 393220
  1.5 9.2 %collective-permute-start = (f32[64,128]{1,0:T(8,128)S(1)}, f32[64,128]{1,0:T(8,128)S(1)}, u32[]{:S(2)}, u32[]{:S(2)}) collective-permute-start(f32[64,128]{1,0:T(8,128)S(1)} %constant_dynamic-slice_fusion), channel_id=1, source_target_pairs={{2,0},{3,1},{0,2},{1,3},{6,4},{7,5},{4,6},{5,7},{10,8},{11,9},{8,1... | collective-permute-start | bytes 98312 | tf_op jit(solution)/shard_map/ppermute | solution.py:275
  4.6 8.8 %copy-start.1 = (f32[4096,512]{1,0:T(8,128)S(1)}, f32[4096,512]{1,0:T(8,128)}, u32[]{:S(2)}) copy-start(f32[4096,512]{1,0:T(8,128)} %y_ref.1) | copy-start | bytes 25165828
  4.6 8.8 %copy-start.2 = (f32[64,4096]{1,0:T(8,128)S(1)}, f32[64,4096]{1,0:T(8,128)}, u32[]{:S(2)}) copy-start(f32[64,4096]{1,0:T(8,128)} %u_cols_ref.1) | copy-start | bytes 3145732
  4.6 8.8 %copy-start.5 = (f32[64,512]{1,0:T(8,128)S(1)}, f32[64,512]{1,0:T(8,128)}, u32[]{:S(2)}) copy-start(f32[64,512]{1,0:T(8,128)} %b_ref.1) | copy-start | bytes 393220
  10.7 25.5 %copy-start.3 = (f32[512,512]{1,0:T(8,128)S(1)}, f32[512,512]{1,0:T(8,128)}, u32[]{:S(2)}) copy-start(f32[512,512]{1,0:T(8,128)} %u_ref.1) | copy-start | bytes 3145732
  10.7 30.6 %copy-start.4 = (f32[512,512]{1,0:T(8,128)S(1)}, f32[512,512]{1,0:T(8,128)}, u32[]{:S(2)}) copy-start(f32[512,512]{1,0:T(8,128)} %l_ref.1) | copy-start | bytes 3145732
  10.7 30.6 %copy-start.6 = (s32[128]{0:T(128)S(1)}, s32[128]{0:T(128)}, u32[]{:S(2)}) copy-start(s32[128]{0:T(128)} %param.15) | copy-start | bytes 1540
  10.8 5.8 %collective-permute-start.1 = (f32[128,128]{1,0:T(8,128)S(1)}, f32[128,128]{1,0:T(8,128)S(1)}, u32[]{:S(2)}, u32[]{:S(2)}) collective-permute-start(f32[128,128]{1,0:T(8,128)S(1)} %pad_maximum_fusion.3.after_ref), channel_id=1, source_target_pairs={{4,0},{5,1},{6,2},{7,3},{0,4},{1,5},{2,6},{3,7},{12,8},{13,9},{14,... | collective-permute-start | bytes 196616 | tf_op jit(solution)/shard_map/ppermute | solution.py:275
  16.5 1.7 %collective-permute-start.2 = (f32[192,256]{1,0:T(8,128)S(1)}, f32[192,256]{1,0:T(8,128)S(1)}, u32[]{:S(2)}, u32[]{:S(2)}) collective-permute-start(f32[192,256]{1,0:T(8,128)S(1)} %get-tuple-element.22), channel_id=1, source_target_pairs={{8,0},{0,8},{24,16},{16,24},{9,1},{1,9},{25,17},{17,25},{10,2},{2,... | collective-permute-start | bytes 589832 | tf_op jit(solution)/shard_map/ppermute | solution.py:275
  16.6 5.9 %collective-permute-start.4 = (f32[256,128]{1,0:T(8,128)S(1)}, f32[256,128]{1,0:T(8,128)S(1)}, u32[]{:S(2)}, u32[]{:S(2)}) collective-permute-start(f32[256,128]{1,0:T(8,128)S(1)} %pad_maximum_fusion.2), channel_id=1, source_target_pairs={{1,0},{0,1},{3,2},{2,3},{5,4},{4,5},{7,6},{6,7},{9,8},{8,9},{11,10... | collective-permute-start | bytes 393224 | tf_op jit(solution)/shard_map/ppermute | solution.py:275
  18.3 4.3 %copy-start.7 = (f32[192,256]{1,0:T(8,128)}, f32[192,256]{1,0:T(8,128)S(1)}, u32[]{:S(2)}) copy-start(f32[192,256]{1,0:T(8,128)S(1)} %add.13) | copy-start | bytes 589828
  18.3 4.2 %collective-permute-start.3 = (f32[64,128]{1,0:T(8,128)S(1)}, f32[64,128]{1,0:T(8,128)S(1)}, u32[]{:S(2)}, u32[]{:S(2)}) collective-permute-start(f32[64,128]{1,0:T(8,128)S(1)} %slice.25), channel_id=1, source_target_pairs={{16,0},{24,8},{0,16},{8,24},{17,1},{25,9},{1,17},{9,25},{18,2},{26... | collective-permute-start | bytes 98312 | tf_op jit(solution)/shard_map/ppermute | solution.py:275
  22.6 6.8 %collective-permute-start.5 = (f32[64,128]{1,0:T(8,128)S(1)}, f32[64,128]{1,0:T(8,128)S(1)}, u32[]{:S(2)}, u32[]{:S(2)}) collective-permute-start(f32[64,128]{1,0:T(8,128)S(1)} %slice_add_fusion.1), channel_id=1, source_target_pairs={{2,0},{3,1},{0,2},{1,3},{6,4},{7,5},{4,6},{5,7},{10,8},{11,9},{8,1... | collective-permute-start | bytes 98312 | tf_op jit(solution)/shard_map/ppermute | solution.py:275
  22.7 6.7 %collective-permute-start.6 = (f32[64,128]{1,0:T(8,128)S(1)}, f32[64,128]{1,0:T(8,128)S(1)}, u32[]{:S(2)}, u32[]{:S(2)}) collective-permute-start(f32[64,128]{1,0:T(8,128)S(1)} %slice_add_fusion.1), channel_id=1, source_target_pairs={{4,0},{5,1},{6,2},{7,3},{0,4},{1,5},{2,6},{3,7},{12,8},{13,9},{14,... | collective-permute-start | bytes 98312 | tf_op jit(solution)/shard_map/ppermute | solution.py:275
  25.5 5.7 %collective-permute-start.7 = (f32[64,128]{1,0:T(8,128)S(1)}, f32[64,128]{1,0:T(8,128)S(1)}, u32[]{:S(2)}, u32[]{:S(2)}) collective-permute-start(f32[64,128]{1,0:T(8,128)S(1)} %slice_add_fusion.1), channel_id=1, source_target_pairs={{6,0},{7,1},{4,2},{5,3},{2,4},{3,5},{0,6},{1,7},{14,8},{15,9},{12,... | collective-permute-start | bytes 98312 | tf_op jit(solution)/shard_map/ppermute | solution.py:275
  27.8 9.5 %collective-permute-start.9 = (f32[640,128]{1,0:T(8,128)}, f32[640,128]{1,0:T(8,128)}, u32[]{:S(2)}, u32[]{:S(2)}) collective-permute-start(f32[640,128]{1,0:T(8,128)} %pad_maximum_fusion), channel_id=1, source_target_pairs={{16,0},{24,8},{0,16},{8,24},{17,1},{25,9},{1,17},{9,25},{18,2},{26... | collective-permute-start | bytes 983048 | tf_op jit(solution)/shard_map/ppermute | solution.py:275
  31.2 5.0 %collective-permute-start.8 = (f32[256,128]{1,0:T(8,128)S(1)}, f32[256,128]{1,0:T(8,128)S(1)}, u32[]{:S(2)}, u32[]{:S(2)}) collective-permute-start(f32[256,128]{1,0:T(8,128)S(1)} %constant_dynamic-update-slice_fusion.refs_0_), channel_id=1, source_target_pairs={{1,0},{0,1},{3,2},{2,3},{5,4},{4,5},{7,6},{6,7},{9,8},{8,9},{11,10... | collective-permute-start | bytes 393224 | tf_op jit(solution)/shard_map/ppermute | solution.py:275
  38.3 3.0 %collective-permute-start.10 = (f32[512,256]{1,0:T(8,128)S(1)}, f32[512,256]{1,0:T(8,128)S(1)}, u32[]{:S(2)}, u32[]{:S(2)}) collective-permute-start(f32[512,256]{1,0:T(8,128)S(1)} %constant_dynamic-update-slice_fusion.4.refs_0_), channel_id=1, source_target_pairs={{8,0},{0,8},{24,16},{16,24},{9,1},{1,9},{25,17},{17,25},{10,2},{2,... | collective-permute-start | bytes 1572872 | tf_op jit(solution)/shard_map/ppermute | solution.py:275
  38.4 5.7 %collective-permute-start.11 = (f32[64,128]{1,0:T(8,128)S(1)}, f32[64,128]{1,0:T(8,128)S(1)}, u32[]{:S(2)}, u32[]{:S(2)}) collective-permute-start(f32[64,128]{1,0:T(8,128)S(1)} %get-tuple-element.31.refs_0_), channel_id=1, source_target_pairs={{8,0},{0,8},{24,16},{16,24},{9,1},{1,9},{25,17},{17,25},{10,2},{2,... | collective-permute-start | bytes 98312 | tf_op jit(solution)/shard_map/ppermute | solution.py:275
  38.9 5.2 %collective-permute-start.12 = (f32[64,128]{1,0:T(8,128)S(1)}, f32[64,128]{1,0:T(8,128)S(1)}, u32[]{:S(2)}, u32[]{:S(2)}) collective-permute-start(f32[64,128]{1,0:T(8,128)S(1)} %get-tuple-element.31.refs_0_), channel_id=1, source_target_pairs={{16,0},{24,8},{0,16},{8,24},{17,1},{25,9},{1,17},{9,25},{18,2},{26... | collective-permute-start | bytes 98312 | tf_op jit(solution)/shard_map/ppermute | solution.py:275
  40.4 3.7 %collective-permute-start.13 = (f32[64,128]{1,0:T(8,128)S(1)}, f32[64,128]{1,0:T(8,128)S(1)}, u32[]{:S(2)}, u32[]{:S(2)}) collective-permute-start(f32[64,128]{1,0:T(8,128)S(1)} %get-tuple-element.31.refs_0_), channel_id=1, source_target_pairs={{24,0},{16,8},{8,16},{0,24},{25,1},{17,9},{9,17},{1,25},{26,2},{18... | collective-permute-start | bytes 98312 | tf_op jit(solution)/shard_map/ppermute | solution.py:275

commit v4 on v3

--- a/solution.py
+++ b/solution.py
@@ -75,53 +75,55 @@
     return copies
 
 
-def invert_kernel(
-    perm_hbm, u_hbm, l_hbm, lp_hbm, du_hbm, dl_hbm, at_ref, perm_ref, u_ref, l_ref, lp_ref, du_ref, dl_ref, sems
-):
+def solve_selected_kernel(perm_hbm, lp_hbm, at_ref, perm_ref, tiles_ref, lp_ref, sems):
     width = lp_ref.shape[0]
     count = width // TILE
     spans = [slice(i * TILE, (i + 1) * TILE) for i in range(count)]
     tiles = [pl.ds(i * TILE, TILE) for i in range(count)]
-    copies = started(
-        [
-            pltpu.make_async_copy(src.at[tiles[i], tiles[i]], dst.at[tiles[i], :], sems.at[k, i])
-            for k, (src, dst) in enumerate([(u_hbm, u_ref), (l_hbm, l_ref)])
-            for i in range(count)
-        ]
-        + [pltpu.make_async_copy(lp_hbm, lp_ref, sems.at[2, 0]), pltpu.make_async_copy(perm_hbm, perm_ref, sems.at[3, 0])]
+    early = started(
+        [pltpu.make_async_copy(lp_hbm.at[tile, tile], tiles_ref.at[tile, :], sems.at[0, i]) for i, tile in enumerate(tiles)]
     )
-    for copy in copies:
+    late = started(
+        [pltpu.make_async_copy(lp_hbm, lp_ref, sems.at[1, 0]), pltpu.make_async_copy(perm_hbm, perm_ref, sems.at[2, 0])]
+    )
+    for copy in early:
         copy.wait()
+    found = unit_lower_inverses([tiles_ref[span, :] for span in spans])
+    for copy in late:
+        copy.wait()
+    perm = perm_ref[...]
+    picks = perm.shape[1]
+    remain = []
+    for i in range(count):
+        row_ids = i * TILE + lax.broadcasted_iota(jnp.int32, (TILE, picks), 0)
+        remain.append((row_ids == perm).astype(F32))
+    for i, span in enumerate(spans):
+        value = joined(halves(found[i]), halves(remain[i]))
+        solved = halves(value)
+        for j in range(i + 1, count):
+            remain[j] = remain[j] - joined(halves(tile_of(lp_ref, j, i)), solved)
+        at_ref[:, span] = value.T
+
+
+def invert_upper_kernel(after_ref, u_ref, du_ref):
+    del after_ref
     rows, cols = iotas()
     diag = rows == cols
     blocks, scales = [], []
-    for span in spans:
-        upper = u_ref[span, :].T
+    for i in range(u_ref.shape[0] // TILE):
+        upper = tile_of(u_ref, i, i).T
         only = jnp.where(diag, upper, 0.0)
         blocks.append(upper * (1.0 / jnp.sum(only, axis=1, keepdims=True)))
         scales.append(1.0 / jnp.sum(only, axis=0, keepdims=True))
-    blocks += [l_ref[span, :] for span in spans]
-    blocks += [tile_of(lp_ref, i, i) for i in range(count)]
-    found = unit_lower_inverses(blocks)
-    for i, span in enumerate(spans):
-        du_ref[span, :] = (found[i] * scales[i]).T
-        dl_ref[span, :] = found[count + i]
-    out = started(
-        [pltpu.make_async_copy(du_ref, du_hbm, sems.at[4, 0]), pltpu.make_async_copy(dl_ref, dl_hbm, sems.at[5, 0])]
-    )
-    perm = perm_ref[...]
-    picks = perm.shape[1]
-    solved = []
-    for i, span in enumerate(spans):
-        row_ids = i * TILE + lax.broadcasted_iota(jnp.int32, (TILE, picks), 0)
-        remain = (row_ids == perm).astype(F32)
-        for j in range(i):
-            remain = remain - joined(halves(tile_of(lp_ref, i, j)), solved[j])
-        value = joined(halves(found[2 * count + i]), halves(remain))
-        solved.append(halves(value))
-        at_ref[:, span] = value.T
-    for copy in out:
-        copy.wait()
+    for i, inv in enumerate(unit_lower_inverses(blocks)):
+        du_ref[i * TILE : (i + 1) * TILE, :] = (inv * scales[i]).T
+
+
+def invert_lower_kernel(after_ref, l_ref, dl_ref):
+    del after_ref
+    blocks = [tile_of(l_ref, i, i) for i in range(l_ref.shape[0] // TILE)]
+    for i, inv in enumerate(unit_lower_inverses(blocks)):
+        dl_ref[i * TILE : (i + 1) * TILE, :] = inv
 
 
 def product_kernel(size, paired, row_ref, at_ref, after_ref, b_ref, u_cols_ref, y_ref, *refs):
@@ -167,7 +169,8 @@
         full_ref[aligned_span(at, share), columns] = piece[turn * share : (turn + 1) * share, :]
 
 
-def solve_u_kernel(inner, outer, share, col_ref, u_ref, du_any, *refs):
+def solve_u_kernel(inner, outer, share, col_ref, after_ref, u_ref, du_any, *refs):
+    del after_ref
     piece_refs = refs[:inner]
     yt_ref, y_ref, full_ref, du_ref, sem = refs[inner:]
     copy = pltpu.make_async_copy(du_any, du_ref, sem)
@@ -312,24 +315,24 @@
     perm_row = jnp.pad(perm, (0, max(TILE - picks, 0)), constant_values=-1)[None, :]
     lanes = perm_row.shape[1]
     sent = share + lanes
-    du, dl, at = call(
-        invert_kernel,
-        [shape(width, TILE), shape(width, TILE), shape(lanes, width)],
+    at = call(
+        solve_selected_kernel,
+        shape(lanes, width),
         6 << 30,
         2 << 20,
-        10,
+        8,
         scratch=[
             pltpu.VMEM(perm_row.shape, jnp.int32),
             pltpu.VMEM((width, TILE), F32),
-            pltpu.VMEM((width, TILE), F32),
             pltpu.VMEM((width, width), F32),
-            pltpu.VMEM((width, TILE), F32),
-            pltpu.VMEM((width, TILE), F32),
-            pltpu.SemaphoreType.DMA((6, width // TILE)),
+            pltpu.SemaphoreType.DMA((3, width // TILE)),
         ],
-        in_specs=[HBM] * 4,
-        out_specs=[HBM, HBM, VMEM],
-    )(*map(in_hbm, (perm_row, u_diag, l_diag, l_prev_diag)))
+        in_specs=[HBM] * 2,
+        out_specs=VMEM,
+    )(in_hbm(perm_row), in_hbm(l_prev_diag))
+    inverses = lambda kernel, after, matrix: call(
+        kernel, shape(width, TILE), 2 << 30, 2 << 20, 8, in_specs=[ANY, VMEM], out_specs=VMEM
+    )(after, matrix)
     outs = [shape(sent, columns // 2)] * 2 if paired else [shape(sent, columns)]
     payload = call(
         functools.partial(product_kernel, row_size, paired),
@@ -343,35 +346,30 @@
     )(row_at, at, lines[0], b_panel, u_cols, y_prev)
 
     payload, line = lax.optimization_barrier((payload, line))
-    far = gather_pieces(line, "col", col_size, inner)
-    mine = jnp.concatenate(far, axis=0)
     if paired:
         keep = payload[0] + swapped(payload[1], "row", row_size, 1)
-        turn = lambda step: slice(step * column_share, (step + 1) * column_share)
-        resid = keep[:share, turn(0)]
+        keep, line = lax.optimization_barrier((keep, line))
+        turn = lambda step: keep[:, step * column_share : (step + 1) * column_share]
+        own = turn(0)
         for step in range(1, chips):
-            resid = resid + swapped(keep[:share, turn(step)], "row", row_size, 2 * step)
-        v = keep[share:, turn(0)]
+            own = own + swapped(turn(step), "row", row_size, 2 * step)
+        resid = own[:share]
     else:
         block = lambda array, place: lax.dynamic_slice_in_dim(array, place * column_share, column_share, 1)
         own = block(payload[0], row)
         for step in range(1, row_size):
             own = own + swapped(block(payload[0], row ^ step), "row", row_size, step)
         resid = own[:share] + block(b_panel, row)
-        v = own[share:]
     rhs = max(TILE, column_share)
-    resid, mine = lax.optimization_barrier((resid, mine))
+    mine = jnp.concatenate(gather_pieces(line, "col", col_size, inner), axis=0)
+    du = inverses(invert_upper_kernel, keep if paired else payload[0], u_diag)
+    resid, mine, du = lax.optimization_barrier((resid, mine, du))
     resid = jnp.pad(resid, ((0, 0), (0, rhs - column_share)))
-    sides = [mine]
-    for step in range(1, chips if paired else 1):
-        if parts > 1:
-            got = swapped(jnp.concatenate([mine, keep[share:, turn(step)]], axis=0), "row", row_size, 2 * step)
-            sides.append(got[:width])
-            v = v + got[width:]
-        else:
-            v = v + swapped(keep[share:, turn(step)], "row", row_size, 2 * step)
-    v = jnp.pad(v, ((0, 0), (0, rhs - column_share)))
-    pieces = gather_pieces(gather_line(resid, "col", col_size, inner), "col", col_size, inner)
+    v = jnp.pad(own[share:], ((0, 0), (0, rhs - column_share)))
+    sides = [mine] + [swapped(mine, "row", row_size, 2 * step) for step in range(1, chips if parts > 1 else 1)]
+    line = gather_line(resid, "col", col_size, inner)
+    dl = inverses(invert_lower_kernel, line, l_diag)
+    pieces = gather_pieces(line, "col", col_size, inner)
 
     yt, y_mine = call(
         functools.partial(solve_u_kernel, inner, outer, share),
@@ -380,9 +378,9 @@
         2 << 20,
         8,
         scratch=[pltpu.VMEM((width, rhs), F32), pltpu.VMEM((width, TILE), F32), pltpu.SemaphoreType.DMA],
-        in_specs=[SMEM, VMEM, ANY] + [VMEM] * inner,
+        in_specs=[SMEM, ANY, VMEM, ANY] + [VMEM] * inner,
         out_specs=[VMEM] * 2,
-    )(col_at, u_diag, du, *pieces)
+    )(col_at, dl, u_diag, du, *pieces)
 
     yt, sides = lax.optimization_barrier((yt, sides))
     mine = jnp.concatenate(sides, axis=1)

time: 45.2 us -> 43.6 us (0.965)
  Pallas kernels: 12.9 us -> 14.6 us
  other arithmetic: 1.7 us -> 0.08 us
  starting transfers between devices: 18.5 us -> 17.3 us
  local copies, waits for them, and re-layouts: 1.97 us -> 1 us
  waiting for transfers between devices: 8.71 us -> 9.32 us
    pallas_call x1 -> x3, Pallas kernels: 6.11 us -> 7.74 us  [the longest x1 4.15 us: per_device(): call(solve_selected_kernel, shape(lanes, width), 6 << 30, 2 << 20, 8, scr...]
    ppermute x14, starting transfers between devices: 18.5 us -> 17.3 us  [swapped(): return lax.ppermute(value, axis, [(dst ^ mask, dst) for dst in range(size)])]
    slice x3, local copies, waits for them, and re-layouts: 0.98 us -> 0.02 us  [the longest x1 0.01 us: per_device(): turn = lambda step: keep[:, step * column_share:(step + 1) * column_share]]
    add x2 -> x1, other arithmetic: 0.89 us -> 0.02 us  [per_device(): own = own + swapped(turn(step), 'row', row_size, 2 * step)]
    concatenate x2 -> x1, other arithmetic: 0.77 us -> 0.02 us  [per_device(): mine = jnp.concatenate(gather_pieces(line, 'col', col_size, inner), axis=0)]
    ppermute x14, waiting for transfers between devices: 8.71 us -> 9.32 us  [swapped(): return lax.ppermute(value, axis, [(dst ^ mask, dst) for dst in range(size)])]
    unnamed x20 -> x18, local copies, waits for them, and re-layouts: 0.96 us -> 0.95 us
  transfers between devices with their start and end apart: 14 -> 14, of which waited for: 4 -> 6; matrix products, arithmetic and copies ran while one was open for 4% -> 0% of each run, Pallas kernels for 27% -> 32%
where the time goes in v4:
time: 43.6 us; the launch traced here: 43.2 us
  starting transfers between devices  17.3 us (40%)
  Pallas kernels  14.6 us (33%)
  waiting for transfers between devices  9.32 us (21%)
  local copies, waits for them, and re-layouts  1 us (2%)
  between operations  0.86 us (2%)
    ppermute x14, starting transfers between devices, swapped(): return lax.ppermute(value, axis, [(dst ^ mask, dst) for dst in range(size)])  17.3 us
    ppermute x14, waiting for transfers between devices, swapped(): return lax.ppermute(value, axis, [(dst ^ mask, dst) for dst in range(size)])  9.32 us
    pallas_call x1, Pallas kernels, per_device(): call(solve_selected_kernel, shape(lanes, width), 6 << 30, 2 << 20, 8, scr...  4.15 us
    pallas_call x2, Pallas kernels, per_device(): call(kernel, shape(width, TILE), 2 << 30, 2 << 20, 8, in_specs=[ANY, VMEM...  3.59 us
    pallas_call x1, Pallas kernels, per_device(): call(functools.partial(finish_kernel, inner, outer, share, parts), shape(...  2.77 us
    pallas_call x1, Pallas kernels, per_device(): call(functools.partial(product_kernel, row_size, paired), outs, 1 << 30,...  2.34 us
    pallas_call x1, Pallas kernels, per_device(): call(functools.partial(solve_u_kernel, inner, outer, share), (shape(rhs,...  1.09 us
    unnamed x18, local copies, waits for them, and re-layouts  0.95 us
  transfers between devices with their start and end apart: 14, of which 6 were waited for; matrix products, arithmetic and copies ran while one was open for 0% of the time, Pallas kernels for 32%

profile of v4, /device:TPU:0, one launch (start us, length us, event | category | flops | bytes accessed | tf_op | source)
XLA Modules:
  0.0 43.2 jit_solution(18204609909439441538)
XLA Ops:
  0.6 0.0 copy-start
  0.7 0.9 %copy-done = f32[64,512]{1,0:T(8,128)S(1)} copy-done((f32[64,512]{1,0:T(8,128)S(1)}, f32[64,512]{1,0:T(8,128)}, u32[]{:S(2)}) %copy-start) | copy-done | bytes 131096
  1.5 3.0 %collective-permute-start = (f32[64,128]{1,0:T(8,128)S(1)}, f32[64,128]{1,0:T(8,128)S(1)}, u32[]{:S(2)}, u32[]{:S(2)}) collective-permute-start(f32[64,128]{1,0:T(8,128)S(1)} %constant_dynamic-slice_fusion), channel_id=1, source_target_pairs={{2,0},{3,1},{0,2},{1,3},{6,4},{7,5},{4,6},{5,7},{10,8},{11,9},{8,1... | collective-permute-start | bytes 98312 | tf_op jit(solution)/shard_map/ppermute | solution.py:278
  4.6 0.0 copy-start.1
  4.6 0.0 copy-start.2
  4.6 0.0 copy-start.5
  4.6 4.2 %shard_map.95.at_ref.at_any = f32[128,512]{1,0:T(8,128)S(1)} custom-call(s32[1,128]{1,0:T(1,128)} %bitcast.3, f32[512,512]{1,0:T(8,128)} %lp_hbm.1), custom_call_target="tpu_custom_call" | custom-call | flops 6442450944 | bytes 2097152 | tf_op jit(solution)/shard_map/pallas_call | solution.py:318
  8.7 0.0 copy-start.3
  8.7 0.0 collective-permute-done
  8.8 2.7 %collective-permute-start.1 = (f32[128,128]{1,0:T(8,128)S(1)}, f32[128,128]{1,0:T(8,128)S(1)}, u32[]{:S(2)}, u32[]{:S(2)}) collective-permute-start(f32[128,128]{1,0:T(8,128)S(1)} %pad_maximum_fusion.2.after_ref), channel_id=1, source_target_pairs={{4,0},{5,1},{6,2},{7,3},{0,4},{1,5},{2,6},{3,7},{12,8},{13,9},{14,... | collective-permute-start | bytes 196616 | tf_op jit(solution)/shard_map/ppermute | solution.py:278
  11.4 0.0 copy-done.1
  11.4 0.0 copy-done.2
  11.4 0.0 copy-done.5
  11.4 0.0 copy-start.4
  11.5 2.3 %shard_map.96 = (f32[192,256]{1,0:T(8,128)S(1)}, f32[192,256]{1,0:T(8,128)S(1)}) custom-call(s32[1,1]{1,0:T(1,128)} %bitcast.row_ref, f32[128,512]{1,0:T(8,128)S(1)} %shard_map.95.at_ref.at_any, f32[128,128]{1,0:T(8,128)S(1)} %pad_maximum_fusion.2.after_ref, f32[64,512]{1,0:T(8,128)S(1)} %copy-done.5, f32[64,4096]{1,0:T(8,128)S(1)} %copy-done.2, ...), custom_call_target="tpu_custom_call" | custom-call | flops 1073741824 | bytes 10485760 | tf_op jit(solution)/shard_map/pallas_call | solution.py:337
  13.8 0.7 %collective-permute-done.1 = f32[128,128]{1,0:T(8,128)S(1)} collective-permute-done((f32[128,128]{1,0:T(8,128)S(1)}, f32[128,128]{1,0:T(8,128)S(1)}, u32[]{:S(2)}, u32[]{:S(2)}) %collective-permute-start.1) | collective-permute-done | bytes 65568 | tf_op jit(solution)/shard_map/ppermute | solution.py:278
  14.5 0.1 collective-permute-start.2
  14.6 1.4 %collective-permute-done.2 = f32[192,256]{1,0:T(8,128)S(1)} collective-permute-done((f32[192,256]{1,0:T(8,128)S(1)}, f32[192,256]{1,0:T(8,128)S(1)}, u32[]{:S(2)}, u32[]{:S(2)}) %collective-permute-start.2) | collective-permute-done | bytes 196640 | tf_op jit(solution)/shard_map/ppermute | solution.py:278
  16.1 0.0 copy-start.6
  16.1 1.6 %collective-permute-start.3 = (f32[192,128]{1,0:T(8,128)S(1)}, f32[192,128]{1,0:T(8,128)S(1)}, u32[]{:S(2)}, u32[]{:S(2)}) collective-permute-start(f32[192,128]{1,0:T(8,128)S(1)} %slice.13), channel_id=1, source_target_pairs={{16,0},{24,8},{0,16},{8,24},{17,1},{25,9},{1,17},{9,25},{18,2},{26... | collective-permute-start | bytes 294920 | tf_op jit(solution)/shard_map/ppermute | solution.py:278
  17.7 1.5 %collective-permute-start.4 = (f32[256,128]{1,0:T(8,128)S(1)}, f32[256,128]{1,0:T(8,128)S(1)}, u32[]{:S(2)}, u32[]{:S(2)}) collective-permute-start(f32[256,128]{1,0:T(8,128)S(1)} %pad_maximum_fusion.1), channel_id=1, source_target_pairs={{1,0},{0,1},{3,2},{2,3},{5,4},{4,5},{7,6},{6,7},{9,8},{8,9},{11,10... | collective-permute-start | bytes 393224 | tf_op jit(solution)/shard_map/ppermute | solution.py:278
  19.2 0.0 copy-done.3
  19.3 1.9 %shard_map.97.du_any = f32[512,128]{1,0:T(8,128)S(1)} custom-call(f32[192,256]{1,0:T(8,128)S(1)} %add.10.after_ref, f32[512,512]{1,0:T(8,128)S(1)} %copy-done.3), custom_call_target="tpu_custom_call" | custom-call | flops 2147483648 | bytes 2097152 | tf_op jit(solution)/shard_map/pallas_call | solution.py:333
  21.2 0.0 collective-permute-done.3
  21.2 1.8 %collective-permute-done.4 = f32[256,128]{1,0:T(8,128)S(1)} collective-permute-done((f32[256,128]{1,0:T(8,128)S(1)}, f32[256,128]{1,0:T(8,128)S(1)}, u32[]{:S(2)}, u32[]{:S(2)}) %collective-permute-start.4) | collective-permute-done | bytes 131104 | tf_op jit(solution)/shard_map/ppermute | solution.py:278
  23.0 0.1 collective-permute-start.5
  23.1 2.7 %collective-permute-start.6 = (f32[64,128]{1,0:T(8,128)S(1)}, f32[64,128]{1,0:T(8,128)S(1)}, u32[]{:S(2)}, u32[]{:S(2)}) collective-permute-start(f32[64,128]{1,0:T(8,128)S(1)} %slice.16), channel_id=1, source_target_pairs={{4,0},{5,1},{6,2},{7,3},{0,4},{1,5},{2,6},{3,7},{12,8},{13,9},{14,... | collective-permute-start | bytes 98312 | tf_op jit(solution)/shard_map/ppermute | solution.py:278
  25.8 1.6 %collective-permute-start.7 = (f32[64,128]{1,0:T(8,128)S(1)}, f32[64,128]{1,0:T(8,128)S(1)}, u32[]{:S(2)}, u32[]{:S(2)}) collective-permute-start(f32[64,128]{1,0:T(8,128)S(1)} %slice.16), channel_id=1, source_target_pairs={{6,0},{7,1},{4,2},{5,3},{2,4},{3,5},{0,6},{1,7},{14,8},{15,9},{12,... | collective-permute-start | bytes 98312 | tf_op jit(solution)/shard_map/ppermute | solution.py:278
  27.5 0.5 %collective-permute-start.9 = (f32[512,128]{1,0:T(8,128)S(1)}, f32[512,128]{1,0:T(8,128)S(1)}, u32[]{:S(2)}, u32[]{:S(2)}) collective-permute-start(f32[512,128]{1,0:T(8,128)S(1)} %pad_maximum_fusion), channel_id=1, source_target_pairs={{16,0},{24,8},{0,16},{8,24},{17,1},{25,9},{1,17},{9,25},{18,2},{26... | collective-permute-start | bytes 786440 | tf_op jit(solution)/shard_map/ppermute | solution.py:278
  27.9 0.0 collective-permute-done.5
  28.0 0.3 collective-permute-done.6
  28.3 3.3 %collective-permute-done.7 = f32[64,128]{1,0:T(8,128)S(1)} collective-permute-done((f32[64,128]{1,0:T(8,128)S(1)}, f32[64,128]{1,0:T(8,128)S(1)}, u32[]{:S(2)}, u32[]{:S(2)}) %collective-permute-start.7) | collective-permute-done | bytes 32800 | tf_op jit(solution)/shard_map/ppermute | solution.py:278
  31.6 1.5 %collective-permute-start.8 = (f32[256,128]{1,0:T(8,128)S(1)}, f32[256,128]{1,0:T(8,128)S(1)}, u32[]{:S(2)}, u32[]{:S(2)}) collective-permute-start(f32[256,128]{1,0:T(8,128)S(1)} %constant_dynamic-update-slice_fusion.after_ref.refs_0_), channel_id=1, source_target_pairs={{1,0},{0,1},{3,2},{2,3},{5,4},{4,5},{7,6},{6,7},{9,8},{8,9},{11,10... | collective-permute-start | bytes 393224 | tf_op jit(solution)/shard_map/ppermute | solution.py:278
  33.1 0.0 copy-done.4
  33.1 1.7 %shard_map.98.after_ref.dl_any = f32[512,128]{1,0:T(8,128)S(1)} custom-call(f32[256,128]{1,0:T(8,128)S(1)} %constant_dynamic-update-slice_fusion.after_ref.refs_0_, f32[512,512]{1,0:T(8,128)S(1)} %copy-done.4), custom_call_target="tpu_custom_call" | custom-call | flops 2147483648 | bytes 2097152 | tf_op jit(solution)/shard_map/pallas_call | solution.py:333
  34.8 1.8 %collective-permute-done.8.refs_1_ = f32[256,128]{1,0:T(8,128)S(1)} collective-permute-done((f32[256,128]{1,0:T(8,128)S(1)}, f32[256,128]{1,0:T(8,128)S(1)}, u32[]{:S(2)}, u32[]{:S(2)}) %collective-permute-start.8) | collective-permute-done | bytes 131104 | tf_op jit(solution)/shard_map/ppermute | solution.py:278
  36.5 1.1 %shard_map.99 = (f32[128,512]{1,0:T(8,128)S(1)}, f32[64,128]{1,0:T(8,128)S(1)}) custom-call(s32[1,1]{1,0:T(1,128)} %bitcast.1.col_ref, f32[512,128]{1,0:T(8,128)S(1)} %shard_map.98.after_ref.dl_any, f32[512,512]{1,0:T(8,128)S(1)} %copy-done.3, f32[512,128]{1,0:T(8,128)S(1)} %shard_map.97.du_any, ...), custom_call_target="tpu_custom_call" | custom-call | flops 209715200 | bytes 2097152 | tf_op jit(solution)/shard_map/pallas_call | solution.py:374
  37.6 0.0 collective-permute-done.9
  37.7 0.1 collective-permute-start.10
  37.8 0.5 %collective-permute-start.11 = (f32[64,128]{1,0:T(8,128)S(1)}, f32[64,128]{1,0:T(8,128)S(1)}, u32[]{:S(2)}, u32[]{:S(2)}) collective-permute-start(f32[64,128]{1,0:T(8,128)S(1)} %get-tuple-element.31.refs_0_), channel_id=1, source_target_pairs={{8,0},{0,8},{24,16},{16,24},{9,1},{1,9},{25,17},{17,25},{10,2},{2,... | collective-permute-start | bytes 98312 | tf_op jit(solution)/shard_map/ppermute | solution.py:278
  38.3 0.5 %collective-permute-start.12 = (f32[64,128]{1,0:T(8,128)S(1)}, f32[64,128]{1,0:T(8,128)S(1)}, u32[]{:S(2)}, u32[]{:S(2)}) collective-permute-start(f32[64,128]{1,0:T(8,128)S(1)} %get-tuple-element.31.refs_0_), channel_id=1, source_target_pairs={{16,0},{24,8},{0,16},{8,24},{17,1},{25,9},{1,17},{9,25},{18,2},{26... | collective-permute-start | bytes 98312 | tf_op jit(solution)/shard_map/ppermute | solution.py:278
  38.8 0.9 %collective-permute-start.13 = (f32[64,128]{1,0:T(8,128)S(1)}, f32[64,128]{1,0:T(8,128)S(1)}, u32[]{:S(2)}, u32[]{:S(2)}) collective-permute-start(f32[64,128]{1,0:T(8,128)S(1)} %get-tuple-element.31.refs_0_), channel_id=1, source_target_pairs={{24,0},{16,8},{8,16},{0,24},{25,1},{17,9},{9,17},{1,25},{26,2},{18... | collective-permute-start | bytes 98312 | tf_op jit(solution)/shard_map/ppermute | solution.py:278
  39.7 0.0 collective-permute-done.10.refs_1_
  39.7 0.0 copy-done.6
  39.7 2.8 %shard_map.100.after_ref = f32[128,128]{1,0:T(8,128)} custom-call(s32[1,1]{1,0:T(1,128)} %bitcast.1.col_ref, s32[1,1]{1,0:T(1,128)} %bitcast.row_ref, f32[128,512]{1,0:T(8,128)S(1)} %get-tuple-element.28.yt_ref, f32[512,512]{1,0:T(8,128)S(1)} %copy-done.4, f32[512,128]{1,0:T(8,128)S(1)} %shard_map.98.after_ref.dl_any, ...), custom_call_target="tpu_custom_call" | custom-call | flops 419430400 | bytes 4194304 | tf_op jit(solution)/shard_map/pallas_call | solution.py:388
  42.5 0.0 collective-permute-done.11.refs_1_
  42.5 0.0 collective-permute-done.12.refs_2_
  42.5 0.0 collective-permute-done.13.refs_3_
  42.5 0.7 %shard_map.101 = f32[64,512]{1,0:T(8,128)} custom-call(s32[1,1]{1,0:T(1,128)} %bitcast.row_ref, f32[128,128]{1,0:T(8,128)} %shard_map.100.after_ref, f32[64,128]{1,0:T(8,128)S(1)} %get-tuple-element.31.refs_0_, f32[64,128]{1,0:T(8,128)S(1)} %collective-permute-done.11.refs_1_, f32[64,128]{1,0:T(8,128)S(1)} %collective-permute-done.12.refs_2_, ...), custom_call_target="tpu_custom_call" | custom-call | bytes 131072 | tf_op jit(solution)/shard_map/pallas_call | solution.py:407
  (15 shorter events, 0.2 us)
Async XLA Ops:
  0.6 0.9 %copy-start = (f32[64,512]{1,0:T(8,128)S(1)}, f32[64,512]{1,0:T(8,128)}, u32[]{:S(2)}) copy-start(f32[64,512]{1,0:T(8,128)} %param.13) | copy-start | bytes 393220
  1.5 7.2 %collective-permute-start = (f32[64,128]{1,0:T(8,128)S(1)}, f32[64,128]{1,0:T(8,128)S(1)}, u32[]{:S(2)}, u32[]{:S(2)}) collective-permute-start(f32[64,128]{1,0:T(8,128)S(1)} %constant_dynamic-slice_fusion), channel_id=1, source_target_pairs={{2,0},{3,1},{0,2},{1,3},{6,4},{7,5},{4,6},{5,7},{10,8},{11,9},{8,1... | collective-permute-start | bytes 98312 | tf_op jit(solution)/shard_map/ppermute | solution.py:278
  4.6 6.9 %copy-start.1 = (f32[4096,512]{1,0:T(8,128)S(1)}, f32[4096,512]{1,0:T(8,128)}, u32[]{:S(2)}) copy-start(f32[4096,512]{1,0:T(8,128)} %y_ref.1) | copy-start | bytes 25165828
  4.6 6.9 %copy-start.2 = (f32[64,4096]{1,0:T(8,128)S(1)}, f32[64,4096]{1,0:T(8,128)}, u32[]{:S(2)}) copy-start(f32[64,4096]{1,0:T(8,128)} %u_cols_ref.1) | copy-start | bytes 3145732
  4.6 6.9 %copy-start.5 = (f32[64,512]{1,0:T(8,128)S(1)}, f32[64,512]{1,0:T(8,128)}, u32[]{:S(2)}) copy-start(f32[64,512]{1,0:T(8,128)} %b_ref.1) | copy-start | bytes 393220
  8.7 10.5 %copy-start.3 = (f32[512,512]{1,0:T(8,128)S(1)}, f32[512,512]{1,0:T(8,128)}, u32[]{:S(2)}) copy-start(f32[512,512]{1,0:T(8,128)} %u_ref.3) | copy-start | bytes 3145732
  8.8 5.8 %collective-permute-start.1 = (f32[128,128]{1,0:T(8,128)S(1)}, f32[128,128]{1,0:T(8,128)S(1)}, u32[]{:S(2)}, u32[]{:S(2)}) collective-permute-start(f32[128,128]{1,0:T(8,128)S(1)} %pad_maximum_fusion.2.after_ref), channel_id=1, source_target_pairs={{4,0},{5,1},{6,2},{7,3},{0,4},{1,5},{2,6},{3,7},{12,8},{13,9},{14,... | collective-permute-start | bytes 196616 | tf_op jit(solution)/shard_map/ppermute | solution.py:278
  11.4 21.6 %copy-start.4 = (f32[512,512]{1,0:T(8,128)S(1)}, f32[512,512]{1,0:T(8,128)}, u32[]{:S(2)}) copy-start(f32[512,512]{1,0:T(8,128)} %l_ref.3) | copy-start | bytes 3145732
  14.5 1.5 %collective-permute-start.2 = (f32[192,256]{1,0:T(8,128)S(1)}, f32[192,256]{1,0:T(8,128)S(1)}, u32[]{:S(2)}, u32[]{:S(2)}) collective-permute-start(f32[192,256]{1,0:T(8,128)S(1)} %get-tuple-element.20), channel_id=1, source_target_pairs={{8,0},{0,8},{24,16},{16,24},{9,1},{1,9},{25,17},{17,25},{10,2},{2,... | collective-permute-start | bytes 589832 | tf_op jit(solution)/shard_map/ppermute | solution.py:278
  16.1 23.6 %copy-start.6 = (s32[128]{0:T(128)S(1)}, s32[128]{0:T(128)}, u32[]{:S(2)}) copy-start(s32[128]{0:T(128)} %param.15) | copy-start | bytes 1540
  16.1 5.1 %collective-permute-start.3 = (f32[192,128]{1,0:T(8,128)S(1)}, f32[192,128]{1,0:T(8,128)S(1)}, u32[]{:S(2)}, u32[]{:S(2)}) collective-permute-start(f32[192,128]{1,0:T(8,128)S(1)} %slice.13), channel_id=1, source_target_pairs={{16,0},{24,8},{0,16},{8,24},{17,1},{25,9},{1,17},{9,25},{18,2},{26... | collective-permute-start | bytes 294920 | tf_op jit(solution)/shard_map/ppermute | solution.py:278
  17.7 5.3 %collective-permute-start.4 = (f32[256,128]{1,0:T(8,128)S(1)}, f32[256,128]{1,0:T(8,128)S(1)}, u32[]{:S(2)}, u32[]{:S(2)}) collective-permute-start(f32[256,128]{1,0:T(8,128)S(1)} %pad_maximum_fusion.1), channel_id=1, source_target_pairs={{1,0},{0,1},{3,2},{2,3},{5,4},{4,5},{7,6},{6,7},{9,8},{8,9},{11,10... | collective-permute-start | bytes 393224 | tf_op jit(solution)/shard_map/ppermute | solution.py:278
  23.0 4.9 %collective-permute-start.5 = (f32[64,128]{1,0:T(8,128)S(1)}, f32[64,128]{1,0:T(8,128)S(1)}, u32[]{:S(2)}, u32[]{:S(2)}) collective-permute-start(f32[64,128]{1,0:T(8,128)S(1)} %slice.16), channel_id=1, source_target_pairs={{2,0},{3,1},{0,2},{1,3},{6,4},{7,5},{4,6},{5,7},{10,8},{11,9},{8,1... | collective-permute-start | bytes 98312 | tf_op jit(solution)/shard_map/ppermute | solution.py:278
  23.1 5.2 %collective-permute-start.6 = (f32[64,128]{1,0:T(8,128)S(1)}, f32[64,128]{1,0:T(8,128)S(1)}, u32[]{:S(2)}, u32[]{:S(2)}) collective-permute-start(f32[64,128]{1,0:T(8,128)S(1)} %slice.16), channel_id=1, source_target_pairs={{4,0},{5,1},{6,2},{7,3},{0,4},{1,5},{2,6},{3,7},{12,8},{13,9},{14,... | collective-permute-start | bytes 98312 | tf_op jit(solution)/shard_map/ppermute | solution.py:278
  25.8 5.7 %collective-permute-start.7 = (f32[64,128]{1,0:T(8,128)S(1)}, f32[64,128]{1,0:T(8,128)S(1)}, u32[]{:S(2)}, u32[]{:S(2)}) collective-permute-start(f32[64,128]{1,0:T(8,128)S(1)} %slice.16), channel_id=1, source_target_pairs={{6,0},{7,1},{4,2},{5,3},{2,4},{3,5},{0,6},{1,7},{14,8},{15,9},{12,... | collective-permute-start | bytes 98312 | tf_op jit(solution)/shard_map/ppermute | solution.py:278
  27.5 10.1 %collective-permute-start.9 = (f32[512,128]{1,0:T(8,128)S(1)}, f32[512,128]{1,0:T(8,128)S(1)}, u32[]{:S(2)}, u32[]{:S(2)}) collective-permute-start(f32[512,128]{1,0:T(8,128)S(1)} %pad_maximum_fusion), channel_id=1, source_target_pairs={{16,0},{24,8},{0,16},{8,24},{17,1},{25,9},{1,17},{9,25},{18,2},{26... | collective-permute-start | bytes 786440 | tf_op jit(solution)/shard_map/ppermute | solution.py:278
  31.6 5.0 %collective-permute-start.8 = (f32[256,128]{1,0:T(8,128)S(1)}, f32[256,128]{1,0:T(8,128)S(1)}, u32[]{:S(2)}, u32[]{:S(2)}) collective-permute-start(f32[256,128]{1,0:T(8,128)S(1)} %constant_dynamic-update-slice_fusion.after_ref.refs_0_), channel_id=1, source_target_pairs={{1,0},{0,1},{3,2},{2,3},{5,4},{4,5},{7,6},{6,7},{9,8},{8,9},{11,10... | collective-permute-start | bytes 393224 | tf_op jit(solution)/shard_map/ppermute | solution.py:278
  37.7 2.0 %collective-permute-start.10 = (f32[512,256]{1,0:T(8,128)S(1)}, f32[512,256]{1,0:T(8,128)S(1)}, u32[]{:S(2)}, u32[]{:S(2)}) collective-permute-start(f32[512,256]{1,0:T(8,128)S(1)} %constant_dynamic-update-slice_fusion.4.refs_0_), channel_id=1, source_target_pairs={{8,0},{0,8},{24,16},{16,24},{9,1},{1,9},{25,17},{17,25},{10,2},{2,... | collective-permute-start | bytes 1572872 | tf_op jit(solution)/shard_map/ppermute | solution.py:278
  37.8 4.7 %collective-permute-start.11 = (f32[64,128]{1,0:T(8,128)S(1)}, f32[64,128]{1,0:T(8,128)S(1)}, u32[]{:S(2)}, u32[]{:S(2)}) collective-permute-start(f32[64,128]{1,0:T(8,128)S(1)} %get-tuple-element.31.refs_0_), channel_id=1, source_target_pairs={{8,0},{0,8},{24,16},{16,24},{9,1},{1,9},{25,17},{17,25},{10,2},{2,... | collective-permute-start | bytes 98312 | tf_op jit(solution)/shard_map/ppermute | solution.py:278
  38.3 4.2 %collective-permute-start.12 = (f32[64,128]{1,0:T(8,128)S(1)}, f32[64,128]{1,0:T(8,128)S(1)}, u32[]{:S(2)}, u32[]{:S(2)}) collective-permute-start(f32[64,128]{1,0:T(8,128)S(1)} %get-tuple-element.31.refs_0_), channel_id=1, source_target_pairs={{16,0},{24,8},{0,16},{8,24},{17,1},{25,9},{1,17},{9,25},{18,2},{26... | collective-permute-start | bytes 98312 | tf_op jit(solution)/shard_map/ppermute | solution.py:278
  38.8 3.7 %collective-permute-start.13 = (f32[64,128]{1,0:T(8,128)S(1)}, f32[64,128]{1,0:T(8,128)S(1)}, u32[]{:S(2)}, u32[]{:S(2)}) collective-permute-start(f32[64,128]{1,0:T(8,128)S(1)} %get-tuple-element.31.refs_0_), channel_id=1, source_target_pairs={{24,0},{16,8},{8,16},{0,24},{25,1},{17,9},{9,17},{1,25},{26,2},{18... | collective-permute-start | bytes 98312 | tf_op jit(solution)/shard_map/ppermute | solution.py:278

commit v5 on v4

--- a/solution.py
+++ b/solution.py
@@ -363,7 +363,7 @@
     rhs = max(TILE, column_share)
     mine = jnp.concatenate(gather_pieces(line, "col", col_size, inner), axis=0)
     du = inverses(invert_upper_kernel, keep if paired else payload[0], u_diag)
-    resid, mine, du = lax.optimization_barrier((resid, mine, du))
+    resid, du = lax.optimization_barrier((resid, du))
     resid = jnp.pad(resid, ((0, 0), (0, rhs - column_share)))
     v = jnp.pad(own[share:], ((0, 0), (0, rhs - column_share)))
     sides = [mine] + [swapped(mine, "row", row_size, 2 * step) for step in range(1, chips if parts > 1 else 1)]

time: 43.6 us -> 42.3 us (0.970)
  waiting for transfers between devices: 9.32 us -> 7.53 us
  starting transfers between devices: 17.3 us -> 18.1 us
    ppermute x14, waiting for transfers between devices: 9.32 us -> 7.53 us  [swapped(): return lax.ppermute(value, axis, [(dst ^ mask, dst) for dst in range(size)])]
    ppermute x14, starting transfers between devices: 17.3 us -> 18.1 us  [swapped(): return lax.ppermute(value, axis, [(dst ^ mask, dst) for dst in range(size)])]
    unnamed x18 -> x19, local copies, waits for them, and re-layouts: 0.95 us -> 0.96 us
  transfers between devices with their start and end apart: 14 -> 14, of which waited for: 6 -> 5; matrix products, arithmetic and copies ran while one was open for 0% -> 0% of each run, Pallas kernels for 32% -> 33%
where the time goes in v5:
time: 42.3 us; the launch traced here: 42.2 us
  starting transfers between devices  18.1 us (43%)
  Pallas kernels  14.6 us (35%)
  waiting for transfers between devices  7.53 us (18%)
  local copies, waits for them, and re-layouts  1.02 us (2%)
  between operations  0.87 us (2%)
    ppermute x14, starting transfers between devices, swapped(): return lax.ppermute(value, axis, [(dst ^ mask, dst) for dst in range(size)])  18.1 us
    ppermute x14, waiting for transfers between devices, swapped(): return lax.ppermute(value, axis, [(dst ^ mask, dst) for dst in range(size)])  7.53 us
    pallas_call x1, Pallas kernels, per_device(): call(solve_selected_kernel, shape(lanes, width), 6 << 30, 2 << 20, 8, scr...  4.15 us
    pallas_call x2, Pallas kernels, per_device(): call(kernel, shape(width, TILE), 2 << 30, 2 << 20, 8, in_specs=[ANY, VMEM...  3.59 us
    pallas_call x1, Pallas kernels, per_device(): call(functools.partial(finish_kernel, inner, outer, share, parts), shape(...  2.77 us
    pallas_call x1, Pallas kernels, per_device(): call(functools.partial(product_kernel, row_size, paired), outs, 1 << 30,...  2.34 us
    pallas_call x1, Pallas kernels, per_device(): call(functools.partial(solve_u_kernel, inner, outer, share), (shape(rhs,...  1.09 us
    unnamed x19, local copies, waits for them, and re-layouts  0.96 us
  transfers between devices with their start and end apart: 14, of which 5 were waited for; matrix products, arithmetic and copies ran while one was open for 0% of the time, Pallas kernels for 33%

profile of v5, /device:TPU:0, one launch (start us, length us, event | category | flops | bytes accessed | tf_op | source)
XLA Modules:
  0.0 42.2 jit_solution(4894768218172896137)
XLA Ops:
  0.6 0.0 copy-start
  0.7 0.9 %copy-done = f32[64,512]{1,0:T(8,128)S(1)} copy-done((f32[64,512]{1,0:T(8,128)S(1)}, f32[64,512]{1,0:T(8,128)}, u32[]{:S(2)}) %copy-start) | copy-done | bytes 131096
  1.5 3.0 %collective-permute-start = (f32[64,128]{1,0:T(8,128)S(1)}, f32[64,128]{1,0:T(8,128)S(1)}, u32[]{:S(2)}, u32[]{:S(2)}) collective-permute-start(f32[64,128]{1,0:T(8,128)S(1)} %constant_dynamic-slice_fusion), channel_id=1, source_target_pairs={{2,0},{3,1},{0,2},{1,3},{6,4},{7,5},{4,6},{5,7},{10,8},{11,9},{8,1... | collective-permute-start | bytes 98312 | tf_op jit(solution)/shard_map/ppermute | solution.py:278
  4.6 0.0 copy-start.1
  4.6 0.0 copy-start.2
  4.6 0.0 copy-start.5
  4.6 4.2 %shard_map.95.at_ref.at_any = f32[128,512]{1,0:T(8,128)S(1)} custom-call(s32[1,128]{1,0:T(1,128)} %bitcast.3, f32[512,512]{1,0:T(8,128)} %lp_hbm.1), custom_call_target="tpu_custom_call" | custom-call | flops 6442450944 | bytes 2097152 | tf_op jit(solution)/shard_map/pallas_call | solution.py:318
  8.7 0.0 copy-start.3
  8.7 0.0 collective-permute-done
  8.8 2.7 %collective-permute-start.1 = (f32[128,128]{1,0:T(8,128)S(1)}, f32[128,128]{1,0:T(8,128)S(1)}, u32[]{:S(2)}, u32[]{:S(2)}) collective-permute-start(f32[128,128]{1,0:T(8,128)S(1)} %pad_maximum_fusion.1.after_ref), channel_id=1, source_target_pairs={{4,0},{5,1},{6,2},{7,3},{0,4},{1,5},{2,6},{3,7},{12,8},{13,9},{14,... | collective-permute-start | bytes 196616 | tf_op jit(solution)/shard_map/ppermute | solution.py:278
  11.4 0.0 copy-done.1
  11.4 0.0 copy-done.2
  11.4 0.0 copy-done.5
  11.4 0.0 copy-start.4
  11.5 2.3 %shard_map.96 = (f32[192,256]{1,0:T(8,128)S(1)}, f32[192,256]{1,0:T(8,128)S(1)}) custom-call(s32[1,1]{1,0:T(1,128)} %bitcast.row_ref, f32[128,512]{1,0:T(8,128)S(1)} %shard_map.95.at_ref.at_any, f32[128,128]{1,0:T(8,128)S(1)} %pad_maximum_fusion.1.after_ref, f32[64,512]{1,0:T(8,128)S(1)} %copy-done.5, f32[64,4096]{1,0:T(8,128)S(1)} %copy-done.2, ...), custom_call_target="tpu_custom_call" | custom-call | flops 1073741824 | bytes 10485760 | tf_op jit(solution)/shard_map/pallas_call | solution.py:337
  13.8 0.7 %collective-permute-done.1 = f32[128,128]{1,0:T(8,128)S(1)} collective-permute-done((f32[128,128]{1,0:T(8,128)S(1)}, f32[128,128]{1,0:T(8,128)S(1)}, u32[]{:S(2)}, u32[]{:S(2)}) %collective-permute-start.1) | collective-permute-done | bytes 65568 | tf_op jit(solution)/shard_map/ppermute | solution.py:278
  14.5 0.1 collective-permute-start.2
  14.6 1.4 %collective-permute-done.2 = f32[192,256]{1,0:T(8,128)S(1)} collective-permute-done((f32[192,256]{1,0:T(8,128)S(1)}, f32[192,256]{1,0:T(8,128)S(1)}, u32[]{:S(2)}, u32[]{:S(2)}) %collective-permute-start.2) | collective-permute-done | bytes 196640 | tf_op jit(solution)/shard_map/ppermute | solution.py:278
  16.1 0.0 copy-start.6
  16.1 1.6 %collective-permute-start.3 = (f32[192,128]{1,0:T(8,128)S(1)}, f32[192,128]{1,0:T(8,128)S(1)}, u32[]{:S(2)}, u32[]{:S(2)}) collective-permute-start(f32[192,128]{1,0:T(8,128)S(1)} %slice.13), channel_id=1, source_target_pairs={{16,0},{24,8},{0,16},{8,24},{17,1},{25,9},{1,17},{9,25},{18,2},{26... | collective-permute-start | bytes 294920 | tf_op jit(solution)/shard_map/ppermute | solution.py:278
  17.7 0.0 copy-done.3
  17.7 1.9 %shard_map.97.du_any = f32[512,128]{1,0:T(8,128)S(1)} custom-call(f32[192,256]{1,0:T(8,128)S(1)} %add.10.after_ref, f32[512,512]{1,0:T(8,128)S(1)} %copy-done.3), custom_call_target="tpu_custom_call" | custom-call | flops 2147483648 | bytes 2097152 | tf_op jit(solution)/shard_map/pallas_call | solution.py:333
  19.7 1.6 %collective-permute-start.8 = (f32[256,128]{1,0:T(8,128)S(1)}, f32[256,128]{1,0:T(8,128)S(1)}, u32[]{:S(2)}, u32[]{:S(2)}) collective-permute-start(f32[256,128]{1,0:T(8,128)S(1)} %pad_maximum_fusion), channel_id=1, source_target_pairs={{1,0},{0,1},{3,2},{2,3},{5,4},{4,5},{7,6},{6,7},{9,8},{8,9},{11,10... | collective-permute-start | bytes 393224 | tf_op jit(solution)/shard_map/ppermute | solution.py:278
  21.2 0.0 collective-permute-done.3
  21.3 0.1 collective-permute-start.4
  21.4 2.7 %collective-permute-start.5 = (f32[64,128]{1,0:T(8,128)S(1)}, f32[64,128]{1,0:T(8,128)S(1)}, u32[]{:S(2)}, u32[]{:S(2)}) collective-permute-start(f32[64,128]{1,0:T(8,128)S(1)} %slice.16), channel_id=1, source_target_pairs={{4,0},{5,1},{6,2},{7,3},{0,4},{1,5},{2,6},{3,7},{12,8},{13,9},{14,... | collective-permute-start | bytes 98312 | tf_op jit(solution)/shard_map/ppermute | solution.py:278
  24.1 1.6 %collective-permute-start.6 = (f32[64,128]{1,0:T(8,128)S(1)}, f32[64,128]{1,0:T(8,128)S(1)}, u32[]{:S(2)}, u32[]{:S(2)}) collective-permute-start(f32[64,128]{1,0:T(8,128)S(1)} %slice.16), channel_id=1, source_target_pairs={{6,0},{7,1},{4,2},{5,3},{2,4},{3,5},{0,6},{1,7},{14,8},{15,9},{12,... | collective-permute-start | bytes 98312 | tf_op jit(solution)/shard_map/ppermute | solution.py:278
  25.7 0.0 collective-permute-done.8
  25.8 1.4 %collective-permute-start.9 = (f32[512,128]{1,0:T(8,128)S(1)}, f32[512,128]{1,0:T(8,128)S(1)}, u32[]{:S(2)}, u32[]{:S(2)}) collective-permute-start(f32[512,128]{1,0:T(8,128)S(1)} %constant_dynamic-update-slice_fusion.4), channel_id=1, source_target_pairs={{16,0},{24,8},{0,16},{8,24},{17,1},{25,9},{1,17},{9,25},{18,2},{26... | collective-permute-start | bytes 786440 | tf_op jit(solution)/shard_map/ppermute | solution.py:278
  27.1 0.0 collective-permute-done.4
  27.2 0.0 collective-permute-done.5
  27.2 2.7 %collective-permute-done.6 = f32[64,128]{1,0:T(8,128)S(1)} collective-permute-done((f32[64,128]{1,0:T(8,128)S(1)}, f32[64,128]{1,0:T(8,128)S(1)}, u32[]{:S(2)}, u32[]{:S(2)}) %collective-permute-start.6) | collective-permute-done | bytes 32800 | tf_op jit(solution)/shard_map/ppermute | solution.py:278
  29.8 1.3 %collective-permute-start.7 = (f32[256,128]{1,0:T(8,128)S(1)}, f32[256,128]{1,0:T(8,128)S(1)}, u32[]{:S(2)}, u32[]{:S(2)}) collective-permute-start(f32[256,128]{1,0:T(8,128)S(1)} %constant_dynamic-update-slice_fusion.after_ref.refs_0_), channel_id=1, source_target_pairs={{1,0},{0,1},{3,2},{2,3},{5,4},{4,5},{7,6},{6,7},{9,8},{8,9},{11,10... | collective-permute-start | bytes 393224 | tf_op jit(solution)/shard_map/ppermute | solution.py:278
  31.2 0.0 copy-done.4
  31.2 1.7 %shard_map.98.after_ref.dl_any = f32[512,128]{1,0:T(8,128)S(1)} custom-call(f32[256,128]{1,0:T(8,128)S(1)} %constant_dynamic-update-slice_fusion.after_ref.refs_0_, f32[512,512]{1,0:T(8,128)S(1)} %copy-done.4), custom_call_target="tpu_custom_call" | custom-call | flops 2147483648 | bytes 2097152 | tf_op jit(solution)/shard_map/pallas_call | solution.py:333
  32.8 2.0 %collective-permute-done.7.refs_1_ = f32[256,128]{1,0:T(8,128)S(1)} collective-permute-done((f32[256,128]{1,0:T(8,128)S(1)}, f32[256,128]{1,0:T(8,128)S(1)}, u32[]{:S(2)}, u32[]{:S(2)}) %collective-permute-start.7) | collective-permute-done | bytes 131104 | tf_op jit(solution)/shard_map/ppermute | solution.py:278
  34.8 1.1 %shard_map.99 = (f32[128,512]{1,0:T(8,128)S(1)}, f32[64,128]{1,0:T(8,128)S(1)}) custom-call(s32[1,1]{1,0:T(1,128)} %bitcast.1.col_ref, f32[512,128]{1,0:T(8,128)S(1)} %shard_map.98.after_ref.dl_any, f32[512,512]{1,0:T(8,128)S(1)} %copy-done.3, f32[512,128]{1,0:T(8,128)S(1)} %shard_map.97.du_any, ...), custom_call_target="tpu_custom_call" | custom-call | flops 209715200 | bytes 2097152 | tf_op jit(solution)/shard_map/pallas_call | solution.py:374
  35.9 0.0 collective-permute-done.9
  36.0 0.1 collective-permute-start.10
  36.1 0.5 %collective-permute-start.11 = (f32[64,128]{1,0:T(8,128)S(1)}, f32[64,128]{1,0:T(8,128)S(1)}, u32[]{:S(2)}, u32[]{:S(2)}) collective-permute-start(f32[64,128]{1,0:T(8,128)S(1)} %get-tuple-element.29.refs_0_), channel_id=1, source_target_pairs={{8,0},{0,8},{24,16},{16,24},{9,1},{1,9},{25,17},{17,25},{10,2},{2,... | collective-permute-start | bytes 98312 | tf_op jit(solution)/shard_map/ppermute | solution.py:278
  36.5 1.3 %collective-permute-start.12 = (f32[64,128]{1,0:T(8,128)S(1)}, f32[64,128]{1,0:T(8,128)S(1)}, u32[]{:S(2)}, u32[]{:S(2)}) collective-permute-start(f32[64,128]{1,0:T(8,128)S(1)} %get-tuple-element.29.refs_0_), channel_id=1, source_target_pairs={{16,0},{24,8},{0,16},{8,24},{17,1},{25,9},{1,17},{9,25},{18,2},{26... | collective-permute-start | bytes 98312 | tf_op jit(solution)/shard_map/ppermute | solution.py:278
  37.8 0.1 collective-permute-start.13
  38.0 0.0 collective-permute-done.10.refs_1_
  38.0 0.0 copy-done.6
  38.0 2.8 %shard_map.100.after_ref = f32[128,128]{1,0:T(8,128)} custom-call(s32[1,1]{1,0:T(1,128)} %bitcast.1.col_ref, s32[1,1]{1,0:T(1,128)} %bitcast.row_ref, f32[128,512]{1,0:T(8,128)S(1)} %get-tuple-element.26.yt_ref, f32[512,512]{1,0:T(8,128)S(1)} %copy-done.4, f32[512,128]{1,0:T(8,128)S(1)} %shard_map.98.after_ref.dl_any, ...), custom_call_target="tpu_custom_call" | custom-call | flops 419430400 | bytes 4194304 | tf_op jit(solution)/shard_map/pallas_call | solution.py:388
  40.8 0.0 collective-permute-done.11.refs_1_
  40.8 0.0 collective-permute-done.12.refs_2_
  40.8 0.7 %collective-permute-done.13.refs_3_ = f32[64,128]{1,0:T(8,128)S(1)} collective-permute-done((f32[64,128]{1,0:T(8,128)S(1)}, f32[64,128]{1,0:T(8,128)S(1)}, u32[]{:S(2)}, u32[]{:S(2)}) %collective-permute-start.13) | collective-permute-done | bytes 32800 | tf_op jit(solution)/shard_map/ppermute | solution.py:278
  41.5 0.7 %shard_map.101 = f32[64,512]{1,0:T(8,128)} custom-call(s32[1,1]{1,0:T(1,128)} %bitcast.row_ref, f32[128,128]{1,0:T(8,128)} %shard_map.100.after_ref, f32[64,128]{1,0:T(8,128)S(1)} %get-tuple-element.29.refs_0_, f32[64,128]{1,0:T(8,128)S(1)} %collective-permute-done.11.refs_1_, f32[64,128]{1,0:T(8,128)S(1)} %collective-permute-done.12.refs_2_, ...), custom_call_target="tpu_custom_call" | custom-call | bytes 131072 | tf_op jit(solution)/shard_map/pallas_call | solution.py:407
  (16 shorter events, 0.2 us)
Async XLA Ops:
  0.6 0.9 %copy-start = (f32[64,512]{1,0:T(8,128)S(1)}, f32[64,512]{1,0:T(8,128)}, u32[]{:S(2)}) copy-start(f32[64,512]{1,0:T(8,128)} %param.13) | copy-start | bytes 393220
  1.5 7.2 %collective-permute-start = (f32[64,128]{1,0:T(8,128)S(1)}, f32[64,128]{1,0:T(8,128)S(1)}, u32[]{:S(2)}, u32[]{:S(2)}) collective-permute-start(f32[64,128]{1,0:T(8,128)S(1)} %constant_dynamic-slice_fusion), channel_id=1, source_target_pairs={{2,0},{3,1},{0,2},{1,3},{6,4},{7,5},{4,6},{5,7},{10,8},{11,9},{8,1... | collective-permute-start | bytes 98312 | tf_op jit(solution)/shard_map/ppermute | solution.py:278
  4.6 6.9 %copy-start.1 = (f32[4096,512]{1,0:T(8,128)S(1)}, f32[4096,512]{1,0:T(8,128)}, u32[]{:S(2)}) copy-start(f32[4096,512]{1,0:T(8,128)} %y_ref.1) | copy-start | bytes 25165828
  4.6 6.9 %copy-start.2 = (f32[64,4096]{1,0:T(8,128)S(1)}, f32[64,4096]{1,0:T(8,128)}, u32[]{:S(2)}) copy-start(f32[64,4096]{1,0:T(8,128)} %u_cols_ref.1) | copy-start | bytes 3145732
  4.6 6.9 %copy-start.5 = (f32[64,512]{1,0:T(8,128)S(1)}, f32[64,512]{1,0:T(8,128)}, u32[]{:S(2)}) copy-start(f32[64,512]{1,0:T(8,128)} %b_ref.1) | copy-start | bytes 393220
  8.7 9.0 %copy-start.3 = (f32[512,512]{1,0:T(8,128)S(1)}, f32[512,512]{1,0:T(8,128)}, u32[]{:S(2)}) copy-start(f32[512,512]{1,0:T(8,128)} %u_ref.3) | copy-start | bytes 3145732
  8.8 5.8 %collective-permute-start.1 = (f32[128,128]{1,0:T(8,128)S(1)}, f32[128,128]{1,0:T(8,128)S(1)}, u32[]{:S(2)}, u32[]{:S(2)}) collective-permute-start(f32[128,128]{1,0:T(8,128)S(1)} %pad_maximum_fusion.1.after_ref), channel_id=1, source_target_pairs={{4,0},{5,1},{6,2},{7,3},{0,4},{1,5},{2,6},{3,7},{12,8},{13,9},{14,... | collective-permute-start | bytes 196616 | tf_op jit(solution)/shard_map/ppermute | solution.py:278
  11.4 19.7 %copy-start.4 = (f32[512,512]{1,0:T(8,128)S(1)}, f32[512,512]{1,0:T(8,128)}, u32[]{:S(2)}) copy-start(f32[512,512]{1,0:T(8,128)} %l_ref.3) | copy-start | bytes 3145732
  14.5 1.5 %collective-permute-start.2 = (f32[192,256]{1,0:T(8,128)S(1)}, f32[192,256]{1,0:T(8,128)S(1)}, u32[]{:S(2)}, u32[]{:S(2)}) collective-permute-start(f32[192,256]{1,0:T(8,128)S(1)} %get-tuple-element.19), channel_id=1, source_target_pairs={{8,0},{0,8},{24,16},{16,24},{9,1},{1,9},{25,17},{17,25},{10,2},{2,... | collective-permute-start | bytes 589832 | tf_op jit(solution)/shard_map/ppermute | solution.py:278
  16.1 21.9 %copy-start.6 = (s32[128]{0:T(128)S(1)}, s32[128]{0:T(128)}, u32[]{:S(2)}) copy-start(s32[128]{0:T(128)} %param.15) | copy-start | bytes 1540
  16.1 5.1 %collective-permute-start.3 = (f32[192,128]{1,0:T(8,128)S(1)}, f32[192,128]{1,0:T(8,128)S(1)}, u32[]{:S(2)}, u32[]{:S(2)}) collective-permute-start(f32[192,128]{1,0:T(8,128)S(1)} %slice.13), channel_id=1, source_target_pairs={{16,0},{24,8},{0,16},{8,24},{17,1},{25,9},{1,17},{9,25},{18,2},{26... | collective-permute-start | bytes 294920 | tf_op jit(solution)/shard_map/ppermute | solution.py:278
  19.7 6.1 %collective-permute-start.8 = (f32[256,128]{1,0:T(8,128)S(1)}, f32[256,128]{1,0:T(8,128)S(1)}, u32[]{:S(2)}, u32[]{:S(2)}) collective-permute-start(f32[256,128]{1,0:T(8,128)S(1)} %pad_maximum_fusion), channel_id=1, source_target_pairs={{1,0},{0,1},{3,2},{2,3},{5,4},{4,5},{7,6},{6,7},{9,8},{8,9},{11,10... | collective-permute-start | bytes 393224 | tf_op jit(solution)/shard_map/ppermute | solution.py:278
  21.3 5.9 %collective-permute-start.4 = (f32[64,128]{1,0:T(8,128)S(1)}, f32[64,128]{1,0:T(8,128)S(1)}, u32[]{:S(2)}, u32[]{:S(2)}) collective-permute-start(f32[64,128]{1,0:T(8,128)S(1)} %slice.16), channel_id=1, source_target_pairs={{2,0},{3,1},{0,2},{1,3},{6,4},{7,5},{4,6},{5,7},{10,8},{11,9},{8,1... | collective-permute-start | bytes 98312 | tf_op jit(solution)/shard_map/ppermute | solution.py:278
  21.4 5.8 %collective-permute-start.5 = (f32[64,128]{1,0:T(8,128)S(1)}, f32[64,128]{1,0:T(8,128)S(1)}, u32[]{:S(2)}, u32[]{:S(2)}) collective-permute-start(f32[64,128]{1,0:T(8,128)S(1)} %slice.16), channel_id=1, source_target_pairs={{4,0},{5,1},{6,2},{7,3},{0,4},{1,5},{2,6},{3,7},{12,8},{13,9},{14,... | collective-permute-start | bytes 98312 | tf_op jit(solution)/shard_map/ppermute | solution.py:278
  24.1 5.7 %collective-permute-start.6 = (f32[64,128]{1,0:T(8,128)S(1)}, f32[64,128]{1,0:T(8,128)S(1)}, u32[]{:S(2)}, u32[]{:S(2)}) collective-permute-start(f32[64,128]{1,0:T(8,128)S(1)} %slice.16), channel_id=1, source_target_pairs={{6,0},{7,1},{4,2},{5,3},{2,4},{3,5},{0,6},{1,7},{14,8},{15,9},{12,... | collective-permute-start | bytes 98312 | tf_op jit(solution)/shard_map/ppermute | solution.py:278
  25.8 10.1 %collective-permute-start.9 = (f32[512,128]{1,0:T(8,128)S(1)}, f32[512,128]{1,0:T(8,128)S(1)}, u32[]{:S(2)}, u32[]{:S(2)}) collective-permute-start(f32[512,128]{1,0:T(8,128)S(1)} %constant_dynamic-update-slice_fusion.4), channel_id=1, source_target_pairs={{16,0},{24,8},{0,16},{8,24},{17,1},{25,9},{1,17},{9,25},{18,2},{26... | collective-permute-start | bytes 786440 | tf_op jit(solution)/shard_map/ppermute | solution.py:278
  29.8 5.0 %collective-permute-start.7 = (f32[256,128]{1,0:T(8,128)S(1)}, f32[256,128]{1,0:T(8,128)S(1)}, u32[]{:S(2)}, u32[]{:S(2)}) collective-permute-start(f32[256,128]{1,0:T(8,128)S(1)} %constant_dynamic-update-slice_fusion.after_ref.refs_0_), channel_id=1, source_target_pairs={{1,0},{0,1},{3,2},{2,3},{5,4},{4,5},{7,6},{6,7},{9,8},{8,9},{11,10... | collective-permute-start | bytes 393224 | tf_op jit(solution)/shard_map/ppermute | solution.py:278
  36.0 2.0 %collective-permute-start.10 = (f32[512,256]{1,0:T(8,128)S(1)}, f32[512,256]{1,0:T(8,128)S(1)}, u32[]{:S(2)}, u32[]{:S(2)}) collective-permute-start(f32[512,256]{1,0:T(8,128)S(1)} %constant_dynamic-update-slice_fusion.6.refs_0_), channel_id=1, source_target_pairs={{8,0},{0,8},{24,16},{16,24},{9,1},{1,9},{25,17},{17,25},{10,2},{2,... | collective-permute-start | bytes 1572872 | tf_op jit(solution)/shard_map/ppermute | solution.py:278
  36.1 4.7 %collective-permute-start.11 = (f32[64,128]{1,0:T(8,128)S(1)}, f32[64,128]{1,0:T(8,128)S(1)}, u32[]{:S(2)}, u32[]{:S(2)}) collective-permute-start(f32[64,128]{1,0:T(8,128)S(1)} %get-tuple-element.29.refs_0_), channel_id=1, source_target_pairs={{8,0},{0,8},{24,16},{16,24},{9,1},{1,9},{25,17},{17,25},{10,2},{2,... | collective-permute-start | bytes 98312 | tf_op jit(solution)/shard_map/ppermute | solution.py:278
  36.5 4.2 %collective-permute-start.12 = (f32[64,128]{1,0:T(8,128)S(1)}, f32[64,128]{1,0:T(8,128)S(1)}, u32[]{:S(2)}, u32[]{:S(2)}) collective-permute-start(f32[64,128]{1,0:T(8,128)S(1)} %get-tuple-element.29.refs_0_), channel_id=1, source_target_pairs={{16,0},{24,8},{0,16},{8,24},{17,1},{25,9},{1,17},{9,25},{18,2},{26... | collective-permute-start | bytes 98312 | tf_op jit(solution)/shard_map/ppermute | solution.py:278
  37.8 3.7 %collective-permute-start.13 = (f32[64,128]{1,0:T(8,128)S(1)}, f32[64,128]{1,0:T(8,128)S(1)}, u32[]{:S(2)}, u32[]{:S(2)}) collective-permute-start(f32[64,128]{1,0:T(8,128)S(1)} %get-tuple-element.29.refs_0_), channel_id=1, source_target_pairs={{24,0},{16,8},{8,16},{0,24},{25,1},{17,9},{9,17},{1,25},{26,2},{18... | collective-permute-start | bytes 98312 | tf_op jit(solution)/shard_map/ppermute | solution.py:278

commit v6 on v5

--- a/solution.py
+++ b/solution.py
@@ -162,23 +162,20 @@
     return pl.ds(pl.multiple_of(place * size, size), size)
 
 
-def place_piece(col, inner, outer, share, step, piece, full_ref, columns):
+def place_piece(col, inner, outer, share, step, piece, full_ref, columns, down=False):
     low, high = lax.rem(col, inner), lax.div(col, inner)
     for turn in range(outer):
-        at = (high ^ turn) * inner + (low ^ step)
+        at = (high ^ ((outer - turn) % outer if down else turn)) * inner + (low ^ step)
         full_ref[aligned_span(at, share), columns] = piece[turn * share : (turn + 1) * share, :]
 
 
-def solve_u_kernel(inner, outer, share, col_ref, after_ref, u_ref, du_any, *refs):
+def solve_u_kernel(inner, outer, share, col_ref, after_ref, u_ref, du_ref, *refs):
     del after_ref
     piece_refs = refs[:inner]
-    yt_ref, y_ref, full_ref, du_ref, sem = refs[inner:]
-    copy = pltpu.make_async_copy(du_any, du_ref, sem)
-    copy.start()
+    yt_ref, y_ref, full_ref = refs[inner:]
     col = col_ref[0, 0]
     for step, piece_ref in enumerate(piece_refs):
-        place_piece(col, inner, outer, share, step, piece_ref[...], full_ref, slice(None))
-    copy.wait()
+        place_piece(col, inner, outer, share, step, piece_ref[...], full_ref, slice(None), True)
     count = u_ref.shape[0] // TILE
     solved = []
     for i in range(count):
@@ -193,15 +190,9 @@
     y_ref[...] = full_ref[aligned_span(col, share), :]
 
 
-def finish_kernel(inner, outer, share, parts, col_ref, row_ref, yt_ref, l_ref, dl_any, at_any, perm_ref, v_any, *refs):
+def finish_kernel(inner, outer, share, parts, col_ref, row_ref, yt_ref, l_ref, dl_ref, at_ref, perm_ref, v_ref, *refs):
     side_refs = refs[: 1 if parts == 1 else 2]
-    x_ref, lc_ref, dl_ref, at_ref, v_ref, sems = refs[len(side_refs) :]
-    copies = started(
-        [
-            pltpu.make_async_copy(src, dst, sems.at[k])
-            for k, (src, dst) in enumerate([(dl_any, dl_ref), (at_any, at_ref), (v_any, v_ref)])
-        ]
-    )
+    x_ref, lc_ref = refs[len(side_refs) :]
     row, col = row_ref[0, 0], col_ref[0, 0]
     rows = outer * share
     columns = lc_ref.shape[1] // parts
@@ -215,8 +206,6 @@
             for piece in range(inner):
                 value = side_ref[piece * rows : (piece + 1) * rows, step * columns : (step + 1) * columns]
                 place_piece(col, inner, outer, share, piece, value, lc_ref, target)
-    for copy in copies:
-        copy.wait()
     width = l_ref.shape[0]
     count = width // TILE
     perm = perm_ref[...]
@@ -245,7 +234,7 @@
     del after_ref
     out_ref = refs[-1]
     for step, ref in enumerate(refs[:-1]):
-        out_ref[:, aligned_span(row_ref[0, 0] ^ step, ref.shape[1])] = ref[...]
+        out_ref[:, aligned_span(row_ref[0, 0] ^ ((len(refs) - 1 - step) % (len(refs) - 1)), ref.shape[1])] = ref[...]
 
 
 def call(kernel, outs, flops, bytes_accessed, limit, scratch=(), **specs):
@@ -279,7 +268,7 @@
 
 
 def gather_line(value, axis, size, inner):
-    return jnp.concatenate([value] + [swapped(value, axis, size, mask) for mask in range(inner, size, inner)], axis=0)
+    return jnp.concatenate([value] + [swapped(value, axis, size, mask) for mask in range(size - inner, 0, -inner)], axis=0)
 
 
 def gather_pieces(line, axis, size, inner):
@@ -377,8 +366,8 @@
         200 << 20,
         2 << 20,
         8,
-        scratch=[pltpu.VMEM((width, rhs), F32), pltpu.VMEM((width, TILE), F32), pltpu.SemaphoreType.DMA],
-        in_specs=[SMEM, ANY, VMEM, ANY] + [VMEM] * inner,
+        scratch=[pltpu.VMEM((width, rhs), F32)],
+        in_specs=[SMEM, ANY, VMEM, VMEM] + [VMEM] * inner,
         out_specs=[VMEM] * 2,
     )(col_at, dl, u_diag, du, *pieces)
 
@@ -393,17 +382,13 @@
         8,
         scratch=[
             pltpu.VMEM((width, width), F32),
-            pltpu.VMEM((width, TILE), F32),
-            pltpu.VMEM((lanes, width), F32),
-            pltpu.VMEM((lanes, rhs), F32),
-            pltpu.SemaphoreType.DMA((3,)),
         ],
-        in_specs=[SMEM, SMEM, VMEM, VMEM, ANY, ANY, VMEM, ANY] + [VMEM] * len(coupling),
+        in_specs=[SMEM, SMEM] + [VMEM] * 6 + [VMEM] * len(coupling),
         out_specs=VMEM,
     )(col_at, row_at, yt, l_diag, dl, at, perm_row, v, *coupling)
 
     if paired:
-        blocks = [y_mine] + [swapped(y_mine, "row", row_size, step) for step in range(1, row_size)]
+        blocks = [y_mine] + [swapped(y_mine, "row", row_size, step) for step in range(row_size - 1, 0, -1)]
         y_part = call(
             merge_kernel,
             shape(share, columns),

time: 42.3 us -> 40.9 us (0.967)
  waiting for transfers between devices: 7.53 us -> 6.17 us
    ppermute x14, waiting for transfers between devices: 7.53 us -> 6.17 us  [swapped(): return lax.ppermute(value, axis, [(dst ^ mask, dst) for dst in range(size)])]
  transfers between devices with their start and end apart: 14 -> 14, of which waited for: 5 -> 5; matrix products, arithmetic and copies ran while one was open for 0% -> 0% of each run, Pallas kernels for 33% -> 34%
where the time goes in v6:
time: 40.9 us; the launch traced here: 40.8 us
  starting transfers between devices  18.3 us (45%)
  Pallas kernels  14.4 us (35%)
  waiting for transfers between devices  6.17 us (15%)
  local copies, waits for them, and re-layouts  1.02 us (2%)
  between operations  0.83 us (2%)
    ppermute x14, starting transfers between devices, swapped(): return lax.ppermute(value, axis, [(dst ^ mask, dst) for dst in range(size)])  18.3 us
    ppermute x14, waiting for transfers between devices, swapped(): return lax.ppermute(value, axis, [(dst ^ mask, dst) for dst in range(size)])  6.17 us
    pallas_call x1, Pallas kernels, per_device(): call(solve_selected_kernel, shape(lanes, width), 6 << 30, 2 << 20, 8, scr...  4.15 us
    pallas_call x2, Pallas kernels, per_device(): call(kernel, shape(width, TILE), 2 << 30, 2 << 20, 8, in_specs=[ANY, VMEM...  3.58 us
    pallas_call x1, Pallas kernels, per_device(): call(functools.partial(finish_kernel, inner, outer, share, parts), shape(...  2.56 us
    pallas_call x1, Pallas kernels, per_device(): call(functools.partial(product_kernel, row_size, paired), outs, 1 << 30,...  2.34 us
    pallas_call x1, Pallas kernels, per_device(): call(functools.partial(solve_u_kernel, inner, outer, share), (shape(rhs,...  1.05 us
    unnamed x19, local copies, waits for them, and re-layouts  0.96 us
  transfers between devices with their start and end apart: 14, of which 5 were waited for; matrix products, arithmetic and copies ran while one was open for 0% of the time, Pallas kernels for 34%

profile of v6, /device:TPU:0, one launch (start us, length us, event | category | flops | bytes accessed | tf_op | source)
XLA Modules:
  0.0 40.8 jit_solution(14272320015219853542)
XLA Ops:
  0.6 0.0 copy-start
  0.7 0.9 %copy-done = f32[64,512]{1,0:T(8,128)S(1)} copy-done((f32[64,512]{1,0:T(8,128)S(1)}, f32[64,512]{1,0:T(8,128)}, u32[]{:S(2)}) %copy-start) | copy-done | bytes 131096
  1.5 3.0 %collective-permute-start = (f32[64,128]{1,0:T(8,128)S(1)}, f32[64,128]{1,0:T(8,128)S(1)}, u32[]{:S(2)}, u32[]{:S(2)}) collective-permute-start(f32[64,128]{1,0:T(8,128)S(1)} %constant_dynamic-slice_fusion), channel_id=1, source_target_pairs={{2,0},{3,1},{0,2},{1,3},{6,4},{7,5},{4,6},{5,7},{10,8},{11,9},{8,1... | collective-permute-start | bytes 98312 | tf_op jit(solution)/shard_map/ppermute | solution.py:267
  4.6 0.0 copy-start.1
  4.6 0.0 copy-start.2
  4.6 0.0 copy-start.5
  4.6 4.2 %shard_map.95.at_ref = f32[128,512]{1,0:T(8,128)S(1)} custom-call(s32[1,128]{1,0:T(1,128)} %bitcast.3, f32[512,512]{1,0:T(8,128)} %lp_hbm.1), custom_call_target="tpu_custom_call" | custom-call | flops 6442450944 | bytes 2097152 | tf_op jit(solution)/shard_map/pallas_call | solution.py:307
  8.7 0.0 copy-start.3
  8.7 0.0 collective-permute-done
  8.8 2.7 %collective-permute-start.1 = (f32[128,128]{1,0:T(8,128)S(1)}, f32[128,128]{1,0:T(8,128)S(1)}, u32[]{:S(2)}, u32[]{:S(2)}) collective-permute-start(f32[128,128]{1,0:T(8,128)S(1)} %pad_maximum_fusion.1.after_ref), channel_id=1, source_target_pairs={{4,0},{5,1},{6,2},{7,3},{0,4},{1,5},{2,6},{3,7},{12,8},{13,9},{14,... | collective-permute-start | bytes 196616 | tf_op jit(solution)/shard_map/ppermute | solution.py:267
  11.4 0.0 copy-done.1
  11.4 0.0 copy-done.2
  11.4 0.0 copy-done.5
  11.4 0.0 copy-start.4
  11.5 2.3 %shard_map.96 = (f32[192,256]{1,0:T(8,128)S(1)}, f32[192,256]{1,0:T(8,128)S(1)}) custom-call(s32[1,1]{1,0:T(1,128)} %bitcast.row_ref, f32[128,512]{1,0:T(8,128)S(1)} %shard_map.95.at_ref, f32[128,128]{1,0:T(8,128)S(1)} %pad_maximum_fusion.1.after_ref, f32[64,512]{1,0:T(8,128)S(1)} %copy-done.5, f32[64,4096]{1,0:T(8,128)S(1)} %copy-done.2, ...), custom_call_target="tpu_custom_call" | custom-call | flops 1073741824 | bytes 10485760 | tf_op jit(solution)/shard_map/pallas_call | solution.py:326
  13.8 0.7 %collective-permute-done.1 = f32[128,128]{1,0:T(8,128)S(1)} collective-permute-done((f32[128,128]{1,0:T(8,128)S(1)}, f32[128,128]{1,0:T(8,128)S(1)}, u32[]{:S(2)}, u32[]{:S(2)}) %collective-permute-start.1) | collective-permute-done | bytes 65568 | tf_op jit(solution)/shard_map/ppermute | solution.py:267
  14.5 0.1 collective-permute-start.2
  14.6 1.4 %collective-permute-done.2 = f32[192,256]{1,0:T(8,128)S(1)} collective-permute-done((f32[192,256]{1,0:T(8,128)S(1)}, f32[192,256]{1,0:T(8,128)S(1)}, u32[]{:S(2)}, u32[]{:S(2)}) %collective-permute-start.2) | collective-permute-done | bytes 196640 | tf_op jit(solution)/shard_map/ppermute | solution.py:267
  16.1 0.0 copy-start.6
  16.1 1.6 %collective-permute-start.3 = (f32[192,128]{1,0:T(8,128)S(1)}, f32[192,128]{1,0:T(8,128)S(1)}, u32[]{:S(2)}, u32[]{:S(2)}) collective-permute-start(f32[192,128]{1,0:T(8,128)S(1)} %slice.13), channel_id=1, source_target_pairs={{16,0},{24,8},{0,16},{8,24},{17,1},{25,9},{1,17},{9,25},{18,2},{26... | collective-permute-start | bytes 294920 | tf_op jit(solution)/shard_map/ppermute | solution.py:267
  17.7 0.0 copy-done.3
  17.7 1.9 %shard_map.97.du_ref = f32[512,128]{1,0:T(8,128)S(1)} custom-call(f32[192,256]{1,0:T(8,128)S(1)} %add.10.after_ref, f32[512,512]{1,0:T(8,128)S(1)} %copy-done.3), custom_call_target="tpu_custom_call" | custom-call | flops 2147483648 | bytes 2097152 | tf_op jit(solution)/shard_map/pallas_call | solution.py:322
  19.7 1.6 %collective-permute-start.8 = (f32[256,128]{1,0:T(8,128)S(1)}, f32[256,128]{1,0:T(8,128)S(1)}, u32[]{:S(2)}, u32[]{:S(2)}) collective-permute-start(f32[256,128]{1,0:T(8,128)S(1)} %pad_maximum_fusion), channel_id=1, source_target_pairs={{1,0},{0,1},{3,2},{2,3},{5,4},{4,5},{7,6},{6,7},{9,8},{8,9},{11,10... | collective-permute-start | bytes 393224 | tf_op jit(solution)/shard_map/ppermute | solution.py:267
  21.2 0.0 collective-permute-done.3
  21.3 2.3 %collective-permute-start.4 = (f32[64,128]{1,0:T(8,128)S(1)}, f32[64,128]{1,0:T(8,128)S(1)}, u32[]{:S(2)}, u32[]{:S(2)}) collective-permute-start(f32[64,128]{1,0:T(8,128)S(1)} %slice.16), channel_id=1, source_target_pairs={{6,0},{7,1},{4,2},{5,3},{2,4},{3,5},{0,6},{1,7},{14,8},{15,9},{12,... | collective-permute-start | bytes 98312 | tf_op jit(solution)/shard_map/ppermute | solution.py:267
  23.5 0.0 collective-permute-start.5
  23.6 2.2 %collective-permute-start.6 = (f32[64,128]{1,0:T(8,128)S(1)}, f32[64,128]{1,0:T(8,128)S(1)}, u32[]{:S(2)}, u32[]{:S(2)}) collective-permute-start(f32[64,128]{1,0:T(8,128)S(1)} %slice.16), channel_id=1, source_target_pairs={{2,0},{3,1},{0,2},{1,3},{6,4},{7,5},{4,6},{5,7},{10,8},{11,9},{8,1... | collective-permute-start | bytes 98312 | tf_op jit(solution)/shard_map/ppermute | solution.py:267
  25.7 0.0 collective-permute-done.8
  25.8 1.4 %collective-permute-start.9 = (f32[512,128]{1,0:T(8,128)S(1)}, f32[512,128]{1,0:T(8,128)S(1)}, u32[]{:S(2)}, u32[]{:S(2)}) collective-permute-start(f32[512,128]{1,0:T(8,128)S(1)} %constant_dynamic-update-slice_fusion.4), channel_id=1, source_target_pairs={{16,0},{24,8},{0,16},{8,24},{17,1},{25,9},{1,17},{9,25},{18,2},{26... | collective-permute-start | bytes 786440 | tf_op jit(solution)/shard_map/ppermute | solution.py:267
  27.1 0.0 collective-permute-done.4
  27.2 1.4 %collective-permute-done.5 = f32[64,128]{1,0:T(8,128)S(1)} collective-permute-done((f32[64,128]{1,0:T(8,128)S(1)}, f32[64,128]{1,0:T(8,128)S(1)}, u32[]{:S(2)}, u32[]{:S(2)}) %collective-permute-start.5) | collective-permute-done | bytes 32800 | tf_op jit(solution)/shard_map/ppermute | solution.py:267
  28.6 0.0 collective-permute-done.6
  28.6 1.3 %collective-permute-start.7 = (f32[256,128]{1,0:T(8,128)S(1)}, f32[256,128]{1,0:T(8,128)S(1)}, u32[]{:S(2)}, u32[]{:S(2)}) collective-permute-start(f32[256,128]{1,0:T(8,128)S(1)} %constant_dynamic-update-slice_fusion.after_ref.refs_0_), channel_id=1, source_target_pairs={{1,0},{0,1},{3,2},{2,3},{5,4},{4,5},{7,6},{6,7},{9,8},{8,9},{11,10... | collective-permute-start | bytes 393224 | tf_op jit(solution)/shard_map/ppermute | solution.py:267
  29.9 0.0 copy-done.4
  29.9 1.7 %shard_map.98.after_ref.dl_ref = f32[512,128]{1,0:T(8,128)S(1)} custom-call(f32[256,128]{1,0:T(8,128)S(1)} %constant_dynamic-update-slice_fusion.after_ref.refs_0_, f32[512,512]{1,0:T(8,128)S(1)} %copy-done.4), custom_call_target="tpu_custom_call" | custom-call | flops 2147483648 | bytes 2097152 | tf_op jit(solution)/shard_map/pallas_call | solution.py:322
  31.6 2.0 %collective-permute-done.7.refs_1_ = f32[256,128]{1,0:T(8,128)S(1)} collective-permute-done((f32[256,128]{1,0:T(8,128)S(1)}, f32[256,128]{1,0:T(8,128)S(1)}, u32[]{:S(2)}, u32[]{:S(2)}) %collective-permute-start.7) | collective-permute-done | bytes 131104 | tf_op jit(solution)/shard_map/ppermute | solution.py:267
  33.6 1.1 %shard_map.99 = (f32[128,512]{1,0:T(8,128)S(1)}, f32[64,128]{1,0:T(8,128)S(1)}) custom-call(s32[1,1]{1,0:T(1,128)} %bitcast.1.col_ref, f32[512,128]{1,0:T(8,128)S(1)} %shard_map.98.after_ref.dl_ref, f32[512,512]{1,0:T(8,128)S(1)} %copy-done.3, f32[512,128]{1,0:T(8,128)S(1)} %shard_map.97.du_ref, ...), custom_call_target="tpu_custom_call" | custom-call | flops 209715200 | bytes 2097152 | tf_op jit(solution)/shard_map/pallas_call | solution.py:363
  34.7 0.0 collective-permute-done.9
  34.7 0.1 collective-permute-start.10
  34.8 1.4 %collective-permute-start.11 = (f32[64,128]{1,0:T(8,128)S(1)}, f32[64,128]{1,0:T(8,128)S(1)}, u32[]{:S(2)}, u32[]{:S(2)}) collective-permute-start(f32[64,128]{1,0:T(8,128)S(1)} %get-tuple-element.29.refs_0_), channel_id=1, source_target_pairs={{24,0},{16,8},{8,16},{0,24},{25,1},{17,9},{9,17},{1,25},{26,2},{18... | collective-permute-start | bytes 98312 | tf_op jit(solution)/shard_map/ppermute | solution.py:267
  36.2 0.8 %collective-permute-start.12 = (f32[64,128]{1,0:T(8,128)S(1)}, f32[64,128]{1,0:T(8,128)S(1)}, u32[]{:S(2)}, u32[]{:S(2)}) collective-permute-start(f32[64,128]{1,0:T(8,128)S(1)} %get-tuple-element.29.refs_0_), channel_id=1, source_target_pairs={{16,0},{24,8},{0,16},{8,24},{17,1},{25,9},{1,17},{9,25},{18,2},{26... | collective-permute-start | bytes 98312 | tf_op jit(solution)/shard_map/ppermute | solution.py:267
  37.0 0.0 collective-permute-start.13
  37.0 0.0 collective-permute-done.10.refs_1_
  37.0 0.0 copy-done.6
  37.0 2.6 %shard_map.100.after_ref = f32[128,128]{1,0:T(8,128)} custom-call(s32[1,1]{1,0:T(1,128)} %bitcast.1.col_ref, s32[1,1]{1,0:T(1,128)} %bitcast.row_ref, f32[128,512]{1,0:T(8,128)S(1)} %get-tuple-element.26.yt_ref, f32[512,512]{1,0:T(8,128)S(1)} %copy-done.4, f32[512,128]{1,0:T(8,128)S(1)} %shard_map.98.after_ref.dl_ref, f32[128,512]{1,0:T(8,128)S(1)} %shard_map.95.at_ref, ...), custom_call_target="tpu_custom_call" | custom-call | flops 419430400 | bytes 4194304 | tf_op jit(solution)/shard_map/pallas_call | solution.py:377
  39.5 0.0 collective-permute-done.11.refs_1_
  39.5 0.6 %collective-permute-done.12.refs_2_ = f32[64,128]{1,0:T(8,128)S(1)} collective-permute-done((f32[64,128]{1,0:T(8,128)S(1)}, f32[64,128]{1,0:T(8,128)S(1)}, u32[]{:S(2)}, u32[]{:S(2)}) %collective-permute-start.12) | collective-permute-done | bytes 32800 | tf_op jit(solution)/shard_map/ppermute | solution.py:267
  40.1 0.0 collective-permute-done.13.refs_3_
  40.1 0.7 %shard_map.101 = f32[64,512]{1,0:T(8,128)} custom-call(s32[1,1]{1,0:T(1,128)} %bitcast.row_ref, f32[128,128]{1,0:T(8,128)} %shard_map.100.after_ref, f32[64,128]{1,0:T(8,128)S(1)} %get-tuple-element.29.refs_0_, f32[64,128]{1,0:T(8,128)S(1)} %collective-permute-done.11.refs_1_, f32[64,128]{1,0:T(8,128)S(1)} %collective-permute-done.12.refs_2_, ...), custom_call_target="tpu_custom_call" | custom-call | bytes 131072 | tf_op jit(solution)/shard_map/pallas_call | solution.py:392
  (16 shorter events, 0.2 us)
Async XLA Ops:
  0.6 0.9 %copy-start = (f32[64,512]{1,0:T(8,128)S(1)}, f32[64,512]{1,0:T(8,128)}, u32[]{:S(2)}) copy-start(f32[64,512]{1,0:T(8,128)} %param.13) | copy-start | bytes 393220
  1.5 7.2 %collective-permute-start = (f32[64,128]{1,0:T(8,128)S(1)}, f32[64,128]{1,0:T(8,128)S(1)}, u32[]{:S(2)}, u32[]{:S(2)}) collective-permute-start(f32[64,128]{1,0:T(8,128)S(1)} %constant_dynamic-slice_fusion), channel_id=1, source_target_pairs={{2,0},{3,1},{0,2},{1,3},{6,4},{7,5},{4,6},{5,7},{10,8},{11,9},{8,1... | collective-permute-start | bytes 98312 | tf_op jit(solution)/shard_map/ppermute | solution.py:267
  4.6 6.9 %copy-start.1 = (f32[4096,512]{1,0:T(8,128)S(1)}, f32[4096,512]{1,0:T(8,128)}, u32[]{:S(2)}) copy-start(f32[4096,512]{1,0:T(8,128)} %y_ref.1) | copy-start | bytes 25165828
  4.6 6.9 %copy-start.2 = (f32[64,4096]{1,0:T(8,128)S(1)}, f32[64,4096]{1,0:T(8,128)}, u32[]{:S(2)}) copy-start(f32[64,4096]{1,0:T(8,128)} %u_cols_ref.1) | copy-start | bytes 3145732
  4.6 6.9 %copy-start.5 = (f32[64,512]{1,0:T(8,128)S(1)}, f32[64,512]{1,0:T(8,128)}, u32[]{:S(2)}) copy-start(f32[64,512]{1,0:T(8,128)} %b_ref.1) | copy-start | bytes 393220
  8.7 9.0 %copy-start.3 = (f32[512,512]{1,0:T(8,128)S(1)}, f32[512,512]{1,0:T(8,128)}, u32[]{:S(2)}) copy-start(f32[512,512]{1,0:T(8,128)} %u_ref.3) | copy-start | bytes 3145732
  8.8 5.8 %collective-permute-start.1 = (f32[128,128]{1,0:T(8,128)S(1)}, f32[128,128]{1,0:T(8,128)S(1)}, u32[]{:S(2)}, u32[]{:S(2)}) collective-permute-start(f32[128,128]{1,0:T(8,128)S(1)} %pad_maximum_fusion.1.after_ref), channel_id=1, source_target_pairs={{4,0},{5,1},{6,2},{7,3},{0,4},{1,5},{2,6},{3,7},{12,8},{13,9},{14,... | collective-permute-start | bytes 196616 | tf_op jit(solution)/shard_map/ppermute | solution.py:267
  11.4 18.5 %copy-start.4 = (f32[512,512]{1,0:T(8,128)S(1)}, f32[512,512]{1,0:T(8,128)}, u32[]{:S(2)}) copy-start(f32[512,512]{1,0:T(8,128)} %l_ref.3) | copy-start | bytes 3145732
  14.5 1.5 %collective-permute-start.2 = (f32[192,256]{1,0:T(8,128)S(1)}, f32[192,256]{1,0:T(8,128)S(1)}, u32[]{:S(2)}, u32[]{:S(2)}) collective-permute-start(f32[192,256]{1,0:T(8,128)S(1)} %get-tuple-element.19), channel_id=1, source_target_pairs={{8,0},{0,8},{24,16},{16,24},{9,1},{1,9},{25,17},{17,25},{10,2},{2,... | collective-permute-start | bytes 589832 | tf_op jit(solution)/shard_map/ppermute | solution.py:267
  16.1 20.9 %copy-start.6 = (s32[128]{0:T(128)S(1)}, s32[128]{0:T(128)}, u32[]{:S(2)}) copy-start(s32[128]{0:T(128)} %param.15) | copy-start | bytes 1540
  16.1 5.1 %collective-permute-start.3 = (f32[192,128]{1,0:T(8,128)S(1)}, f32[192,128]{1,0:T(8,128)S(1)}, u32[]{:S(2)}, u32[]{:S(2)}) collective-permute-start(f32[192,128]{1,0:T(8,128)S(1)} %slice.13), channel_id=1, source_target_pairs={{16,0},{24,8},{0,16},{8,24},{17,1},{25,9},{1,17},{9,25},{18,2},{26... | collective-permute-start | bytes 294920 | tf_op jit(solution)/shard_map/ppermute | solution.py:267
  19.7 6.1 %collective-permute-start.8 = (f32[256,128]{1,0:T(8,128)S(1)}, f32[256,128]{1,0:T(8,128)S(1)}, u32[]{:S(2)}, u32[]{:S(2)}) collective-permute-start(f32[256,128]{1,0:T(8,128)S(1)} %pad_maximum_fusion), channel_id=1, source_target_pairs={{1,0},{0,1},{3,2},{2,3},{5,4},{4,5},{7,6},{6,7},{9,8},{8,9},{11,10... | collective-permute-start | bytes 393224 | tf_op jit(solution)/shard_map/ppermute | solution.py:267
  21.3 5.9 %collective-permute-start.4 = (f32[64,128]{1,0:T(8,128)S(1)}, f32[64,128]{1,0:T(8,128)S(1)}, u32[]{:S(2)}, u32[]{:S(2)}) collective-permute-start(f32[64,128]{1,0:T(8,128)S(1)} %slice.16), channel_id=1, source_target_pairs={{6,0},{7,1},{4,2},{5,3},{2,4},{3,5},{0,6},{1,7},{14,8},{15,9},{12,... | collective-permute-start | bytes 98312 | tf_op jit(solution)/shard_map/ppermute | solution.py:267
  23.5 5.0 %collective-permute-start.5 = (f32[64,128]{1,0:T(8,128)S(1)}, f32[64,128]{1,0:T(8,128)S(1)}, u32[]{:S(2)}, u32[]{:S(2)}) collective-permute-start(f32[64,128]{1,0:T(8,128)S(1)} %slice.16), channel_id=1, source_target_pairs={{4,0},{5,1},{6,2},{7,3},{0,4},{1,5},{2,6},{3,7},{12,8},{13,9},{14,... | collective-permute-start | bytes 98312 | tf_op jit(solution)/shard_map/ppermute | solution.py:267
  23.6 5.0 %collective-permute-start.6 = (f32[64,128]{1,0:T(8,128)S(1)}, f32[64,128]{1,0:T(8,128)S(1)}, u32[]{:S(2)}, u32[]{:S(2)}) collective-permute-start(f32[64,128]{1,0:T(8,128)S(1)} %slice.16), channel_id=1, source_target_pairs={{2,0},{3,1},{0,2},{1,3},{6,4},{7,5},{4,6},{5,7},{10,8},{11,9},{8,1... | collective-permute-start | bytes 98312 | tf_op jit(solution)/shard_map/ppermute | solution.py:267
  25.8 8.9 %collective-permute-start.9 = (f32[512,128]{1,0:T(8,128)S(1)}, f32[512,128]{1,0:T(8,128)S(1)}, u32[]{:S(2)}, u32[]{:S(2)}) collective-permute-start(f32[512,128]{1,0:T(8,128)S(1)} %constant_dynamic-update-slice_fusion.4), channel_id=1, source_target_pairs={{16,0},{24,8},{0,16},{8,24},{17,1},{25,9},{1,17},{9,25},{18,2},{26... | collective-permute-start | bytes 786440 | tf_op jit(solution)/shard_map/ppermute | solution.py:267
  28.6 5.0 %collective-permute-start.7 = (f32[256,128]{1,0:T(8,128)S(1)}, f32[256,128]{1,0:T(8,128)S(1)}, u32[]{:S(2)}, u32[]{:S(2)}) collective-permute-start(f32[256,128]{1,0:T(8,128)S(1)} %constant_dynamic-update-slice_fusion.after_ref.refs_0_), channel_id=1, source_target_pairs={{1,0},{0,1},{3,2},{2,3},{5,4},{4,5},{7,6},{6,7},{9,8},{8,9},{11,10... | collective-permute-start | bytes 393224 | tf_op jit(solution)/shard_map/ppermute | solution.py:267
  34.7 2.2 %collective-permute-start.10 = (f32[512,256]{1,0:T(8,128)S(1)}, f32[512,256]{1,0:T(8,128)S(1)}, u32[]{:S(2)}, u32[]{:S(2)}) collective-permute-start(f32[512,256]{1,0:T(8,128)S(1)} %constant_dynamic-update-slice_fusion.6.refs_0_), channel_id=1, source_target_pairs={{8,0},{0,8},{24,16},{16,24},{9,1},{1,9},{25,17},{17,25},{10,2},{2,... | collective-permute-start | bytes 1572872 | tf_op jit(solution)/shard_map/ppermute | solution.py:267
  34.8 4.7 %collective-permute-start.11 = (f32[64,128]{1,0:T(8,128)S(1)}, f32[64,128]{1,0:T(8,128)S(1)}, u32[]{:S(2)}, u32[]{:S(2)}) collective-permute-start(f32[64,128]{1,0:T(8,128)S(1)} %get-tuple-element.29.refs_0_), channel_id=1, source_target_pairs={{24,0},{16,8},{8,16},{0,24},{25,1},{17,9},{9,17},{1,25},{26,2},{18... | collective-permute-start | bytes 98312 | tf_op jit(solution)/shard_map/ppermute | solution.py:267
  36.2 3.9 %collective-permute-start.12 = (f32[64,128]{1,0:T(8,128)S(1)}, f32[64,128]{1,0:T(8,128)S(1)}, u32[]{:S(2)}, u32[]{:S(2)}) collective-permute-start(f32[64,128]{1,0:T(8,128)S(1)} %get-tuple-element.29.refs_0_), channel_id=1, source_target_pairs={{16,0},{24,8},{0,16},{8,24},{17,1},{25,9},{1,17},{9,25},{18,2},{26... | collective-permute-start | bytes 98312 | tf_op jit(solution)/shard_map/ppermute | solution.py:267
  37.0 3.1 %collective-permute-start.13 = (f32[64,128]{1,0:T(8,128)S(1)}, f32[64,128]{1,0:T(8,128)S(1)}, u32[]{:S(2)}, u32[]{:S(2)}) collective-permute-start(f32[64,128]{1,0:T(8,128)S(1)} %get-tuple-element.29.refs_0_), channel_id=1, source_target_pairs={{8,0},{0,8},{24,16},{16,24},{9,1},{1,9},{25,17},{17,25},{10,2},{2,... | collective-permute-start | bytes 98312 | tf_op jit(solution)/shard_map/ppermute | solution.py:267

commit v7 on v6

--- a/solution.py
+++ b/solution.py
@@ -162,10 +162,17 @@
     return pl.ds(pl.multiple_of(place * size, size), size)
 
 
-def place_piece(col, inner, outer, share, step, piece, full_ref, columns, down=False):
+def doubled(size):
+    order = [0]
+    for bit in reversed(range(size.bit_length() - 1)):
+        order += [far ^ (1 << bit) for far in order]
+    return order
+
+
+def place_piece(col, inner, order, share, step, piece, full_ref, columns):
     low, high = lax.rem(col, inner), lax.div(col, inner)
-    for turn in range(outer):
-        at = (high ^ ((outer - turn) % outer if down else turn)) * inner + (low ^ step)
+    for turn, far in enumerate(order):
+        at = (high ^ far) * inner + (low ^ step)
         full_ref[aligned_span(at, share), columns] = piece[turn * share : (turn + 1) * share, :]
 
 
@@ -175,7 +182,7 @@
     yt_ref, y_ref, full_ref = refs[inner:]
     col = col_ref[0, 0]
     for step, piece_ref in enumerate(piece_refs):
-        place_piece(col, inner, outer, share, step, piece_ref[...], full_ref, slice(None), True)
+        place_piece(col, inner, [0, *range(outer - 1, 0, -1)], share, step, piece_ref[...], full_ref, slice(None))
     count = u_ref.shape[0] // TILE
     solved = []
     for i in range(count):
@@ -195,6 +202,7 @@
     x_ref, lc_ref = refs[len(side_refs) :]
     row, col = row_ref[0, 0], col_ref[0, 0]
     rows = outer * share
+    order = doubled(outer)
     columns = lc_ref.shape[1] // parts
     chips = max(parts // 2, 1)
     for turn, side_ref in enumerate(side_refs):
@@ -205,7 +213,7 @@
                 target = aligned_span(row ^ (2 * step) ^ turn, columns)
             for piece in range(inner):
                 value = side_ref[piece * rows : (piece + 1) * rows, step * columns : (step + 1) * columns]
-                place_piece(col, inner, outer, share, piece, value, lc_ref, target)
+                place_piece(col, inner, order, share, piece, value, lc_ref, target)
     width = l_ref.shape[0]
     count = width // TILE
     perm = perm_ref[...]
@@ -295,11 +303,11 @@
     quarter = width // parts
     line = lax.dynamic_slice_in_dim(l_coupling, lax.rem(row, parts) * quarter, quarter, 1)
     lines = []
-    mask = inner
-    while mask < col_size:
+    mask = col_size // 2
+    while mask >= inner:
         line = jnp.concatenate([line, swapped(line, "col", col_size, mask)], axis=0)
         lines.append(line)
-        mask *= 2
+        mask //= 2
 
     perm_row = jnp.pad(perm, (0, max(TILE - picks, 0)), constant_values=-1)[None, :]
     lanes = perm_row.shape[1]

time: 40.9 us -> 40.3 us (0.985)
  waiting for transfers between devices: 6.17 us -> 5.59 us
    ppermute x14, waiting for transfers between devices: 6.17 us -> 5.59 us  [swapped(): return lax.ppermute(value, axis, [(dst ^ mask, dst) for dst in range(size)])]
  transfers between devices with their start and end apart: 14 -> 14, of which waited for: 5 -> 6; matrix products, arithmetic and copies ran while one was open for 0% -> 0% of each run, Pallas kernels for 34% -> 34%
where the time goes in v7:
time: 40.3 us; the launch traced here: 40.2 us
  starting transfers between devices  18.3 us (45%)
  Pallas kernels  14.4 us (36%)
  waiting for transfers between devices  5.59 us (14%)
  local copies, waits for them, and re-layouts  1.02 us (3%)
  between operations  0.83 us (2%)
    ppermute x14, starting transfers between devices, swapped(): return lax.ppermute(value, axis, [(dst ^ mask, dst) for dst in range(size)])  18.3 us
    ppermute x14, waiting for transfers between devices, swapped(): return lax.ppermute(value, axis, [(dst ^ mask, dst) for dst in range(size)])  5.59 us
    pallas_call x1, Pallas kernels, per_device(): call(solve_selected_kernel, shape(lanes, width), 6 << 30, 2 << 20, 8, scr...  4.15 us
    pallas_call x2, Pallas kernels, per_device(): call(kernel, shape(width, TILE), 2 << 30, 2 << 20, 8, in_specs=[ANY, VMEM...  3.59 us
    pallas_call x1, Pallas kernels, per_device(): call(functools.partial(finish_kernel, inner, outer, share, parts), shape(...  2.56 us
    pallas_call x1, Pallas kernels, per_device(): call(functools.partial(product_kernel, row_size, paired), outs, 1 << 30,...  2.34 us
    pallas_call x1, Pallas kernels, per_device(): call(functools.partial(solve_u_kernel, inner, outer, share), (shape(rhs,...  1.05 us
    unnamed x19, local copies, waits for them, and re-layouts  0.96 us
  transfers between devices with their start and end apart: 14, of which 6 were waited for; matrix products, arithmetic and copies ran while one was open for 0% of the time, Pallas kernels for 34%

profile of v7, /device:TPU:0, one launch (start us, length us, event | category | flops | bytes accessed | tf_op | source)
XLA Modules:
  0.0 40.2 jit_solution(4409820972196078351)
XLA Ops:
  0.6 0.0 copy-start
  0.7 0.9 %copy-done = f32[64,512]{1,0:T(8,128)S(1)} copy-done((f32[64,512]{1,0:T(8,128)S(1)}, f32[64,512]{1,0:T(8,128)}, u32[]{:S(2)}) %copy-start) | copy-done | bytes 131096
  1.5 4.0 %collective-permute-start = (f32[64,128]{1,0:T(8,128)S(1)}, f32[64,128]{1,0:T(8,128)S(1)}, u32[]{:S(2)}, u32[]{:S(2)}) collective-permute-start(f32[64,128]{1,0:T(8,128)S(1)} %constant_dynamic-slice_fusion), channel_id=1, source_target_pairs={{4,0},{5,1},{6,2},{7,3},{0,4},{1,5},{2,6},{3,7},{12,8},{13,9},{14,... | collective-permute-start | bytes 98312 | tf_op jit(solution)/shard_map/ppermute | solution.py:275
  5.6 0.0 copy-start.1
  5.6 0.0 copy-start.2
  5.6 0.0 copy-start.5
  5.6 4.1 %shard_map.95.at_ref = f32[128,512]{1,0:T(8,128)S(1)} custom-call(s32[1,128]{1,0:T(1,128)} %bitcast.3, f32[512,512]{1,0:T(8,128)} %lp_hbm.1), custom_call_target="tpu_custom_call" | custom-call | flops 6442450944 | bytes 2097152 | tf_op jit(solution)/shard_map/pallas_call | solution.py:315
  9.7 0.0 copy-start.3
  9.8 0.0 collective-permute-done
  9.8 1.6 %collective-permute-start.1 = (f32[128,128]{1,0:T(8,128)S(1)}, f32[128,128]{1,0:T(8,128)S(1)}, u32[]{:S(2)}, u32[]{:S(2)}) collective-permute-start(f32[128,128]{1,0:T(8,128)S(1)} %pad_maximum_fusion.1.after_ref), channel_id=1, source_target_pairs={{2,0},{3,1},{0,2},{1,3},{6,4},{7,5},{4,6},{5,7},{10,8},{11,9},{8,1... | collective-permute-start | bytes 196616 | tf_op jit(solution)/shard_map/ppermute | solution.py:275
  11.4 0.0 copy-done.1
  11.4 0.0 copy-done.2
  11.4 0.0 copy-done.5
  11.4 0.0 copy-start.4
  11.4 2.3 %shard_map.96 = (f32[192,256]{1,0:T(8,128)S(1)}, f32[192,256]{1,0:T(8,128)S(1)}) custom-call(s32[1,1]{1,0:T(1,128)} %bitcast.row_ref, f32[128,512]{1,0:T(8,128)S(1)} %shard_map.95.at_ref, f32[128,128]{1,0:T(8,128)S(1)} %pad_maximum_fusion.1.after_ref, f32[64,512]{1,0:T(8,128)S(1)} %copy-done.5, f32[64,4096]{1,0:T(8,128)S(1)} %copy-done.2, ...), custom_call_target="tpu_custom_call" | custom-call | flops 1073741824 | bytes 10485760 | tf_op jit(solution)/shard_map/pallas_call | solution.py:334
  13.8 0.3 collective-permute-done.1
  14.1 0.1 collective-permute-start.2
  14.2 1.4 %collective-permute-done.2 = f32[192,256]{1,0:T(8,128)S(1)} collective-permute-done((f32[192,256]{1,0:T(8,128)S(1)}, f32[192,256]{1,0:T(8,128)S(1)}, u32[]{:S(2)}, u32[]{:S(2)}) %collective-permute-start.2) | collective-permute-done | bytes 196640 | tf_op jit(solution)/shard_map/ppermute | solution.py:275
  15.7 0.0 copy-start.6
  15.7 1.6 %collective-permute-start.3 = (f32[192,128]{1,0:T(8,128)S(1)}, f32[192,128]{1,0:T(8,128)S(1)}, u32[]{:S(2)}, u32[]{:S(2)}) collective-permute-start(f32[192,128]{1,0:T(8,128)S(1)} %slice.13), channel_id=1, source_target_pairs={{16,0},{24,8},{0,16},{8,24},{17,1},{25,9},{1,17},{9,25},{18,2},{26... | collective-permute-start | bytes 294920 | tf_op jit(solution)/shard_map/ppermute | solution.py:275
  17.3 0.0 copy-done.3
  17.3 1.9 %shard_map.97.du_ref = f32[512,128]{1,0:T(8,128)S(1)} custom-call(f32[192,256]{1,0:T(8,128)S(1)} %add.10.after_ref, f32[512,512]{1,0:T(8,128)S(1)} %copy-done.3), custom_call_target="tpu_custom_call" | custom-call | flops 2147483648 | bytes 2097152 | tf_op jit(solution)/shard_map/pallas_call | solution.py:330
  19.2 1.6 %collective-permute-start.8 = (f32[256,128]{1,0:T(8,128)S(1)}, f32[256,128]{1,0:T(8,128)S(1)}, u32[]{:S(2)}, u32[]{:S(2)}) collective-permute-start(f32[256,128]{1,0:T(8,128)S(1)} %pad_maximum_fusion), channel_id=1, source_target_pairs={{1,0},{0,1},{3,2},{2,3},{5,4},{4,5},{7,6},{6,7},{9,8},{8,9},{11,10... | collective-permute-start | bytes 393224 | tf_op jit(solution)/shard_map/ppermute | solution.py:275
  20.8 0.0 collective-permute-done.3
  20.8 1.9 %collective-permute-start.4 = (f32[64,128]{1,0:T(8,128)S(1)}, f32[64,128]{1,0:T(8,128)S(1)}, u32[]{:S(2)}, u32[]{:S(2)}) collective-permute-start(f32[64,128]{1,0:T(8,128)S(1)} %slice.16), channel_id=1, source_target_pairs={{6,0},{7,1},{4,2},{5,3},{2,4},{3,5},{0,6},{1,7},{14,8},{15,9},{12,... | collective-permute-start | bytes 98312 | tf_op jit(solution)/shard_map/ppermute | solution.py:275
  22.7 1.2 %collective-permute-start.5 = (f32[64,128]{1,0:T(8,128)S(1)}, f32[64,128]{1,0:T(8,128)S(1)}, u32[]{:S(2)}, u32[]{:S(2)}) collective-permute-start(f32[64,128]{1,0:T(8,128)S(1)} %slice.16), channel_id=1, source_target_pairs={{4,0},{5,1},{6,2},{7,3},{0,4},{1,5},{2,6},{3,7},{12,8},{13,9},{14,... | collective-permute-start | bytes 98312 | tf_op jit(solution)/shard_map/ppermute | solution.py:275
  23.9 1.3 %collective-permute-start.6 = (f32[64,128]{1,0:T(8,128)S(1)}, f32[64,128]{1,0:T(8,128)S(1)}, u32[]{:S(2)}, u32[]{:S(2)}) collective-permute-start(f32[64,128]{1,0:T(8,128)S(1)} %slice.16), channel_id=1, source_target_pairs={{2,0},{3,1},{0,2},{1,3},{6,4},{7,5},{4,6},{5,7},{10,8},{11,9},{8,1... | collective-permute-start | bytes 98312 | tf_op jit(solution)/shard_map/ppermute | solution.py:275
  25.3 0.0 collective-permute-done.8
  25.3 1.4 %collective-permute-start.9 = (f32[512,128]{1,0:T(8,128)S(1)}, f32[512,128]{1,0:T(8,128)S(1)}, u32[]{:S(2)}, u32[]{:S(2)}) collective-permute-start(f32[512,128]{1,0:T(8,128)S(1)} %constant_dynamic-update-slice_fusion.4), channel_id=1, source_target_pairs={{16,0},{24,8},{0,16},{8,24},{17,1},{25,9},{1,17},{9,25},{18,2},{26... | collective-permute-start | bytes 786440 | tf_op jit(solution)/shard_map/ppermute | solution.py:275
  26.7 0.0 collective-permute-done.4
  26.7 0.9 %collective-permute-done.5 = f32[64,128]{1,0:T(8,128)S(1)} collective-permute-done((f32[64,128]{1,0:T(8,128)S(1)}, f32[64,128]{1,0:T(8,128)S(1)}, u32[]{:S(2)}, u32[]{:S(2)}) %collective-permute-start.5) | collective-permute-done | bytes 32800 | tf_op jit(solution)/shard_map/ppermute | solution.py:275
  27.6 0.3 collective-permute-done.6
  27.9 1.4 %collective-permute-start.7 = (f32[256,128]{1,0:T(8,128)S(1)}, f32[256,128]{1,0:T(8,128)S(1)}, u32[]{:S(2)}, u32[]{:S(2)}) collective-permute-start(f32[256,128]{1,0:T(8,128)S(1)} %constant_dynamic-update-slice_fusion.after_ref.refs_0_), channel_id=1, source_target_pairs={{1,0},{0,1},{3,2},{2,3},{5,4},{4,5},{7,6},{6,7},{9,8},{8,9},{11,10... | collective-permute-start | bytes 393224 | tf_op jit(solution)/shard_map/ppermute | solution.py:275
  29.3 0.0 copy-done.4
  29.3 1.7 %shard_map.98.after_ref.dl_ref = f32[512,128]{1,0:T(8,128)S(1)} custom-call(f32[256,128]{1,0:T(8,128)S(1)} %constant_dynamic-update-slice_fusion.after_ref.refs_0_, f32[512,512]{1,0:T(8,128)S(1)} %copy-done.4), custom_call_target="tpu_custom_call" | custom-call | flops 2147483648 | bytes 2097152 | tf_op jit(solution)/shard_map/pallas_call | solution.py:330
  31.0 1.9 %collective-permute-done.7.refs_1_ = f32[256,128]{1,0:T(8,128)S(1)} collective-permute-done((f32[256,128]{1,0:T(8,128)S(1)}, f32[256,128]{1,0:T(8,128)S(1)}, u32[]{:S(2)}, u32[]{:S(2)}) %collective-permute-start.7) | collective-permute-done | bytes 131104 | tf_op jit(solution)/shard_map/ppermute | solution.py:275
  32.9 1.1 %shard_map.99 = (f32[128,512]{1,0:T(8,128)S(1)}, f32[64,128]{1,0:T(8,128)S(1)}) custom-call(s32[1,1]{1,0:T(1,128)} %bitcast.1.col_ref, f32[512,128]{1,0:T(8,128)S(1)} %shard_map.98.after_ref.dl_ref, f32[512,512]{1,0:T(8,128)S(1)} %copy-done.3, f32[512,128]{1,0:T(8,128)S(1)} %shard_map.97.du_ref, ...), custom_call_target="tpu_custom_call" | custom-call | flops 209715200 | bytes 2097152 | tf_op jit(solution)/shard_map/pallas_call | solution.py:371
  34.0 0.0 collective-permute-done.9
  34.0 0.1 collective-permute-start.10
  34.1 1.5 %collective-permute-start.11 = (f32[64,128]{1,0:T(8,128)S(1)}, f32[64,128]{1,0:T(8,128)S(1)}, u32[]{:S(2)}, u32[]{:S(2)}) collective-permute-start(f32[64,128]{1,0:T(8,128)S(1)} %get-tuple-element.29.refs_0_), channel_id=1, source_target_pairs={{24,0},{16,8},{8,16},{0,24},{25,1},{17,9},{9,17},{1,25},{26,2},{18... | collective-permute-start | bytes 98312 | tf_op jit(solution)/shard_map/ppermute | solution.py:275
  35.6 0.7 %collective-permute-start.12 = (f32[64,128]{1,0:T(8,128)S(1)}, f32[64,128]{1,0:T(8,128)S(1)}, u32[]{:S(2)}, u32[]{:S(2)}) collective-permute-start(f32[64,128]{1,0:T(8,128)S(1)} %get-tuple-element.29.refs_0_), channel_id=1, source_target_pairs={{16,0},{24,8},{0,16},{8,24},{17,1},{25,9},{1,17},{9,25},{18,2},{26... | collective-permute-start | bytes 98312 | tf_op jit(solution)/shard_map/ppermute | solution.py:275
  36.2 0.0 collective-permute-start.13
  36.3 0.0 collective-permute-done.10.refs_1_
  36.3 0.0 copy-done.6
  36.3 2.6 %shard_map.100.after_ref = f32[128,128]{1,0:T(8,128)} custom-call(s32[1,1]{1,0:T(1,128)} %bitcast.1.col_ref, s32[1,1]{1,0:T(1,128)} %bitcast.row_ref, f32[128,512]{1,0:T(8,128)S(1)} %get-tuple-element.26.yt_ref, f32[512,512]{1,0:T(8,128)S(1)} %copy-done.4, f32[512,128]{1,0:T(8,128)S(1)} %shard_map.98.after_ref.dl_ref, f32[128,512]{1,0:T(8,128)S(1)} %shard_map.95.at_ref, ...), custom_call_target="tpu_custom_call" | custom-call | flops 419430400 | bytes 4194304 | tf_op jit(solution)/shard_map/pallas_call | solution.py:385
  38.8 0.0 collective-permute-done.11.refs_1_
  38.8 0.7 %collective-permute-done.12.refs_2_ = f32[64,128]{1,0:T(8,128)S(1)} collective-permute-done((f32[64,128]{1,0:T(8,128)S(1)}, f32[64,128]{1,0:T(8,128)S(1)}, u32[]{:S(2)}, u32[]{:S(2)}) %collective-permute-start.12) | collective-permute-done | bytes 32800 | tf_op jit(solution)/shard_map/ppermute | solution.py:275
  39.5 0.0 collective-permute-done.13.refs_3_
  39.5 0.7 %shard_map.101 = f32[64,512]{1,0:T(8,128)} custom-call(s32[1,1]{1,0:T(1,128)} %bitcast.row_ref, f32[128,128]{1,0:T(8,128)} %shard_map.100.after_ref, f32[64,128]{1,0:T(8,128)S(1)} %get-tuple-element.29.refs_0_, f32[64,128]{1,0:T(8,128)S(1)} %collective-permute-done.11.refs_1_, f32[64,128]{1,0:T(8,128)S(1)} %collective-permute-done.12.refs_2_, ...), custom_call_target="tpu_custom_call" | custom-call | bytes 131072 | tf_op jit(solution)/shard_map/pallas_call | solution.py:400
  (16 shorter events, 0.2 us)
Async XLA Ops:
  0.6 0.9 %copy-start = (f32[64,512]{1,0:T(8,128)S(1)}, f32[64,512]{1,0:T(8,128)}, u32[]{:S(2)}) copy-start(f32[64,512]{1,0:T(8,128)} %param.13) | copy-start | bytes 393220
  1.5 8.2 %collective-permute-start = (f32[64,128]{1,0:T(8,128)S(1)}, f32[64,128]{1,0:T(8,128)S(1)}, u32[]{:S(2)}, u32[]{:S(2)}) collective-permute-start(f32[64,128]{1,0:T(8,128)S(1)} %constant_dynamic-slice_fusion), channel_id=1, source_target_pairs={{4,0},{5,1},{6,2},{7,3},{0,4},{1,5},{2,6},{3,7},{12,8},{13,9},{14,... | collective-permute-start | bytes 98312 | tf_op jit(solution)/shard_map/ppermute | solution.py:275
  5.6 5.8 %copy-start.1 = (f32[4096,512]{1,0:T(8,128)S(1)}, f32[4096,512]{1,0:T(8,128)}, u32[]{:S(2)}) copy-start(f32[4096,512]{1,0:T(8,128)} %y_ref.1) | copy-start | bytes 25165828
  5.6 5.8 %copy-start.2 = (f32[64,4096]{1,0:T(8,128)S(1)}, f32[64,4096]{1,0:T(8,128)}, u32[]{:S(2)}) copy-start(f32[64,4096]{1,0:T(8,128)} %u_cols_ref.1) | copy-start | bytes 3145732
  5.6 5.8 %copy-start.5 = (f32[64,512]{1,0:T(8,128)S(1)}, f32[64,512]{1,0:T(8,128)}, u32[]{:S(2)}) copy-start(f32[64,512]{1,0:T(8,128)} %b_ref.1) | copy-start | bytes 393220
  9.7 7.5 %copy-start.3 = (f32[512,512]{1,0:T(8,128)S(1)}, f32[512,512]{1,0:T(8,128)}, u32[]{:S(2)}) copy-start(f32[512,512]{1,0:T(8,128)} %u_ref.3) | copy-start | bytes 3145732
  9.8 4.3 %collective-permute-start.1 = (f32[128,128]{1,0:T(8,128)S(1)}, f32[128,128]{1,0:T(8,128)S(1)}, u32[]{:S(2)}, u32[]{:S(2)}) collective-permute-start(f32[128,128]{1,0:T(8,128)S(1)} %pad_maximum_fusion.1.after_ref), channel_id=1, source_target_pairs={{2,0},{3,1},{0,2},{1,3},{6,4},{7,5},{4,6},{5,7},{10,8},{11,9},{8,1... | collective-permute-start | bytes 196616 | tf_op jit(solution)/shard_map/ppermute | solution.py:275
  11.4 17.9 %copy-start.4 = (f32[512,512]{1,0:T(8,128)S(1)}, f32[512,512]{1,0:T(8,128)}, u32[]{:S(2)}) copy-start(f32[512,512]{1,0:T(8,128)} %l_ref.3) | copy-start | bytes 3145732
  14.1 1.5 %collective-permute-start.2 = (f32[192,256]{1,0:T(8,128)S(1)}, f32[192,256]{1,0:T(8,128)S(1)}, u32[]{:S(2)}, u32[]{:S(2)}) collective-permute-start(f32[192,256]{1,0:T(8,128)S(1)} %get-tuple-element.19), channel_id=1, source_target_pairs={{8,0},{0,8},{24,16},{16,24},{9,1},{1,9},{25,17},{17,25},{10,2},{2,... | collective-permute-start | bytes 589832 | tf_op jit(solution)/shard_map/ppermute | solution.py:275
  15.7 20.6 %copy-start.6 = (s32[128]{0:T(128)S(1)}, s32[128]{0:T(128)}, u32[]{:S(2)}) copy-start(s32[128]{0:T(128)} %param.15) | copy-start | bytes 1540
  15.7 5.1 %collective-permute-start.3 = (f32[192,128]{1,0:T(8,128)S(1)}, f32[192,128]{1,0:T(8,128)S(1)}, u32[]{:S(2)}, u32[]{:S(2)}) collective-permute-start(f32[192,128]{1,0:T(8,128)S(1)} %slice.13), channel_id=1, source_target_pairs={{16,0},{24,8},{0,16},{8,24},{17,1},{25,9},{1,17},{9,25},{18,2},{26... | collective-permute-start | bytes 294920 | tf_op jit(solution)/shard_map/ppermute | solution.py:275
  19.2 6.1 %collective-permute-start.8 = (f32[256,128]{1,0:T(8,128)S(1)}, f32[256,128]{1,0:T(8,128)S(1)}, u32[]{:S(2)}, u32[]{:S(2)}) collective-permute-start(f32[256,128]{1,0:T(8,128)S(1)} %pad_maximum_fusion), channel_id=1, source_target_pairs={{1,0},{0,1},{3,2},{2,3},{5,4},{4,5},{7,6},{6,7},{9,8},{8,9},{11,10... | collective-permute-start | bytes 393224 | tf_op jit(solution)/shard_map/ppermute | solution.py:275
  20.8 5.9 %collective-permute-start.4 = (f32[64,128]{1,0:T(8,128)S(1)}, f32[64,128]{1,0:T(8,128)S(1)}, u32[]{:S(2)}, u32[]{:S(2)}) collective-permute-start(f32[64,128]{1,0:T(8,128)S(1)} %slice.16), channel_id=1, source_target_pairs={{6,0},{7,1},{4,2},{5,3},{2,4},{3,5},{0,6},{1,7},{14,8},{15,9},{12,... | collective-permute-start | bytes 98312 | tf_op jit(solution)/shard_map/ppermute | solution.py:275
  22.7 4.9 %collective-permute-start.5 = (f32[64,128]{1,0:T(8,128)S(1)}, f32[64,128]{1,0:T(8,128)S(1)}, u32[]{:S(2)}, u32[]{:S(2)}) collective-permute-start(f32[64,128]{1,0:T(8,128)S(1)} %slice.16), channel_id=1, source_target_pairs={{4,0},{5,1},{6,2},{7,3},{0,4},{1,5},{2,6},{3,7},{12,8},{13,9},{14,... | collective-permute-start | bytes 98312 | tf_op jit(solution)/shard_map/ppermute | solution.py:275
  23.9 4.0 %collective-permute-start.6 = (f32[64,128]{1,0:T(8,128)S(1)}, f32[64,128]{1,0:T(8,128)S(1)}, u32[]{:S(2)}, u32[]{:S(2)}) collective-permute-start(f32[64,128]{1,0:T(8,128)S(1)} %slice.16), channel_id=1, source_target_pairs={{2,0},{3,1},{0,2},{1,3},{6,4},{7,5},{4,6},{5,7},{10,8},{11,9},{8,1... | collective-permute-start | bytes 98312 | tf_op jit(solution)/shard_map/ppermute | solution.py:275
  25.3 8.7 %collective-permute-start.9 = (f32[512,128]{1,0:T(8,128)S(1)}, f32[512,128]{1,0:T(8,128)S(1)}, u32[]{:S(2)}, u32[]{:S(2)}) collective-permute-start(f32[512,128]{1,0:T(8,128)S(1)} %constant_dynamic-update-slice_fusion.4), channel_id=1, source_target_pairs={{16,0},{24,8},{0,16},{8,24},{17,1},{25,9},{1,17},{9,25},{18,2},{26... | collective-permute-start | bytes 786440 | tf_op jit(solution)/shard_map/ppermute | solution.py:275
  27.9 5.0 %collective-permute-start.7 = (f32[256,128]{1,0:T(8,128)S(1)}, f32[256,128]{1,0:T(8,128)S(1)}, u32[]{:S(2)}, u32[]{:S(2)}) collective-permute-start(f32[256,128]{1,0:T(8,128)S(1)} %constant_dynamic-update-slice_fusion.after_ref.refs_0_), channel_id=1, source_target_pairs={{1,0},{0,1},{3,2},{2,3},{5,4},{4,5},{7,6},{6,7},{9,8},{8,9},{11,10... | collective-permute-start | bytes 393224 | tf_op jit(solution)/shard_map/ppermute | solution.py:275
  34.0 2.2 %collective-permute-start.10 = (f32[512,256]{1,0:T(8,128)S(1)}, f32[512,256]{1,0:T(8,128)S(1)}, u32[]{:S(2)}, u32[]{:S(2)}) collective-permute-start(f32[512,256]{1,0:T(8,128)S(1)} %constant_dynamic-update-slice_fusion.6.refs_0_), channel_id=1, source_target_pairs={{8,0},{0,8},{24,16},{16,24},{9,1},{1,9},{25,17},{17,25},{10,2},{2,... | collective-permute-start | bytes 1572872 | tf_op jit(solution)/shard_map/ppermute | solution.py:275
  34.1 4.7 %collective-permute-start.11 = (f32[64,128]{1,0:T(8,128)S(1)}, f32[64,128]{1,0:T(8,128)S(1)}, u32[]{:S(2)}, u32[]{:S(2)}) collective-permute-start(f32[64,128]{1,0:T(8,128)S(1)} %get-tuple-element.29.refs_0_), channel_id=1, source_target_pairs={{24,0},{16,8},{8,16},{0,24},{25,1},{17,9},{9,17},{1,25},{26,2},{18... | collective-permute-start | bytes 98312 | tf_op jit(solution)/shard_map/ppermute | solution.py:275
  35.6 3.9 %collective-permute-start.12 = (f32[64,128]{1,0:T(8,128)S(1)}, f32[64,128]{1,0:T(8,128)S(1)}, u32[]{:S(2)}, u32[]{:S(2)}) collective-permute-start(f32[64,128]{1,0:T(8,128)S(1)} %get-tuple-element.29.refs_0_), channel_id=1, source_target_pairs={{16,0},{24,8},{0,16},{8,24},{17,1},{25,9},{1,17},{9,25},{18,2},{26... | collective-permute-start | bytes 98312 | tf_op jit(solution)/shard_map/ppermute | solution.py:275
  36.2 3.3 %collective-permute-start.13 = (f32[64,128]{1,0:T(8,128)S(1)}, f32[64,128]{1,0:T(8,128)S(1)}, u32[]{:S(2)}, u32[]{:S(2)}) collective-permute-start(f32[64,128]{1,0:T(8,128)S(1)} %get-tuple-element.29.refs_0_), channel_id=1, source_target_pairs={{8,0},{0,8},{24,16},{16,24},{9,1},{1,9},{25,17},{17,25},{10,2},{2,... | collective-permute-start | bytes 98312 | tf_op jit(solution)/shard_map/ppermute | solution.py:275

commit v8 on v7

--- a/solution.py
+++ b/solution.py
@@ -345,7 +345,6 @@
     payload, line = lax.optimization_barrier((payload, line))
     if paired:
         keep = payload[0] + swapped(payload[1], "row", row_size, 1)
-        keep, line = lax.optimization_barrier((keep, line))
         turn = lambda step: keep[:, step * column_share : (step + 1) * column_share]
         own = turn(0)
         for step in range(1, chips):
@@ -358,9 +357,9 @@
             own = own + swapped(block(payload[0], row ^ step), "row", row_size, step)
         resid = own[:share] + block(b_panel, row)
     rhs = max(TILE, column_share)
+    du = inverses(invert_upper_kernel, keep if paired else payload[0], u_diag)
+    resid, du, line = lax.optimization_barrier((resid, du, line))
     mine = jnp.concatenate(gather_pieces(line, "col", col_size, inner), axis=0)
-    du = inverses(invert_upper_kernel, keep if paired else payload[0], u_diag)
-    resid, du = lax.optimization_barrier((resid, du))
     resid = jnp.pad(resid, ((0, 0), (0, rhs - column_share)))
     v = jnp.pad(own[share:], ((0, 0), (0, rhs - column_share)))
     sides = [mine] + [swapped(mine, "row", row_size, 2 * step) for step in range(1, chips if parts > 1 else 1)]

time: 40.3 us -> 43.5 us (1.079)
  waiting for transfers between devices: 5.59 us -> 8.38 us
    ppermute x14, waiting for transfers between devices: 5.59 us -> 8.38 us  [swapped(): return lax.ppermute(value, axis, [(dst ^ mask, dst) for dst in range(size)])]
  transfers between devices with their start and end apart: 14 -> 14, of which waited for: 6 -> 6; matrix products, arithmetic and copies ran while one was open for 0% -> 0% of each run, Pallas kernels for 34% -> 32%
where the time goes in v8:
time: 43.5 us; the launch traced here: 43.3 us
  starting transfers between devices  18.6 us (43%)
  Pallas kernels  14.4 us (33%)
  waiting for transfers between devices  8.38 us (19%)
  local copies, waits for them, and re-layouts  1.02 us (2%)
  between operations  0.83 us (2%)
    ppermute x14, starting transfers between devices, swapped(): return lax.ppermute(value, axis, [(dst ^ mask, dst) for dst in range(size)])  18.6 us
    ppermute x14, waiting for transfers between devices, swapped(): return lax.ppermute(value, axis, [(dst ^ mask, dst) for dst in range(size)])  8.38 us
    pallas_call x1, Pallas kernels, per_device(): call(solve_selected_kernel, shape(lanes, width), 6 << 30, 2 << 20, 8, scr...  4.15 us
    pallas_call x2, Pallas kernels, per_device(): call(kernel, shape(width, TILE), 2 << 30, 2 << 20, 8, in_specs=[ANY, VMEM...  3.59 us
    pallas_call x1, Pallas kernels, per_device(): call(functools.partial(finish_kernel, inner, outer, share, parts), shape(...  2.56 us
    pallas_call x1, Pallas kernels, per_device(): call(functools.partial(product_kernel, row_size, paired), outs, 1 << 30,...  2.34 us
    pallas_call x1, Pallas kernels, per_device(): call(functools.partial(solve_u_kernel, inner, outer, share), (shape(rhs,...  1.05 us
    unnamed x19, local copies, waits for them, and re-layouts  0.96 us
  transfers between devices with their start and end apart: 14, of which 6 were waited for; matrix products, arithmetic and copies ran while one was open for 0% of the time, Pallas kernels for 32%

profile of v8, /device:TPU:0, one launch (start us, length us, event | category | flops | bytes accessed | tf_op | source)
XLA Modules:
  0.0 43.3 jit_solution(10065353540229508913)
XLA Ops:
  0.6 0.0 copy-start
  0.7 0.9 %copy-done = f32[64,512]{1,0:T(8,128)S(1)} copy-done((f32[64,512]{1,0:T(8,128)S(1)}, f32[64,512]{1,0:T(8,128)}, u32[]{:S(2)}) %copy-start) | copy-done | bytes 131096
  1.5 4.0 %collective-permute-start = (f32[64,128]{1,0:T(8,128)S(1)}, f32[64,128]{1,0:T(8,128)S(1)}, u32[]{:S(2)}, u32[]{:S(2)}) collective-permute-start(f32[64,128]{1,0:T(8,128)S(1)} %constant_dynamic-slice_fusion), channel_id=1, source_target_pairs={{4,0},{5,1},{6,2},{7,3},{0,4},{1,5},{2,6},{3,7},{12,8},{13,9},{14,... | collective-permute-start | bytes 98312 | tf_op jit(solution)/shard_map/ppermute | solution.py:275
  5.6 0.0 copy-start.1
  5.6 0.0 copy-start.2
  5.6 0.0 copy-start.5
  5.6 4.1 %shard_map.95.at_ref = f32[128,512]{1,0:T(8,128)S(1)} custom-call(s32[1,128]{1,0:T(1,128)} %bitcast.3, f32[512,512]{1,0:T(8,128)} %lp_hbm.1), custom_call_target="tpu_custom_call" | custom-call | flops 6442450944 | bytes 2097152 | tf_op jit(solution)/shard_map/pallas_call | solution.py:315
  9.7 0.0 copy-start.3
  9.8 0.0 collective-permute-done
  9.8 1.6 %collective-permute-start.1 = (f32[128,128]{1,0:T(8,128)S(1)}, f32[128,128]{1,0:T(8,128)S(1)}, u32[]{:S(2)}, u32[]{:S(2)}) collective-permute-start(f32[128,128]{1,0:T(8,128)S(1)} %pad_maximum_fusion.1.after_ref), channel_id=1, source_target_pairs={{2,0},{3,1},{0,2},{1,3},{6,4},{7,5},{4,6},{5,7},{10,8},{11,9},{8,1... | collective-permute-start | bytes 196616 | tf_op jit(solution)/shard_map/ppermute | solution.py:275
  11.4 0.0 copy-done.1
  11.4 0.0 copy-done.2
  11.4 0.0 copy-done.5
  11.4 0.0 copy-start.4
  11.4 2.3 %shard_map.96 = (f32[192,256]{1,0:T(8,128)S(1)}, f32[192,256]{1,0:T(8,128)S(1)}) custom-call(s32[1,1]{1,0:T(1,128)} %bitcast.row_ref, f32[128,512]{1,0:T(8,128)S(1)} %shard_map.95.at_ref, f32[128,128]{1,0:T(8,128)S(1)} %pad_maximum_fusion.1.after_ref, f32[64,512]{1,0:T(8,128)S(1)} %copy-done.5, f32[64,4096]{1,0:T(8,128)S(1)} %copy-done.2, ...), custom_call_target="tpu_custom_call" | custom-call | flops 1073741824 | bytes 10485760 | tf_op jit(solution)/shard_map/pallas_call | solution.py:334
  13.8 0.3 collective-permute-done.1
  14.1 0.1 collective-permute-start.2
  14.2 1.4 %collective-permute-done.2 = f32[192,256]{1,0:T(8,128)S(1)} collective-permute-done((f32[192,256]{1,0:T(8,128)S(1)}, f32[192,256]{1,0:T(8,128)S(1)}, u32[]{:S(2)}, u32[]{:S(2)}) %collective-permute-start.2) | collective-permute-done | bytes 196640 | tf_op jit(solution)/shard_map/ppermute | solution.py:275
  15.7 0.0 copy-start.6
  15.7 1.6 %collective-permute-start.3 = (f32[192,128]{1,0:T(8,128)S(1)}, f32[192,128]{1,0:T(8,128)S(1)}, u32[]{:S(2)}, u32[]{:S(2)}) collective-permute-start(f32[192,128]{1,0:T(8,128)S(1)} %slice.17), channel_id=1, source_target_pairs={{16,0},{24,8},{0,16},{8,24},{17,1},{25,9},{1,17},{9,25},{18,2},{26... | collective-permute-start | bytes 294920 | tf_op jit(solution)/shard_map/ppermute | solution.py:275
  17.3 0.0 copy-done.3
  17.3 1.9 %shard_map.97.du_ref = f32[512,128]{1,0:T(8,128)S(1)} custom-call(f32[192,256]{1,0:T(8,128)S(1)} %add.10.after_ref, f32[512,512]{1,0:T(8,128)S(1)} %copy-done.3), custom_call_target="tpu_custom_call" | custom-call | flops 2147483648 | bytes 2097152 | tf_op jit(solution)/shard_map/pallas_call | solution.py:330
  19.2 1.4 %collective-permute-done.3 = f32[192,128]{1,0:T(8,128)S(1)} collective-permute-done((f32[192,128]{1,0:T(8,128)S(1)}, f32[192,128]{1,0:T(8,128)S(1)}, u32[]{:S(2)}, u32[]{:S(2)}) %collective-permute-start.3) | collective-permute-done | bytes 98336 | tf_op jit(solution)/shard_map/ppermute | solution.py:275
  20.6 1.9 %collective-permute-start.4 = (f32[64,128]{1,0:T(8,128)S(1)}, f32[64,128]{1,0:T(8,128)S(1)}, u32[]{:S(2)}, u32[]{:S(2)}) collective-permute-start(f32[64,128]{1,0:T(8,128)S(1)} %slice.18), channel_id=1, source_target_pairs={{6,0},{7,1},{4,2},{5,3},{2,4},{3,5},{0,6},{1,7},{14,8},{15,9},{12,... | collective-permute-start | bytes 98312 | tf_op jit(solution)/shard_map/ppermute | solution.py:275
  22.5 1.2 %collective-permute-start.5 = (f32[64,128]{1,0:T(8,128)S(1)}, f32[64,128]{1,0:T(8,128)S(1)}, u32[]{:S(2)}, u32[]{:S(2)}) collective-permute-start(f32[64,128]{1,0:T(8,128)S(1)} %slice.18), channel_id=1, source_target_pairs={{4,0},{5,1},{6,2},{7,3},{0,4},{1,5},{2,6},{3,7},{12,8},{13,9},{14,... | collective-permute-start | bytes 98312 | tf_op jit(solution)/shard_map/ppermute | solution.py:275
  23.7 1.3 %collective-permute-start.6 = (f32[64,128]{1,0:T(8,128)S(1)}, f32[64,128]{1,0:T(8,128)S(1)}, u32[]{:S(2)}, u32[]{:S(2)}) collective-permute-start(f32[64,128]{1,0:T(8,128)S(1)} %slice.18), channel_id=1, source_target_pairs={{2,0},{3,1},{0,2},{1,3},{6,4},{7,5},{4,6},{5,7},{10,8},{11,9},{8,1... | collective-permute-start | bytes 98312 | tf_op jit(solution)/shard_map/ppermute | solution.py:275
  25.1 1.6 %collective-permute-start.8 = (f32[256,128]{1,0:T(8,128)S(1)}, f32[256,128]{1,0:T(8,128)S(1)}, u32[]{:S(2)}, u32[]{:S(2)}) collective-permute-start(f32[256,128]{1,0:T(8,128)S(1)} %pad_maximum_fusion), channel_id=1, source_target_pairs={{1,0},{0,1},{3,2},{2,3},{5,4},{4,5},{7,6},{6,7},{9,8},{8,9},{11,10... | collective-permute-start | bytes 393224 | tf_op jit(solution)/shard_map/ppermute | solution.py:275
  26.7 0.0 collective-permute-done.4
  26.7 0.8 %collective-permute-done.5 = f32[64,128]{1,0:T(8,128)S(1)} collective-permute-done((f32[64,128]{1,0:T(8,128)S(1)}, f32[64,128]{1,0:T(8,128)S(1)}, u32[]{:S(2)}, u32[]{:S(2)}) %collective-permute-start.5) | collective-permute-done | bytes 32800 | tf_op jit(solution)/shard_map/ppermute | solution.py:275
  27.5 2.7 %collective-permute-done.8 = f32[256,128]{1,0:T(8,128)S(1)} collective-permute-done((f32[256,128]{1,0:T(8,128)S(1)}, f32[256,128]{1,0:T(8,128)S(1)}, u32[]{:S(2)}, u32[]{:S(2)}) %collective-permute-start.8) | collective-permute-done | bytes 131104 | tf_op jit(solution)/shard_map/ppermute | solution.py:275
  30.2 1.6 %collective-permute-start.9 = (f32[512,128]{1,0:T(8,128)S(1)}, f32[512,128]{1,0:T(8,128)S(1)}, u32[]{:S(2)}, u32[]{:S(2)}) collective-permute-start(f32[512,128]{1,0:T(8,128)S(1)} %constant_dynamic-update-slice_fusion.4), channel_id=1, source_target_pairs={{16,0},{24,8},{0,16},{8,24},{17,1},{25,9},{1,17},{9,25},{18,2},{26... | collective-permute-start | bytes 786440 | tf_op jit(solution)/shard_map/ppermute | solution.py:275
  31.7 0.0 collective-permute-done.6
  31.7 1.5 %collective-permute-start.7 = (f32[256,128]{1,0:T(8,128)S(1)}, f32[256,128]{1,0:T(8,128)S(1)}, u32[]{:S(2)}, u32[]{:S(2)}) collective-permute-start(f32[256,128]{1,0:T(8,128)S(1)} %constant_dynamic-update-slice_fusion.after_ref.refs_0_), channel_id=1, source_target_pairs={{1,0},{0,1},{3,2},{2,3},{5,4},{4,5},{7,6},{6,7},{9,8},{8,9},{11,10... | collective-permute-start | bytes 393224 | tf_op jit(solution)/shard_map/ppermute | solution.py:275
  33.2 0.0 copy-done.4
  33.2 1.7 %shard_map.98.after_ref.dl_ref = f32[512,128]{1,0:T(8,128)S(1)} custom-call(f32[256,128]{1,0:T(8,128)S(1)} %constant_dynamic-update-slice_fusion.after_ref.refs_0_, f32[512,512]{1,0:T(8,128)S(1)} %copy-done.4), custom_call_target="tpu_custom_call" | custom-call | flops 2147483648 | bytes 2097152 | tf_op jit(solution)/shard_map/pallas_call | solution.py:330
  34.9 1.8 %collective-permute-done.7.refs_1_ = f32[256,128]{1,0:T(8,128)S(1)} collective-permute-done((f32[256,128]{1,0:T(8,128)S(1)}, f32[256,128]{1,0:T(8,128)S(1)}, u32[]{:S(2)}, u32[]{:S(2)}) %collective-permute-start.7) | collective-permute-done | bytes 131104 | tf_op jit(solution)/shard_map/ppermute | solution.py:275
  36.7 1.1 %shard_map.99 = (f32[128,512]{1,0:T(8,128)S(1)}, f32[64,128]{1,0:T(8,128)S(1)}) custom-call(s32[1,1]{1,0:T(1,128)} %bitcast.1.col_ref, f32[512,128]{1,0:T(8,128)S(1)} %shard_map.98.after_ref.dl_ref, f32[512,512]{1,0:T(8,128)S(1)} %copy-done.3, f32[512,128]{1,0:T(8,128)S(1)} %shard_map.97.du_ref, ...), custom_call_target="tpu_custom_call" | custom-call | flops 209715200 | bytes 2097152 | tf_op jit(solution)/shard_map/pallas_call | solution.py:370
  37.7 0.0 collective-permute-done.9
  37.8 0.1 collective-permute-start.10
  37.9 0.6 %collective-permute-start.11 = (f32[64,128]{1,0:T(8,128)S(1)}, f32[64,128]{1,0:T(8,128)S(1)}, u32[]{:S(2)}, u32[]{:S(2)}) collective-permute-start(f32[64,128]{1,0:T(8,128)S(1)} %get-tuple-element.27.refs_0_), channel_id=1, source_target_pairs={{24,0},{16,8},{8,16},{0,24},{25,1},{17,9},{9,17},{1,25},{26,2},{18... | collective-permute-start | bytes 98312 | tf_op jit(solution)/shard_map/ppermute | solution.py:275
  38.5 1.5 %collective-permute-start.12 = (f32[64,128]{1,0:T(8,128)S(1)}, f32[64,128]{1,0:T(8,128)S(1)}, u32[]{:S(2)}, u32[]{:S(2)}) collective-permute-start(f32[64,128]{1,0:T(8,128)S(1)} %get-tuple-element.27.refs_0_), channel_id=1, source_target_pairs={{16,0},{24,8},{0,16},{8,24},{17,1},{25,9},{1,17},{9,25},{18,2},{26... | collective-permute-start | bytes 98312 | tf_op jit(solution)/shard_map/ppermute | solution.py:275
  40.0 0.0 collective-permute-start.13
  40.0 0.0 collective-permute-done.10.refs_1_
  40.0 0.0 copy-done.6
  40.0 2.6 %shard_map.100.after_ref = f32[128,128]{1,0:T(8,128)} custom-call(s32[1,1]{1,0:T(1,128)} %bitcast.1.col_ref, s32[1,1]{1,0:T(1,128)} %bitcast.row_ref, f32[128,512]{1,0:T(8,128)S(1)} %get-tuple-element.24.yt_ref, f32[512,512]{1,0:T(8,128)S(1)} %copy-done.4, f32[512,128]{1,0:T(8,128)S(1)} %shard_map.98.after_ref.dl_ref, f32[128,512]{1,0:T(8,128)S(1)} %shard_map.95.at_ref, ...), custom_call_target="tpu_custom_call" | custom-call | flops 419430400 | bytes 4194304 | tf_op jit(solution)/shard_map/pallas_call | solution.py:384
  42.6 0.0 collective-permute-done.11.refs_1_
  42.6 0.0 collective-permute-done.12.refs_2_
  42.6 0.0 collective-permute-done.13.refs_3_
  42.6 0.7 %shard_map.101 = f32[64,512]{1,0:T(8,128)} custom-call(s32[1,1]{1,0:T(1,128)} %bitcast.row_ref, f32[128,128]{1,0:T(8,128)} %shard_map.100.after_ref, f32[64,128]{1,0:T(8,128)S(1)} %get-tuple-element.27.refs_0_, f32[64,128]{1,0:T(8,128)S(1)} %collective-permute-done.11.refs_1_, f32[64,128]{1,0:T(8,128)S(1)} %collective-permute-done.12.refs_2_, ...), custom_call_target="tpu_custom_call" | custom-call | bytes 131072 | tf_op jit(solution)/shard_map/pallas_call | solution.py:399
  (16 shorter events, 0.2 us)
Async XLA Ops:
  0.6 0.9 %copy-start = (f32[64,512]{1,0:T(8,128)S(1)}, f32[64,512]{1,0:T(8,128)}, u32[]{:S(2)}) copy-start(f32[64,512]{1,0:T(8,128)} %param.13) | copy-start | bytes 393220
  1.5 8.2 %collective-permute-start = (f32[64,128]{1,0:T(8,128)S(1)}, f32[64,128]{1,0:T(8,128)S(1)}, u32[]{:S(2)}, u32[]{:S(2)}) collective-permute-start(f32[64,128]{1,0:T(8,128)S(1)} %constant_dynamic-slice_fusion), channel_id=1, source_target_pairs={{4,0},{5,1},{6,2},{7,3},{0,4},{1,5},{2,6},{3,7},{12,8},{13,9},{14,... | collective-permute-start | bytes 98312 | tf_op jit(solution)/shard_map/ppermute | solution.py:275
  5.6 5.8 %copy-start.1 = (f32[4096,512]{1,0:T(8,128)S(1)}, f32[4096,512]{1,0:T(8,128)}, u32[]{:S(2)}) copy-start(f32[4096,512]{1,0:T(8,128)} %y_ref.1) | copy-start | bytes 25165828
  5.6 5.8 %copy-start.2 = (f32[64,4096]{1,0:T(8,128)S(1)}, f32[64,4096]{1,0:T(8,128)}, u32[]{:S(2)}) copy-start(f32[64,4096]{1,0:T(8,128)} %u_cols_ref.1) | copy-start | bytes 3145732
  5.6 5.8 %copy-start.5 = (f32[64,512]{1,0:T(8,128)S(1)}, f32[64,512]{1,0:T(8,128)}, u32[]{:S(2)}) copy-start(f32[64,512]{1,0:T(8,128)} %b_ref.1) | copy-start | bytes 393220
  9.7 7.5 %copy-start.3 = (f32[512,512]{1,0:T(8,128)S(1)}, f32[512,512]{1,0:T(8,128)}, u32[]{:S(2)}) copy-start(f32[512,512]{1,0:T(8,128)} %u_ref.3) | copy-start | bytes 3145732
  9.8 4.3 %collective-permute-start.1 = (f32[128,128]{1,0:T(8,128)S(1)}, f32[128,128]{1,0:T(8,128)S(1)}, u32[]{:S(2)}, u32[]{:S(2)}) collective-permute-start(f32[128,128]{1,0:T(8,128)S(1)} %pad_maximum_fusion.1.after_ref), channel_id=1, source_target_pairs={{2,0},{3,1},{0,2},{1,3},{6,4},{7,5},{4,6},{5,7},{10,8},{11,9},{8,1... | collective-permute-start | bytes 196616 | tf_op jit(solution)/shard_map/ppermute | solution.py:275
  11.4 21.8 %copy-start.4 = (f32[512,512]{1,0:T(8,128)S(1)}, f32[512,512]{1,0:T(8,128)}, u32[]{:S(2)}) copy-start(f32[512,512]{1,0:T(8,128)} %l_ref.3) | copy-start | bytes 3145732
  14.1 1.5 %collective-permute-start.2 = (f32[192,256]{1,0:T(8,128)S(1)}, f32[192,256]{1,0:T(8,128)S(1)}, u32[]{:S(2)}, u32[]{:S(2)}) collective-permute-start(f32[192,256]{1,0:T(8,128)S(1)} %get-tuple-element.18), channel_id=1, source_target_pairs={{8,0},{0,8},{24,16},{16,24},{9,1},{1,9},{25,17},{17,25},{10,2},{2,... | collective-permute-start | bytes 589832 | tf_op jit(solution)/shard_map/ppermute | solution.py:275
  15.7 24.4 %copy-start.6 = (s32[128]{0:T(128)S(1)}, s32[128]{0:T(128)}, u32[]{:S(2)}) copy-start(s32[128]{0:T(128)} %param.15) | copy-start | bytes 1540
  15.7 4.9 %collective-permute-start.3 = (f32[192,128]{1,0:T(8,128)S(1)}, f32[192,128]{1,0:T(8,128)S(1)}, u32[]{:S(2)}, u32[]{:S(2)}) collective-permute-start(f32[192,128]{1,0:T(8,128)S(1)} %slice.17), channel_id=1, source_target_pairs={{16,0},{24,8},{0,16},{8,24},{17,1},{25,9},{1,17},{9,25},{18,2},{26... | collective-permute-start | bytes 294920 | tf_op jit(solution)/shard_map/ppermute | solution.py:275
  20.6 6.1 %collective-permute-start.4 = (f32[64,128]{1,0:T(8,128)S(1)}, f32[64,128]{1,0:T(8,128)S(1)}, u32[]{:S(2)}, u32[]{:S(2)}) collective-permute-start(f32[64,128]{1,0:T(8,128)S(1)} %slice.18), channel_id=1, source_target_pairs={{6,0},{7,1},{4,2},{5,3},{2,4},{3,5},{0,6},{1,7},{14,8},{15,9},{12,... | collective-permute-start | bytes 98312 | tf_op jit(solution)/shard_map/ppermute | solution.py:275
  22.5 5.0 %collective-permute-start.5 = (f32[64,128]{1,0:T(8,128)S(1)}, f32[64,128]{1,0:T(8,128)S(1)}, u32[]{:S(2)}, u32[]{:S(2)}) collective-permute-start(f32[64,128]{1,0:T(8,128)S(1)} %slice.18), channel_id=1, source_target_pairs={{4,0},{5,1},{6,2},{7,3},{0,4},{1,5},{2,6},{3,7},{12,8},{13,9},{14,... | collective-permute-start | bytes 98312 | tf_op jit(solution)/shard_map/ppermute | solution.py:275
  23.7 8.0 %collective-permute-start.6 = (f32[64,128]{1,0:T(8,128)S(1)}, f32[64,128]{1,0:T(8,128)S(1)}, u32[]{:S(2)}, u32[]{:S(2)}) collective-permute-start(f32[64,128]{1,0:T(8,128)S(1)} %slice.18), channel_id=1, source_target_pairs={{2,0},{3,1},{0,2},{1,3},{6,4},{7,5},{4,6},{5,7},{10,8},{11,9},{8,1... | collective-permute-start | bytes 98312 | tf_op jit(solution)/shard_map/ppermute | solution.py:275
  25.1 5.0 %collective-permute-start.8 = (f32[256,128]{1,0:T(8,128)S(1)}, f32[256,128]{1,0:T(8,128)S(1)}, u32[]{:S(2)}, u32[]{:S(2)}) collective-permute-start(f32[256,128]{1,0:T(8,128)S(1)} %pad_maximum_fusion), channel_id=1, source_target_pairs={{1,0},{0,1},{3,2},{2,3},{5,4},{4,5},{7,6},{6,7},{9,8},{8,9},{11,10... | collective-permute-start | bytes 393224 | tf_op jit(solution)/shard_map/ppermute | solution.py:275
  30.2 7.6 %collective-permute-start.9 = (f32[512,128]{1,0:T(8,128)S(1)}, f32[512,128]{1,0:T(8,128)S(1)}, u32[]{:S(2)}, u32[]{:S(2)}) collective-permute-start(f32[512,128]{1,0:T(8,128)S(1)} %constant_dynamic-update-slice_fusion.4), channel_id=1, source_target_pairs={{16,0},{24,8},{0,16},{8,24},{17,1},{25,9},{1,17},{9,25},{18,2},{26... | collective-permute-start | bytes 786440 | tf_op jit(solution)/shard_map/ppermute | solution.py:275
  31.7 5.0 %collective-permute-start.7 = (f32[256,128]{1,0:T(8,128)S(1)}, f32[256,128]{1,0:T(8,128)S(1)}, u32[]{:S(2)}, u32[]{:S(2)}) collective-permute-start(f32[256,128]{1,0:T(8,128)S(1)} %constant_dynamic-update-slice_fusion.after_ref.refs_0_), channel_id=1, source_target_pairs={{1,0},{0,1},{3,2},{2,3},{5,4},{4,5},{7,6},{6,7},{9,8},{8,9},{11,10... | collective-permute-start | bytes 393224 | tf_op jit(solution)/shard_map/ppermute | solution.py:275
  37.8 2.2 %collective-permute-start.10 = (f32[512,256]{1,0:T(8,128)S(1)}, f32[512,256]{1,0:T(8,128)S(1)}, u32[]{:S(2)}, u32[]{:S(2)}) collective-permute-start(f32[512,256]{1,0:T(8,128)S(1)} %constant_dynamic-update-slice_fusion.6.refs_0_), channel_id=1, source_target_pairs={{8,0},{0,8},{24,16},{16,24},{9,1},{1,9},{25,17},{17,25},{10,2},{2,... | collective-permute-start | bytes 1572872 | tf_op jit(solution)/shard_map/ppermute | solution.py:275
  37.9 4.7 %collective-permute-start.11 = (f32[64,128]{1,0:T(8,128)S(1)}, f32[64,128]{1,0:T(8,128)S(1)}, u32[]{:S(2)}, u32[]{:S(2)}) collective-permute-start(f32[64,128]{1,0:T(8,128)S(1)} %get-tuple-element.27.refs_0_), channel_id=1, source_target_pairs={{24,0},{16,8},{8,16},{0,24},{25,1},{17,9},{9,17},{1,25},{26,2},{18... | collective-permute-start | bytes 98312 | tf_op jit(solution)/shard_map/ppermute | solution.py:275
  38.5 4.1 %collective-permute-start.12 = (f32[64,128]{1,0:T(8,128)S(1)}, f32[64,128]{1,0:T(8,128)S(1)}, u32[]{:S(2)}, u32[]{:S(2)}) collective-permute-start(f32[64,128]{1,0:T(8,128)S(1)} %get-tuple-element.27.refs_0_), channel_id=1, source_target_pairs={{16,0},{24,8},{0,16},{8,24},{17,1},{25,9},{1,17},{9,25},{18,2},{26... | collective-permute-start | bytes 98312 | tf_op jit(solution)/shard_map/ppermute | solution.py:275
  40.0 2.6 %collective-permute-start.13 = (f32[64,128]{1,0:T(8,128)S(1)}, f32[64,128]{1,0:T(8,128)S(1)}, u32[]{:S(2)}, u32[]{:S(2)}) collective-permute-start(f32[64,128]{1,0:T(8,128)S(1)} %get-tuple-element.27.refs_0_), channel_id=1, source_target_pairs={{8,0},{0,8},{24,16},{16,24},{9,1},{1,9},{25,17},{17,25},{10,2},{2,... | collective-permute-start | bytes 98312 | tf_op jit(solution)/shard_map/ppermute | solution.py:275

commit v9 on v7

--- a/solution.py
+++ b/solution.py
@@ -238,11 +238,15 @@
     x_ref[...] = total.T + v_ref[...]
 
 
+def partners(size):
+    return [0, *range(2, size, 2), *range(size - 1, 0, -2)]
+
+
 def merge_kernel(row_ref, after_ref, *refs):
     del after_ref
     out_ref = refs[-1]
     for step, ref in enumerate(refs[:-1]):
-        out_ref[:, aligned_span(row_ref[0, 0] ^ ((len(refs) - 1 - step) % (len(refs) - 1)), ref.shape[1])] = ref[...]
+        out_ref[:, aligned_span(row_ref[0, 0] ^ partners(len(refs) - 1)[step], ref.shape[1])] = ref[...]
 
 
 def call(kernel, outs, flops, bytes_accessed, limit, scratch=(), **specs):
@@ -396,7 +400,7 @@
     )(col_at, row_at, yt, l_diag, dl, at, perm_row, v, *coupling)
 
     if paired:
-        blocks = [y_mine] + [swapped(y_mine, "row", row_size, step) for step in range(row_size - 1, 0, -1)]
+        blocks = [y_mine] + [swapped(y_mine, "row", row_size, step) for step in partners(row_size)[1:]]
         y_part = call(
             merge_kernel,
             shape(share, columns),

time: 40.3 us -> 39.7 us (0.985)
  waiting for transfers between devices: 5.59 us -> 4.93 us
    ppermute x14, waiting for transfers between devices: 5.59 us -> 4.93 us  [swapped(): return lax.ppermute(value, axis, [(dst ^ mask, dst) for dst in range(size)])]
  transfers between devices with their start and end apart: 14 -> 14, of which waited for: 6 -> 5; matrix products, arithmetic and copies ran while one was open for 0% -> 0% of each run, Pallas kernels for 34% -> 35%
where the time goes in v9:
time: 39.7 us; the launch traced here: 39.6 us
  starting transfers between devices  18.4 us (46%)
  Pallas kernels  14.4 us (36%)
  waiting for transfers between devices  4.93 us (12%)
  local copies, waits for them, and re-layouts  1.02 us (3%)
  between operations  0.82 us (2%)
    ppermute x14, starting transfers between devices, swapped(): return lax.ppermute(value, axis, [(dst ^ mask, dst) for dst in range(size)])  18.4 us
    ppermute x14, waiting for transfers between devices, swapped(): return lax.ppermute(value, axis, [(dst ^ mask, dst) for dst in range(size)])  4.93 us
    pallas_call x1, Pallas kernels, per_device(): call(solve_selected_kernel, shape(lanes, width), 6 << 30, 2 << 20, 8, scr...  4.15 us
    pallas_call x2, Pallas kernels, per_device(): call(kernel, shape(width, TILE), 2 << 30, 2 << 20, 8, in_specs=[ANY, VMEM...  3.59 us
    pallas_call x1, Pallas kernels, per_device(): call(functools.partial(finish_kernel, inner, outer, share, parts), shape(...  2.55 us
    pallas_call x1, Pallas kernels, per_device(): call(functools.partial(product_kernel, row_size, paired), outs, 1 << 30,...  2.34 us
    pallas_call x1, Pallas kernels, per_device(): call(functools.partial(solve_u_kernel, inner, outer, share), (shape(rhs,...  1.05 us
    unnamed x19, local copies, waits for them, and re-layouts  0.96 us
  transfers between devices with their start and end apart: 14, of which 5 were waited for; matrix products, arithmetic and copies ran while one was open for 0% of the time, Pallas kernels for 35%

profile of v9, /device:TPU:0, one launch (start us, length us, event | category | flops | bytes accessed | tf_op | source)
XLA Modules:
  0.0 39.6 jit_solution(489303705544358091)
XLA Ops:
  0.6 0.0 copy-start
  0.7 0.9 %copy-done = f32[64,512]{1,0:T(8,128)S(1)} copy-done((f32[64,512]{1,0:T(8,128)S(1)}, f32[64,512]{1,0:T(8,128)}, u32[]{:S(2)}) %copy-start) | copy-done | bytes 131096
  1.5 4.0 %collective-permute-start = (f32[64,128]{1,0:T(8,128)S(1)}, f32[64,128]{1,0:T(8,128)S(1)}, u32[]{:S(2)}, u32[]{:S(2)}) collective-permute-start(f32[64,128]{1,0:T(8,128)S(1)} %constant_dynamic-slice_fusion), channel_id=1, source_target_pairs={{4,0},{5,1},{6,2},{7,3},{0,4},{1,5},{2,6},{3,7},{12,8},{13,9},{14,... | collective-permute-start | bytes 98312 | tf_op jit(solution)/shard_map/ppermute | solution.py:279
  5.6 0.0 copy-start.1
  5.6 0.0 copy-start.2
  5.6 0.0 copy-start.5
  5.6 4.1 %shard_map.95.at_ref = f32[128,512]{1,0:T(8,128)S(1)} custom-call(s32[1,128]{1,0:T(1,128)} %bitcast.3, f32[512,512]{1,0:T(8,128)} %lp_hbm.1), custom_call_target="tpu_custom_call" | custom-call | flops 6442450944 | bytes 2097152 | tf_op jit(solution)/shard_map/pallas_call | solution.py:319
  9.7 0.0 copy-start.3
  9.8 0.0 collective-permute-done
  9.8 1.6 %collective-permute-start.1 = (f32[128,128]{1,0:T(8,128)S(1)}, f32[128,128]{1,0:T(8,128)S(1)}, u32[]{:S(2)}, u32[]{:S(2)}) collective-permute-start(f32[128,128]{1,0:T(8,128)S(1)} %pad_maximum_fusion.1.after_ref), channel_id=1, source_target_pairs={{2,0},{3,1},{0,2},{1,3},{6,4},{7,5},{4,6},{5,7},{10,8},{11,9},{8,1... | collective-permute-start | bytes 196616 | tf_op jit(solution)/shard_map/ppermute | solution.py:279
  11.4 0.0 copy-done.1
  11.4 0.0 copy-done.2
  11.4 0.0 copy-done.5
  11.4 0.0 copy-start.4
  11.4 2.3 %shard_map.96 = (f32[192,256]{1,0:T(8,128)S(1)}, f32[192,256]{1,0:T(8,128)S(1)}) custom-call(s32[1,1]{1,0:T(1,128)} %bitcast.row_ref, f32[128,512]{1,0:T(8,128)S(1)} %shard_map.95.at_ref, f32[128,128]{1,0:T(8,128)S(1)} %pad_maximum_fusion.1.after_ref, f32[64,512]{1,0:T(8,128)S(1)} %copy-done.5, f32[64,4096]{1,0:T(8,128)S(1)} %copy-done.2, ...), custom_call_target="tpu_custom_call" | custom-call | flops 1073741824 | bytes 10485760 | tf_op jit(solution)/shard_map/pallas_call | solution.py:338
  13.8 0.3 collective-permute-done.1
  14.1 0.1 collective-permute-start.2
  14.2 1.4 %collective-permute-done.2 = f32[192,256]{1,0:T(8,128)S(1)} collective-permute-done((f32[192,256]{1,0:T(8,128)S(1)}, f32[192,256]{1,0:T(8,128)S(1)}, u32[]{:S(2)}, u32[]{:S(2)}) %collective-permute-start.2) | collective-permute-done | bytes 196640 | tf_op jit(solution)/shard_map/ppermute | solution.py:279
  15.7 0.0 copy-start.6
  15.7 1.6 %collective-permute-start.3 = (f32[192,128]{1,0:T(8,128)S(1)}, f32[192,128]{1,0:T(8,128)S(1)}, u32[]{:S(2)}, u32[]{:S(2)}) collective-permute-start(f32[192,128]{1,0:T(8,128)S(1)} %slice.13), channel_id=1, source_target_pairs={{16,0},{24,8},{0,16},{8,24},{17,1},{25,9},{1,17},{9,25},{18,2},{26... | collective-permute-start | bytes 294920 | tf_op jit(solution)/shard_map/ppermute | solution.py:279
  17.3 0.0 copy-done.3
  17.3 1.9 %shard_map.97.du_ref = f32[512,128]{1,0:T(8,128)S(1)} custom-call(f32[192,256]{1,0:T(8,128)S(1)} %add.10.after_ref, f32[512,512]{1,0:T(8,128)S(1)} %copy-done.3), custom_call_target="tpu_custom_call" | custom-call | flops 2147483648 | bytes 2097152 | tf_op jit(solution)/shard_map/pallas_call | solution.py:334
  19.2 1.6 %collective-permute-start.8 = (f32[256,128]{1,0:T(8,128)S(1)}, f32[256,128]{1,0:T(8,128)S(1)}, u32[]{:S(2)}, u32[]{:S(2)}) collective-permute-start(f32[256,128]{1,0:T(8,128)S(1)} %pad_maximum_fusion), channel_id=1, source_target_pairs={{1,0},{0,1},{3,2},{2,3},{5,4},{4,5},{7,6},{6,7},{9,8},{8,9},{11,10... | collective-permute-start | bytes 393224 | tf_op jit(solution)/shard_map/ppermute | solution.py:279
  20.8 0.0 collective-permute-done.3
  20.8 1.9 %collective-permute-start.4 = (f32[64,128]{1,0:T(8,128)S(1)}, f32[64,128]{1,0:T(8,128)S(1)}, u32[]{:S(2)}, u32[]{:S(2)}) collective-permute-start(f32[64,128]{1,0:T(8,128)S(1)} %slice.16), channel_id=1, source_target_pairs={{6,0},{7,1},{4,2},{5,3},{2,4},{3,5},{0,6},{1,7},{14,8},{15,9},{12,... | collective-permute-start | bytes 98312 | tf_op jit(solution)/shard_map/ppermute | solution.py:279
  22.7 1.2 %collective-permute-start.5 = (f32[64,128]{1,0:T(8,128)S(1)}, f32[64,128]{1,0:T(8,128)S(1)}, u32[]{:S(2)}, u32[]{:S(2)}) collective-permute-start(f32[64,128]{1,0:T(8,128)S(1)} %slice.16), channel_id=1, source_target_pairs={{4,0},{5,1},{6,2},{7,3},{0,4},{1,5},{2,6},{3,7},{12,8},{13,9},{14,... | collective-permute-start | bytes 98312 | tf_op jit(solution)/shard_map/ppermute | solution.py:279
  23.9 1.3 %collective-permute-start.6 = (f32[64,128]{1,0:T(8,128)S(1)}, f32[64,128]{1,0:T(8,128)S(1)}, u32[]{:S(2)}, u32[]{:S(2)}) collective-permute-start(f32[64,128]{1,0:T(8,128)S(1)} %slice.16), channel_id=1, source_target_pairs={{2,0},{3,1},{0,2},{1,3},{6,4},{7,5},{4,6},{5,7},{10,8},{11,9},{8,1... | collective-permute-start | bytes 98312 | tf_op jit(solution)/shard_map/ppermute | solution.py:279
  25.3 0.0 collective-permute-done.8
  25.3 1.4 %collective-permute-start.9 = (f32[512,128]{1,0:T(8,128)S(1)}, f32[512,128]{1,0:T(8,128)S(1)}, u32[]{:S(2)}, u32[]{:S(2)}) collective-permute-start(f32[512,128]{1,0:T(8,128)S(1)} %constant_dynamic-update-slice_fusion.4), channel_id=1, source_target_pairs={{16,0},{24,8},{0,16},{8,24},{17,1},{25,9},{1,17},{9,25},{18,2},{26... | collective-permute-start | bytes 786440 | tf_op jit(solution)/shard_map/ppermute | solution.py:279
  26.7 0.0 collective-permute-done.4
  26.7 0.9 %collective-permute-done.5 = f32[64,128]{1,0:T(8,128)S(1)} collective-permute-done((f32[64,128]{1,0:T(8,128)S(1)}, f32[64,128]{1,0:T(8,128)S(1)}, u32[]{:S(2)}, u32[]{:S(2)}) %collective-permute-start.5) | collective-permute-done | bytes 32800 | tf_op jit(solution)/shard_map/ppermute | solution.py:279
  27.6 0.3 collective-permute-done.6
  27.9 1.4 %collective-permute-start.7 = (f32[256,128]{1,0:T(8,128)S(1)}, f32[256,128]{1,0:T(8,128)S(1)}, u32[]{:S(2)}, u32[]{:S(2)}) collective-permute-start(f32[256,128]{1,0:T(8,128)S(1)} %constant_dynamic-update-slice_fusion.after_ref.refs_0_), channel_id=1, source_target_pairs={{1,0},{0,1},{3,2},{2,3},{5,4},{4,5},{7,6},{6,7},{9,8},{8,9},{11,10... | collective-permute-start | bytes 393224 | tf_op jit(solution)/shard_map/ppermute | solution.py:279
  29.3 0.0 copy-done.4
  29.3 1.7 %shard_map.98.after_ref.dl_ref = f32[512,128]{1,0:T(8,128)S(1)} custom-call(f32[256,128]{1,0:T(8,128)S(1)} %constant_dynamic-update-slice_fusion.after_ref.refs_0_, f32[512,512]{1,0:T(8,128)S(1)} %copy-done.4), custom_call_target="tpu_custom_call" | custom-call | flops 2147483648 | bytes 2097152 | tf_op jit(solution)/shard_map/pallas_call | solution.py:334
  31.0 1.9 %collective-permute-done.7.refs_1_ = f32[256,128]{1,0:T(8,128)S(1)} collective-permute-done((f32[256,128]{1,0:T(8,128)S(1)}, f32[256,128]{1,0:T(8,128)S(1)}, u32[]{:S(2)}, u32[]{:S(2)}) %collective-permute-start.7) | collective-permute-done | bytes 131104 | tf_op jit(solution)/shard_map/ppermute | solution.py:279
  32.9 1.1 %shard_map.99 = (f32[128,512]{1,0:T(8,128)S(1)}, f32[64,128]{1,0:T(8,128)S(1)}) custom-call(s32[1,1]{1,0:T(1,128)} %bitcast.1.col_ref, f32[512,128]{1,0:T(8,128)S(1)} %shard_map.98.after_ref.dl_ref, f32[512,512]{1,0:T(8,128)S(1)} %copy-done.3, f32[512,128]{1,0:T(8,128)S(1)} %shard_map.97.du_ref, ...), custom_call_target="tpu_custom_call" | custom-call | flops 209715200 | bytes 2097152 | tf_op jit(solution)/shard_map/pallas_call | solution.py:375
  34.0 0.0 collective-permute-done.9
  34.0 0.1 collective-permute-start.10
  34.1 1.4 %collective-permute-start.11 = (f32[64,128]{1,0:T(8,128)S(1)}, f32[64,128]{1,0:T(8,128)S(1)}, u32[]{:S(2)}, u32[]{:S(2)}) collective-permute-start(f32[64,128]{1,0:T(8,128)S(1)} %get-tuple-element.29.refs_0_), channel_id=1, source_target_pairs={{16,0},{24,8},{0,16},{8,24},{17,1},{25,9},{1,17},{9,25},{18,2},{26... | collective-permute-start | bytes 98312 | tf_op jit(solution)/shard_map/ppermute | solution.py:279
  35.6 0.4 %collective-permute-start.12 = (f32[64,128]{1,0:T(8,128)S(1)}, f32[64,128]{1,0:T(8,128)S(1)}, u32[]{:S(2)}, u32[]{:S(2)}) collective-permute-start(f32[64,128]{1,0:T(8,128)S(1)} %get-tuple-element.29.refs_0_), channel_id=1, source_target_pairs={{24,0},{16,8},{8,16},{0,24},{25,1},{17,9},{9,17},{1,25},{26,2},{18... | collective-permute-start | bytes 98312 | tf_op jit(solution)/shard_map/ppermute | solution.py:279
  36.0 0.4 collective-permute-start.13
  36.3 0.0 collective-permute-done.10.refs_1_
  36.3 0.0 copy-done.6
  36.3 2.6 %shard_map.100.after_ref = f32[128,128]{1,0:T(8,128)} custom-call(s32[1,1]{1,0:T(1,128)} %bitcast.1.col_ref, s32[1,1]{1,0:T(1,128)} %bitcast.row_ref, f32[128,512]{1,0:T(8,128)S(1)} %get-tuple-element.26.yt_ref, f32[512,512]{1,0:T(8,128)S(1)} %copy-done.4, f32[512,128]{1,0:T(8,128)S(1)} %shard_map.98.after_ref.dl_ref, f32[128,512]{1,0:T(8,128)S(1)} %shard_map.95.at_ref, ...), custom_call_target="tpu_custom_call" | custom-call | flops 419430400 | bytes 4194304 | tf_op jit(solution)/shard_map/pallas_call | solution.py:389
  38.9 0.0 collective-permute-done.11.refs_1_
  38.9 0.0 collective-permute-done.12.refs_2_
  38.9 0.0 collective-permute-done.13.refs_3_
  38.9 0.7 %shard_map.101 = f32[64,512]{1,0:T(8,128)} custom-call(s32[1,1]{1,0:T(1,128)} %bitcast.row_ref, f32[128,128]{1,0:T(8,128)} %shard_map.100.after_ref, f32[64,128]{1,0:T(8,128)S(1)} %get-tuple-element.29.refs_0_, f32[64,128]{1,0:T(8,128)S(1)} %collective-permute-done.11.refs_1_, f32[64,128]{1,0:T(8,128)S(1)} %collective-permute-done.12.refs_2_, ...), custom_call_target="tpu_custom_call" | custom-call | bytes 131072 | tf_op jit(solution)/shard_map/pallas_call | solution.py:404
  (16 shorter events, 0.2 us)
Async XLA Ops:
  0.6 0.9 %copy-start = (f32[64,512]{1,0:T(8,128)S(1)}, f32[64,512]{1,0:T(8,128)}, u32[]{:S(2)}) copy-start(f32[64,512]{1,0:T(8,128)} %param.13) | copy-start | bytes 393220
  1.5 8.2 %collective-permute-start = (f32[64,128]{1,0:T(8,128)S(1)}, f32[64,128]{1,0:T(8,128)S(1)}, u32[]{:S(2)}, u32[]{:S(2)}) collective-permute-start(f32[64,128]{1,0:T(8,128)S(1)} %constant_dynamic-slice_fusion), channel_id=1, source_target_pairs={{4,0},{5,1},{6,2},{7,3},{0,4},{1,5},{2,6},{3,7},{12,8},{13,9},{14,... | collective-permute-start | bytes 98312 | tf_op jit(solution)/shard_map/ppermute | solution.py:279
  5.6 5.8 %copy-start.1 = (f32[4096,512]{1,0:T(8,128)S(1)}, f32[4096,512]{1,0:T(8,128)}, u32[]{:S(2)}) copy-start(f32[4096,512]{1,0:T(8,128)} %y_ref.1) | copy-start | bytes 25165828
  5.6 5.8 %copy-start.2 = (f32[64,4096]{1,0:T(8,128)S(1)}, f32[64,4096]{1,0:T(8,128)}, u32[]{:S(2)}) copy-start(f32[64,4096]{1,0:T(8,128)} %u_cols_ref.1) | copy-start | bytes 3145732
  5.6 5.8 %copy-start.5 = (f32[64,512]{1,0:T(8,128)S(1)}, f32[64,512]{1,0:T(8,128)}, u32[]{:S(2)}) copy-start(f32[64,512]{1,0:T(8,128)} %b_ref.1) | copy-start | bytes 393220
  9.7 7.5 %copy-start.3 = (f32[512,512]{1,0:T(8,128)S(1)}, f32[512,512]{1,0:T(8,128)}, u32[]{:S(2)}) copy-start(f32[512,512]{1,0:T(8,128)} %u_ref.3) | copy-start | bytes 3145732
  9.8 4.3 %collective-permute-start.1 = (f32[128,128]{1,0:T(8,128)S(1)}, f32[128,128]{1,0:T(8,128)S(1)}, u32[]{:S(2)}, u32[]{:S(2)}) collective-permute-start(f32[128,128]{1,0:T(8,128)S(1)} %pad_maximum_fusion.1.after_ref), channel_id=1, source_target_pairs={{2,0},{3,1},{0,2},{1,3},{6,4},{7,5},{4,6},{5,7},{10,8},{11,9},{8,1... | collective-permute-start | bytes 196616 | tf_op jit(solution)/shard_map/ppermute | solution.py:279
  11.4 17.9 %copy-start.4 = (f32[512,512]{1,0:T(8,128)S(1)}, f32[512,512]{1,0:T(8,128)}, u32[]{:S(2)}) copy-start(f32[512,512]{1,0:T(8,128)} %l_ref.3) | copy-start | bytes 3145732
  14.1 1.5 %collective-permute-start.2 = (f32[192,256]{1,0:T(8,128)S(1)}, f32[192,256]{1,0:T(8,128)S(1)}, u32[]{:S(2)}, u32[]{:S(2)}) collective-permute-start(f32[192,256]{1,0:T(8,128)S(1)} %get-tuple-element.19), channel_id=1, source_target_pairs={{8,0},{0,8},{24,16},{16,24},{9,1},{1,9},{25,17},{17,25},{10,2},{2,... | collective-permute-start | bytes 589832 | tf_op jit(solution)/shard_map/ppermute | solution.py:279
  15.7 20.6 %copy-start.6 = (s32[128]{0:T(128)S(1)}, s32[128]{0:T(128)}, u32[]{:S(2)}) copy-start(s32[128]{0:T(128)} %param.15) | copy-start | bytes 1540
  15.7 5.1 %collective-permute-start.3 = (f32[192,128]{1,0:T(8,128)S(1)}, f32[192,128]{1,0:T(8,128)S(1)}, u32[]{:S(2)}, u32[]{:S(2)}) collective-permute-start(f32[192,128]{1,0:T(8,128)S(1)} %slice.13), channel_id=1, source_target_pairs={{16,0},{24,8},{0,16},{8,24},{17,1},{25,9},{1,17},{9,25},{18,2},{26... | collective-permute-start | bytes 294920 | tf_op jit(solution)/shard_map/ppermute | solution.py:279
  19.2 6.1 %collective-permute-start.8 = (f32[256,128]{1,0:T(8,128)S(1)}, f32[256,128]{1,0:T(8,128)S(1)}, u32[]{:S(2)}, u32[]{:S(2)}) collective-permute-start(f32[256,128]{1,0:T(8,128)S(1)} %pad_maximum_fusion), channel_id=1, source_target_pairs={{1,0},{0,1},{3,2},{2,3},{5,4},{4,5},{7,6},{6,7},{9,8},{8,9},{11,10... | collective-permute-start | bytes 393224 | tf_op jit(solution)/shard_map/ppermute | solution.py:279
  20.8 5.9 %collective-permute-start.4 = (f32[64,128]{1,0:T(8,128)S(1)}, f32[64,128]{1,0:T(8,128)S(1)}, u32[]{:S(2)}, u32[]{:S(2)}) collective-permute-start(f32[64,128]{1,0:T(8,128)S(1)} %slice.16), channel_id=1, source_target_pairs={{6,0},{7,1},{4,2},{5,3},{2,4},{3,5},{0,6},{1,7},{14,8},{15,9},{12,... | collective-permute-start | bytes 98312 | tf_op jit(solution)/shard_map/ppermute | solution.py:279
  22.7 4.9 %collective-permute-start.5 = (f32[64,128]{1,0:T(8,128)S(1)}, f32[64,128]{1,0:T(8,128)S(1)}, u32[]{:S(2)}, u32[]{:S(2)}) collective-permute-start(f32[64,128]{1,0:T(8,128)S(1)} %slice.16), channel_id=1, source_target_pairs={{4,0},{5,1},{6,2},{7,3},{0,4},{1,5},{2,6},{3,7},{12,8},{13,9},{14,... | collective-permute-start | bytes 98312 | tf_op jit(solution)/shard_map/ppermute | solution.py:279
  23.9 4.0 %collective-permute-start.6 = (f32[64,128]{1,0:T(8,128)S(1)}, f32[64,128]{1,0:T(8,128)S(1)}, u32[]{:S(2)}, u32[]{:S(2)}) collective-permute-start(f32[64,128]{1,0:T(8,128)S(1)} %slice.16), channel_id=1, source_target_pairs={{2,0},{3,1},{0,2},{1,3},{6,4},{7,5},{4,6},{5,7},{10,8},{11,9},{8,1... | collective-permute-start | bytes 98312 | tf_op jit(solution)/shard_map/ppermute | solution.py:279
  25.3 8.7 %collective-permute-start.9 = (f32[512,128]{1,0:T(8,128)S(1)}, f32[512,128]{1,0:T(8,128)S(1)}, u32[]{:S(2)}, u32[]{:S(2)}) collective-permute-start(f32[512,128]{1,0:T(8,128)S(1)} %constant_dynamic-update-slice_fusion.4), channel_id=1, source_target_pairs={{16,0},{24,8},{0,16},{8,24},{17,1},{25,9},{1,17},{9,25},{18,2},{26... | collective-permute-start | bytes 786440 | tf_op jit(solution)/shard_map/ppermute | solution.py:279
  27.9 5.0 %collective-permute-start.7 = (f32[256,128]{1,0:T(8,128)S(1)}, f32[256,128]{1,0:T(8,128)S(1)}, u32[]{:S(2)}, u32[]{:S(2)}) collective-permute-start(f32[256,128]{1,0:T(8,128)S(1)} %constant_dynamic-update-slice_fusion.after_ref.refs_0_), channel_id=1, source_target_pairs={{1,0},{0,1},{3,2},{2,3},{5,4},{4,5},{7,6},{6,7},{9,8},{8,9},{11,10... | collective-permute-start | bytes 393224 | tf_op jit(solution)/shard_map/ppermute | solution.py:279
  34.0 2.3 %collective-permute-start.10 = (f32[512,256]{1,0:T(8,128)S(1)}, f32[512,256]{1,0:T(8,128)S(1)}, u32[]{:S(2)}, u32[]{:S(2)}) collective-permute-start(f32[512,256]{1,0:T(8,128)S(1)} %constant_dynamic-update-slice_fusion.6.refs_0_), channel_id=1, source_target_pairs={{8,0},{0,8},{24,16},{16,24},{9,1},{1,9},{25,17},{17,25},{10,2},{2,... | collective-permute-start | bytes 1572872 | tf_op jit(solution)/shard_map/ppermute | solution.py:279
  34.1 4.8 %collective-permute-start.11 = (f32[64,128]{1,0:T(8,128)S(1)}, f32[64,128]{1,0:T(8,128)S(1)}, u32[]{:S(2)}, u32[]{:S(2)}) collective-permute-start(f32[64,128]{1,0:T(8,128)S(1)} %get-tuple-element.29.refs_0_), channel_id=1, source_target_pairs={{16,0},{24,8},{0,16},{8,24},{17,1},{25,9},{1,17},{9,25},{18,2},{26... | collective-permute-start | bytes 98312 | tf_op jit(solution)/shard_map/ppermute | solution.py:279
  35.6 3.4 %collective-permute-start.12 = (f32[64,128]{1,0:T(8,128)S(1)}, f32[64,128]{1,0:T(8,128)S(1)}, u32[]{:S(2)}, u32[]{:S(2)}) collective-permute-start(f32[64,128]{1,0:T(8,128)S(1)} %get-tuple-element.29.refs_0_), channel_id=1, source_target_pairs={{24,0},{16,8},{8,16},{0,24},{25,1},{17,9},{9,17},{1,25},{26,2},{18... | collective-permute-start | bytes 98312 | tf_op jit(solution)/shard_map/ppermute | solution.py:279
  36.0 2.9 %collective-permute-start.13 = (f32[64,128]{1,0:T(8,128)S(1)}, f32[64,128]{1,0:T(8,128)S(1)}, u32[]{:S(2)}, u32[]{:S(2)}) collective-permute-start(f32[64,128]{1,0:T(8,128)S(1)} %get-tuple-element.29.refs_0_), channel_id=1, source_target_pairs={{8,0},{0,8},{24,16},{16,24},{9,1},{1,9},{25,17},{17,25},{10,2},{2,... | collective-permute-start | bytes 98312 | tf_op jit(solution)/shard_map/ppermute | solution.py:279
